TPU v7x, 32 devices: a whole 2x2x4 slice. The times are simulated.
32 devices in a mesh: seq: 4 (over y, core), fsdp: 8 (over z, x).
Axes of the slice: x: 2, y: 2, z: 4, core: 2. Of those that a mesh axis runs over, the one named last changes fastest.
Arguments:
- tokens: bfloat16 [8, 1024, 768], P('fsdp', 'seq'), may hold values from -6 to 6
- segment_ids: int32 [8, 1024], P('fsdp', 'seq'), may hold values from 0 to 3, never falling along the last dimension, each value on 1 to 512 neighbouring positions
- query_weight: bfloat16 [768, 768], P('fsdp'), may hold values from -0.4375 to 0.4375
- key_weight: bfloat16 [768, 768], P('fsdp'), may hold values from -0.21875 to 0.21875
- value_weight: bfloat16 [768, 768], P('fsdp'), may hold values from -0.21875 to 0.21875
- merge_weight: bfloat16 [768, 768], P('fsdp'), may hold values from -0.875 to 0.875
- query_bias: bfloat16 [768], P('fsdp'), may hold values from -3 to 3
- value_bias: bfloat16 [768], P('fsdp'), may hold values from -3 to 3
- merge_bias: bfloat16 [768], P('fsdp'), may hold values from -3 to 3
- first_gain: bfloat16 [768], P('fsdp'), may hold values from 0.5 to 1.5
- first_shift: bfloat16 [768], P('fsdp'), may hold values from -3 to 3
- expand_weight: bfloat16 [768, 3072], P('fsdp'), may hold values from -0.21875 to 0.21875
- expand_bias: bfloat16 [3072], P('fsdp'), may hold values from -3 to 3
- shrink_weight: bfloat16 [3072, 768], P('fsdp'), may hold values from -0.21875 to 0.21875
- shrink_bias: bfloat16 [768], P('fsdp'), may hold values from -3 to 3
- second_gain: bfloat16 [768], P('fsdp'), may hold values from 0.5 to 1.5
- second_shift: bfloat16 [768], P('fsdp'), may hold values from -3 to 3
- cotangent: bfloat16 [8, 1024, 768], P('fsdp', 'seq'), may hold values from -6 to 6
Outputs:
- output: bfloat16 [8, 1024, 768], P('fsdp', 'seq')
- input_grad: bfloat16 [8, 1024, 768], P('fsdp', 'seq')
- query_weight_grad: float32 [768, 768], P('fsdp')
- key_weight_grad: float32 [768, 768], P('fsdp')
- value_weight_grad: float32 [768, 768], P('fsdp')
- merge_weight_grad: float32 [768, 768], P('fsdp')
- query_bias_grad: float32 [768], P('fsdp')
- value_bias_grad: float32 [768], P('fsdp')
- merge_bias_grad: float32 [768], P('fsdp')
- first_gain_grad: float32 [768], P('fsdp')
- first_shift_grad: float32 [768], P('fsdp')
- expand_weight_grad: float32 [768, 3072], P('fsdp')
- expand_bias_grad: float32 [3072], P('fsdp')
- shrink_weight_grad: float32 [3072, 768], P('fsdp')
- shrink_bias_grad: float32 [768], P('fsdp')
- second_gain_grad: float32 [768], P('fsdp')
- second_shift_grad: float32 [768], P('fsdp')
Inputs may be any that keep to these rules, and one draw needn't show every extreme that they name: `segment_ids`: in each sequence the ids never fall, every id appears, a document holds at most 512 tokens, and some document holds exactly that many.
All inputs are finite; a program needn't handle non-finite values.
Results may differ from a plain program's by a relative error of at most 0.019.
Values may be sent and summed in bfloat16 or wider, within the bound.
No kernel may reach another device: no remote copies, remote signals or barrier semaphores. Data moves between devices by JAX's collectives and lax.ppermute only.
A program may use at most 128 MiB of HBM per device.

v0:
```python
from functools import partial

import jax
import jax.numpy as jnp
from jax import lax
from jax.sharding import PartitionSpec as P

HEAD_DIM = 64


def shortened(x):
    return jax.tree.map(lambda a: a.astype(jnp.bfloat16) if a.dtype == jnp.float32 else a, x)


def inner_rows(left, right):
    return lax.dot_general(
        left, right, (((0,), (0,)), ((), ())), preferred_element_type=jnp.float32
    )


def times_trans(left, right):
    return lax.dot_general(
        left, right, (((1,), (1,)), ((), ())), preferred_element_type=jnp.float32
    )


def norm_forward(values, gain, shift):
    center = values - jnp.mean(values, axis=-1, keepdims=True)
    rstd = lax.rsqrt(jnp.mean(center * center, axis=-1, keepdims=True) + 1e-12)
    normed = center * rstd
    return (normed * gain + shift, normed, rstd)


def norm_backward(grad, normed, rstd, gain):
    scaled = grad * gain
    inside = (
        scaled
        - jnp.mean(scaled, axis=-1, keepdims=True)
        - normed * jnp.mean(scaled * normed, axis=-1, keepdims=True)
    )
    return (inside * rstd, jnp.sum(grad * normed, axis=0), jnp.sum(grad, axis=0))


def masked_scores(q_block, s_block, keys, segs):
    raw = jnp.einsum("qhd,khd->hqk", q_block, keys, preferred_element_type=jnp.float32)
    same = (s_block[:, None] == segs[None, :])[None]
    return jnp.where(same, raw * 0.125, -1000000000.0)


def attend_forward(q_blocks, s_blocks, keys, values, segs):

    def one_block(item):
        q_block, s_block = item
        scores = masked_scores(q_block, s_block, keys, segs)
        top = jnp.max(scores, axis=-1, keepdims=True)
        expo = jnp.exp(scores - top)
        total = jnp.sum(expo, axis=-1, keepdims=True)
        prob = (expo / total).astype(jnp.bfloat16)
        mixed = jnp.einsum("hqk,khd->qhd", prob, values, preferred_element_type=jnp.float32)
        return (mixed.astype(jnp.bfloat16), top + jnp.log(total))

    return lax.map(one_block, (q_blocks, s_blocks))


def attend_backward(q_blocks, s_blocks, g_blocks, lse_blocks, keys, values, segs):

    def step(carry, item):
        q_block, s_block, g_block, lse_block = item
        prob = jnp.exp(masked_scores(q_block, s_block, keys, segs) - lse_block)
        dprob = jnp.einsum("qhd,khd->hqk", g_block, values, preferred_element_type=jnp.float32)
        delta = jnp.sum(dprob * prob, axis=-1, keepdims=True)
        dscore = (prob * (dprob - delta)).astype(jnp.bfloat16)
        d_query = (
            jnp.einsum("hqk,khd->qhd", dscore, keys, preferred_element_type=jnp.float32) * 0.125
        )
        d_key = (
            carry[0]
            + jnp.einsum("hqk,qhd->khd", dscore, q_block, preferred_element_type=jnp.float32)
            * 0.125
        )
        d_value = carry[1] + jnp.einsum(
            "hqk,qhd->khd", prob.astype(jnp.bfloat16), g_block, preferred_element_type=jnp.float32
        )
        return ((d_key, d_value), d_query)

    zeros = jnp.zeros(keys.shape, jnp.float32)
    (d_key, d_value), d_query = lax.scan(
        step, (zeros, zeros), (q_blocks, s_blocks, g_blocks, lse_blocks)
    )
    return (d_query, d_key, d_value)


def body(
    tokens,
    segment_ids,
    query_weight,
    key_weight,
    value_weight,
    merge_weight,
    query_bias,
    value_bias,
    merge_bias,
    first_gain,
    first_shift,
    expand_weight,
    expand_bias,
    shrink_weight,
    shrink_bias,
    second_gain,
    second_shift,
    cotangent,
):
    rows = tokens.shape[1]
    width = tokens.shape[2]
    inputs = tokens.reshape(rows, width)
    shards = (
        query_weight,
        key_weight,
        value_weight,
        merge_weight,
        expand_weight,
        shrink_weight,
        query_bias,
        value_bias,
        merge_bias,
        first_gain,
        first_shift,
        expand_bias,
        shrink_bias,
        second_gain,
        second_shift,
    )
    gathered = (
        lax.all_gather(shards[0], "fsdp", axis=0, tiled=True),
        lax.all_gather(shards[1], "fsdp", axis=0, tiled=True),
        lax.all_gather(shards[2], "fsdp", axis=0, tiled=True),
        lax.all_gather(shards[3], "fsdp", axis=0, tiled=True),
        lax.all_gather(shards[4], "fsdp", axis=0, tiled=True),
        lax.all_gather(shards[5], "fsdp", axis=0, tiled=True),
        lax.all_gather(shards[6], "fsdp", axis=0, tiled=True),
        lax.all_gather(shards[7], "fsdp", axis=0, tiled=True),
        lax.all_gather(shards[8], "fsdp", axis=0, tiled=True),
        lax.all_gather(shards[9], "fsdp", axis=0, tiled=True),
        lax.all_gather(shards[10], "fsdp", axis=0, tiled=True),
        lax.all_gather(shards[11], "fsdp", axis=0, tiled=True),
        lax.all_gather(shards[12], "fsdp", axis=0, tiled=True),
        lax.all_gather(shards[13], "fsdp", axis=0, tiled=True),
        lax.all_gather(shards[14], "fsdp", axis=0, tiled=True),
    )
    w_query, w_key, w_value, w_merge, w_expand, w_shrink = gathered[:6]
    vectors = [v.astype(jnp.float32) for v in gathered[6:]]
    b_query, b_value, b_merge, g_first, s_first, b_expand, b_shrink, g_second, s_second = vectors
    query = (jnp.dot(inputs, w_query, preferred_element_type=jnp.float32) + b_query).astype(
        jnp.bfloat16
    )
    key = jnp.dot(inputs, w_key, preferred_element_type=jnp.float32).astype(jnp.bfloat16)
    value = (jnp.dot(inputs, w_value, preferred_element_type=jnp.float32) + b_value).astype(
        jnp.bfloat16
    )
    segs = lax.all_gather(segment_ids.reshape(rows), "seq", axis=0, tiled=True)
    q_heads, k_heads, v_heads = (
        lax.all_to_all(query, "seq", split_axis=1, concat_axis=0, tiled=True),
        lax.all_to_all(key, "seq", split_axis=1, concat_axis=0, tiled=True),
        lax.all_to_all(value, "seq", split_axis=1, concat_axis=0, tiled=True),
    )
    length = q_heads.shape[0]
    local_heads = q_heads.shape[1] // HEAD_DIM
    block = min(512, length)
    count = length // block
    q_blocks = q_heads.reshape(count, block, local_heads, HEAD_DIM)
    s_blocks = segs.reshape(count, block)
    keys = k_heads.reshape(length, local_heads, HEAD_DIM)
    values = v_heads.reshape(length, local_heads, HEAD_DIM)
    mixed, lse_blocks = attend_forward(q_blocks, s_blocks, keys, values, segs)
    attended = lax.all_to_all(
        mixed.reshape(length, local_heads * HEAD_DIM),
        "seq",
        split_axis=0,
        concat_axis=1,
        tiled=True,
    )
    branch = jnp.dot(attended, w_merge, preferred_element_type=jnp.float32) + b_merge
    first, normed_one, rstd_one = norm_forward(
        inputs.astype(jnp.float32) + branch, g_first, s_first
    )
    first_low = first.astype(jnp.bfloat16)
    pre = jnp.dot(first_low, w_expand, preferred_element_type=jnp.float32) + b_expand
    act, gelu_pull = jax.vjp(partial(jax.nn.gelu, approximate=False), pre)
    act_low = act.astype(jnp.bfloat16)
    second = first + jnp.dot(act_low, w_shrink, preferred_element_type=jnp.float32) + b_shrink
    result, normed_two, rstd_two = norm_forward(second, g_second, s_second)
    upstream = cotangent.reshape(rows, width).astype(jnp.float32)
    d_second, d_gain_two, d_shift_two = norm_backward(upstream, normed_two, rstd_two, g_second)
    d_shrunk = d_second.astype(jnp.bfloat16)
    d_bias_shrink = jnp.sum(d_shrunk.astype(jnp.float32), axis=0)
    d_w_shrink = inner_rows(act_low, d_shrunk)
    d_act = times_trans(d_shrunk, w_shrink)
    d_pre = gelu_pull(d_act)[0].astype(jnp.bfloat16)
    d_bias_expand = jnp.sum(d_pre.astype(jnp.float32), axis=0)
    d_w_expand = inner_rows(first_low, d_pre)
    d_first = times_trans(d_pre, w_expand) + d_second
    d_res, d_gain_one, d_shift_one = norm_backward(d_first, normed_one, rstd_one, g_first)
    d_branch = d_res.astype(jnp.bfloat16)
    d_bias_merge = jnp.sum(d_branch.astype(jnp.float32), axis=0)
    d_w_merge = inner_rows(attended, d_branch)
    d_attended = times_trans(d_branch, w_merge).astype(jnp.bfloat16)
    g_heads = lax.all_to_all(d_attended, "seq", split_axis=1, concat_axis=0, tiled=True)
    g_blocks = g_heads.reshape(count, block, local_heads, HEAD_DIM)
    d_query, d_key, d_value = attend_backward(
        q_blocks, s_blocks, g_blocks, lse_blocks, keys, values, segs
    )
    flat = local_heads * HEAD_DIM
    d_q_heads = d_query.reshape(length, flat).astype(jnp.bfloat16)
    d_k_heads = d_key.reshape(length, flat).astype(jnp.bfloat16)
    d_v_heads = d_value.reshape(length, flat).astype(jnp.bfloat16)
    d_q_tok, d_k_tok, d_v_tok = (
        lax.all_to_all(d_q_heads, "seq", split_axis=0, concat_axis=1, tiled=True),
        lax.all_to_all(d_k_heads, "seq", split_axis=0, concat_axis=1, tiled=True),
        lax.all_to_all(d_v_heads, "seq", split_axis=0, concat_axis=1, tiled=True),
    )
    d_w_query = inner_rows(inputs, d_q_tok)
    d_w_key = inner_rows(inputs, d_k_tok)
    d_w_value = inner_rows(inputs, d_v_tok)
    d_bias_query = jnp.sum(d_q_tok.astype(jnp.float32), axis=0)
    d_bias_value = jnp.sum(d_v_tok.astype(jnp.float32), axis=0)
    d_inputs = (
        d_res
        + times_trans(d_q_tok, w_query)
        + times_trans(d_k_tok, w_key)
        + times_trans(d_v_tok, w_value)
    )
    matrices = (d_w_query, d_w_key, d_w_value, d_w_merge, d_w_expand, d_w_shrink)
    small_grads = (
        d_bias_query,
        d_bias_value,
        d_bias_merge,
        d_gain_one,
        d_shift_one,
        d_bias_expand,
        d_bias_shrink,
        d_gain_two,
        d_shift_two,
    )
    owned = lax.psum_scatter(matrices + small_grads, "fsdp", scatter_dimension=0, tiled=True)
    owned = jax.tree.map(lambda part: part.astype(jnp.float32), lax.psum(shortened(owned), "seq"))
    out_tokens = result.astype(jnp.bfloat16).reshape(1, rows, width)
    in_grad = d_inputs.astype(jnp.bfloat16).reshape(1, rows, width)
    return (
        out_tokens,
        in_grad,
        owned[0],
        owned[1],
        owned[2],
        owned[3],
        owned[6],
        owned[7],
        owned[8],
        owned[9],
        owned[10],
        owned[4],
        owned[11],
        owned[5],
        owned[12],
        owned[13],
        owned[14],
    )


def solution(mesh):
    return jax.shard_map(
        body,
        mesh=mesh,
        in_specs=(
            P("fsdp", "seq", None),
            P("fsdp", "seq"),
            P("fsdp", None),
            P("fsdp", None),
            P("fsdp", None),
            P("fsdp", None),
            P("fsdp"),
            P("fsdp"),
            P("fsdp"),
            P("fsdp"),
            P("fsdp"),
            P("fsdp", None),
            P("fsdp"),
            P("fsdp", None),
            P("fsdp"),
            P("fsdp"),
            P("fsdp"),
            P("fsdp", "seq", None),
        ),
        out_specs=(
            P("fsdp", "seq", None),
            P("fsdp", "seq", None),
            P("fsdp", None),
            P("fsdp", None),
            P("fsdp", None),
            P("fsdp", None),
            P("fsdp"),
            P("fsdp"),
            P("fsdp"),
            P("fsdp"),
            P("fsdp"),
            P("fsdp", None),
            P("fsdp"),
            P("fsdp", None),
            P("fsdp"),
            P("fsdp"),
            P("fsdp"),
        ),
        check_vma=False,
    )
```

profile of v0, /device:TPU:9, one launch (start us, length us, event | category | flops | bytes accessed | tf_op | source)
XLA Modules:
  0.0 1042.9 jit_solution(7957347920142836349)
XLA Ops:
  19.3 28.1 %all-reduce.18 = (bf16[768]{0:T(1024)(128)(2,1)S(1)}, bf16[768]{0:T(1024)(128)(2,1)S(1)}, bf16[768]{0:T(1024)(128)(2,1)S(1)}, bf16[768]{0:T(1024)(128)(2,1)S(1)}...) all-reduce(bf16[768]{0:T(1024)(128)(2,1)S(1)} %dynamic-update-slice, ...), channel_id=1, replica_groups=mesh['seq'=4,'fsdp'=8] {'fsdp'}, use_global_device_ids=true, to_apply=%add | all-reduce | flops 6144 | bytes 24576
  47.4 3.8 all-gather.9.cloned.1.call-done
  54.0 7.2 all-to-all-start
  61.2 32.0 %all-gather.13.cloned.1.call-done = bf16[768,768]{1,0:T(8,128)(2,1)} async-done(((bf16[96,768]{1,0:T(8,128)(2,1)}), bf16[768,768]{1,0:T(8,128)(2,1)}) %all-gather.13.cloned.1.call-update) | async-done | bytes 1179664 | tf_op jit(solution)/shard_map/all_gather | solution.py:136
  95.9 5.0 all-to-all-start.2
  100.9 34.4 %all-gather.11.cloned.1.call-done = bf16[768,768]{1,0:T(8,128)(2,1)} async-done(((bf16[96,768]{1,0:T(8,128)(2,1)}), bf16[768,768]{1,0:T(8,128)(2,1)}) %all-gather.11.cloned.1.call-update) | async-done | bytes 1179664 | tf_op jit(solution)/shard_map/all_gather | solution.py:135
  137.9 5.0 all-to-all-start.1
  143.5 7.5 all-gather
  154.0 11.6 %while.27 = (s32[]{:T(128)}, bf16[2,512,3,64]{1,3,2,0:T(8,128)(2,1)S(1)}, f32[2,3,512,1]{2,1,3,0:T(4,128)S(1)}, s32[2,512]{1,0:T(2,128)S(1)}, s32[1024]{0:T(1024...) while((s32[]{:T(128)}, ...), condition=%wide.region_3.4_spmd, body=%wide.region_0.3_spmd.sunk | while | flops 422148608 | bytes 22220908 | solution.py:62
  157.6 2.2 fusion.141
  163.4 2.2 fusion.141
  167.0 3.6 all-to-all-start.3
  170.7 20.6 %all-gather.1 = bf16[8,1,384]{2,1,0:T(2,128)(2,1)S(1)} all-gather(bf16[1,1,384]{2,1,0:T(2,128)(2,1)S(1)} %reshape.272), channel_id=1, replica_groups=mesh['seq'=4,'fsdp'=8] {'fsdp'}, dimensions={0}, use_global_device_ids=true | all-gather | bytes 6912 | tf_op jit(solution)/shard_map/all_gather | solution.py:145
  193.5 62.9 %all-gather.17.cloned.1.call-done = bf16[768,3072]{1,0:T(8,128)(2,1)} async-done(((bf16[96,3072]{1,0:T(8,128)(2,1)}), bf16[768,3072]{1,0:T(8,128)(2,1)}) %all-gather.17.cloned.1.call-update) | async-done | bytes 4718608 | tf_op jit(solution)/shard_map/all_gather | solution.py:138
  256.4 11.7 %multiply_convert_fusion.1 = (bf16[256,3072]{1,0:T(8,128)(2,1)}, f32[256,3072]{1,0:T(8,128)}, f32[256,3072]{1,0:T(8,128)}) fusion(f32[3072]{0:T(1024)S(1)} %bitcast.219, bf16[768,3072]{1,0:T(8,128)(2,1)} %all-gather.17.cloned.1.call-done, f32[256,768]{1,0:T(8,128)S(1)} %get-tuple-element.412, f32[768]{0:T(1024)S(1)} %convert_element_type.220, ...), kind=kOutput, calls=%fused_computation.56 | convolution fusion | flops 1260847104 | bytes 13389824 | tf_op jit(solution)/shard_map/dot_general | solution.py:187
  268.1 68.1 %all-gather.19.cloned.1.call-done = bf16[3072,768]{1,0:T(8,128)(2,1)} async-done(((bf16[384,768]{1,0:T(8,128)(2,1)}), bf16[3072,768]{1,0:T(8,128)(2,1)}) %all-gather.19.cloned.1.call-update) | async-done | bytes 4718608 | tf_op jit(solution)/shard_map/all_gather | solution.py:139
  336.2 4.5 fusion.87
  343.6 2.7 convert_reduce_fusion
  346.4 2.2 multiply_reduce_fusion.1
  351.0 5.9 all-to-all-start.4
  357.1 1.9 fusion.71
  359.1 4.2 all-to-all-done.4
  363.9 29.2 %while.28 = (s32[]{:T(128)}, f32[1024,3,64]{0,2,1:T(8,128)}, f32[1024,3,64]{0,2,1:T(8,128)}, bf16[2,512,3,64]{1,3,2,0:T(8,128)(2,1)}, bf16[2,512,3,64]{1,3,2,0:T...) while((s32[]{:T(128)}, f32[1024,3,64]{0,2,1:T(8,128)}, ...), condition=%wide.region_14.15_spmd.clone, body=%wide.region_12.14_spmd.clone.sunk | while | flops 1031830016 | bytes 118939720 | solution.py:87
  365.5 2.5 multiply_reduce_fusion.7
  369.9 2.6 fusion.152
  374.3 3.9 fusion.153
  379.8 2.5 multiply_reduce_fusion.7
  384.1 2.9 fusion.152
  388.9 4.2 fusion.153
  394.8 10.1 all_to_all.131
  406.1 2.0 copy.122
  408.6 9.8 all_to_all.132
  419.7 2.0 copy.124
  423.3 9.6 all_to_all.133
  434.2 2.0 copy.126
  437.6 5.2 fusion.80
  444.4 5.1 fusion.74
  452.9 47.0 %reduce-scatter.19.cloned.1.call-done = f32[96,768]{1,0:T(8,128)} async-done(((f32[768,768]{1,0:T(8,128)}), f32[96,768]{1,0:T(8,128)}) %reduce-scatter.19.cloned.1.call-update) | async-done | bytes 294928
  501.7 70.6 %reduce-scatter.21.cloned.1.call-done = f32[96,768]{1,0:T(8,128)} async-done(((f32[768,768]{1,0:T(8,128)}), f32[96,768]{1,0:T(8,128)}) %reduce-scatter.21.cloned.1.call-update) | async-done | bytes 294928
  574.1 70.4 %reduce-scatter.23.cloned.1.call-done = f32[96,768]{1,0:T(8,128)} async-done(((f32[768,768]{1,0:T(8,128)}), f32[96,768]{1,0:T(8,128)}) %reduce-scatter.23.cloned.1.call-update) | async-done | bytes 294928
  646.3 164.0 %reduce-scatter.15.cloned.1.call-done = f32[96,3072]{1,0:T(8,128)} async-done(((f32[768,3072]{1,0:T(8,128)}), f32[96,3072]{1,0:T(8,128)}) %reduce-scatter.15.cloned.1.call-update) | async-done | bytes 1179664 | tf_op jit(solution)/shard_map/reduce_scatter | solution.py:244
  810.2 2.2 convert_element_type.262
  812.4 162.5 %reduce-scatter.17.cloned.1.call-done = f32[384,768]{1,0:T(8,128)} async-done(((f32[3072,768]{1,0:T(8,128)}), f32[384,768]{1,0:T(8,128)}) %reduce-scatter.17.cloned.1.call-update) | async-done | bytes 1179664 | tf_op jit(solution)/shard_map/reduce_scatter | solution.py:244
  974.9 2.1 convert_element_type.267
  977.5 27.9 %all-reduce.17 = (bf16[768]{0:T(1024)(128)(2,1)S(1)}, bf16[768]{0:T(1024)(128)(2,1)S(1)}, bf16[768]{0:T(1024)(128)(2,1)S(1)}, bf16[768]{0:T(1024)(128)(2,1)S(1)}...) all-reduce(f32[768]{0:T(1024)S(1)} %reduce_sum.184, ...), channel_id=7, replica_groups=mesh['seq'=4,'fsdp'=8] {'fsdp'}, use_global_device_ids=true, to_apply=%region_24.25.clone | all-reduce | flops 9216 | bytes 55296
  1006.1 12.8 %all-reduce.19 = (bf16[96]{0:T(256)(128)(2,1)S(1)}, bf16[96]{0:T(256)(128)(2,1)S(1)}, bf16[96]{0:T(256)(128)(2,1)S(1)}, bf16[96]{0:T(256)(128)(2,1)S(1)}, bf16[9...) all-reduce(bf16[96]{0:T(256)(128)(2,1)S(1)} %dynamic-slice.43, ...), channel_id=1, replica_groups=mesh['seq'=4,'fsdp'=8] {'seq'}, use_global_device_ids=true, to_apply=%region_25.26 | all-reduce | flops 1152 | bytes 4608 | tf_op jit(solution)/shard_map/psum | solution.py:245
  1028.3 2.2 convert_element_type.263
  1030.5 2.2 convert_element_type.268
  (322 shorter events, 81.3 us)
Async XLA Ops:
  7.2 86.0 %copy-start.13 = (bf16[1,256,768]{2,1,0:T(8,128)(2,1)S(1)}, bf16[1,256,768]{2,1,0:T(8,128)(2,1)}, u32[]{:S(2)}) copy-start(bf16[1,256,768]{2,1,0:T(8,128)(2,1)} %param.22) | copy-start | bytes 1179652
  7.2 44.0 %all-gather.9.cloned.1.call-start = ((), (), s32[]{:S(2)}) async-start(), calls=%async_computation.14 | async-start | bytes 1327104 | tf_op jit(solution)/shard_map/all_gather | solution.py:134
  7.9 85.3 %all-gather.13.cloned.1.call-start = ((), (), s32[]{:S(2)}) async-start(), calls=%async_computation.16 | async-start | bytes 1327104 | tf_op jit(solution)/shard_map/all_gather | solution.py:136
  8.7 126.6 %all-gather.11.cloned.1.call-start = ((), (), s32[]{:S(2)}) async-start(), calls=%async_computation.15 | async-start | bytes 1327104 | tf_op jit(solution)/shard_map/all_gather | solution.py:135
  9.4 181.9 %all-gather.15.cloned.1.call-start = ((), (), s32[]{:S(2)}) async-start(), calls=%async_computation.17 | async-start | bytes 1327104 | tf_op jit(solution)/shard_map/all_gather | solution.py:137
  10.0 246.4 %all-gather.17.cloned.1.call-start = ((), (), s32[]{:S(2)}) async-start(), calls=%async_computation.18 | async-start | bytes 5308416 | tf_op jit(solution)/shard_map/all_gather | solution.py:138
  54.0 41.9 %all-to-all-start = ((bf16[256,4,192]{0,2,1:T(8,128)(2,1)}), bf16[256,4,192]{0,2,1:T(8,128)(2,1)S(1)}, u32[]{:S(2)}, u32[]{:S(2)}) async-start(bf16[256,4,192]{0,2,1:T(8,128)(2,1)} %bitcast.8), calls=%async_computation | async-start | bytes 786432 | tf_op jit(solution)/shard_map/all_to_all | solution.py:162
  95.0 48.5 %copy-start.53 = (s32[1,256]{1,0:T(1,128)S(1)}, s32[1,256]{1,0:T(1,128)}, u32[]{:S(2)}) copy-start(s32[1,256]{1,0:T(1,128)} %param.23) | copy-start | bytes 3076
  95.9 42.0 %all-to-all-start.2 = ((bf16[256,4,192]{0,2,1:T(8,128)(2,1)}), bf16[256,4,192]{0,2,1:T(8,128)(2,1)S(1)}, u32[]{:S(2)}, u32[]{:S(2)}) async-start(bf16[256,4,192]{0,2,1:T(8,128)(2,1)} %bitcast.12), calls=%async_computation.2 | async-start | bytes 786432 | tf_op jit(solution)/shard_map/all_to_all | solution.py:164
  137.9 15.5 %all-to-all-start.1 = ((bf16[256,4,192]{0,2,1:T(8,128)(2,1)}), bf16[256,4,192]{0,2,1:T(8,128)(2,1)S(1)}, u32[]{:S(2)}, u32[]{:S(2)}) async-start(bf16[256,4,192]{0,2,1:T(8,128)(2,1)} %bitcast.10), calls=%async_computation.1 | async-start | bytes 786432 | tf_op jit(solution)/shard_map/all_to_all | solution.py:163
  142.9 193.3 %all-gather.19.cloned.1.call-start = ((), (), s32[]{:S(2)}) async-start(), calls=%async_computation.19 | async-start | bytes 5308416 | tf_op jit(solution)/shard_map/all_gather | solution.py:139
  165.6 5.0 copy-start.54
  167.0 24.3 %all-to-all-start.3 = ((bf16[4,256,192]{1,2,0:T(8,128)(2,1)}), bf16[4,256,192]{1,2,0:T(8,128)(2,1)S(1)}, u32[]{:S(2)}, u32[]{:S(2)}) async-start(bf16[4,256,192]{1,2,0:T(8,128)(2,1)} %copy.106), calls=%async_computation.3 | async-start | bytes 786432 | tf_op jit(solution)/shard_map/all_to_all | solution.py:175
  170.6 165.6 %copy-start.39 = (f32[768]{0:T(1024)}, f32[768]{0:T(1024)S(1)}, u32[]{:S(2)}) copy-start(f32[768]{0:T(1024)S(1)} %convert_element_type.220) | copy-start | bytes 9220
  193.2 155.4 %copy-start.11 = (f32[256,768]{1,0:T(8,128)}, f32[256,768]{1,0:T(8,128)S(1)}, u32[]{:S(2)}) copy-start(f32[256,768]{1,0:T(8,128)S(1)} %get-tuple-element.412) | copy-start | bytes 2359300
  193.2 155.4 %copy-start.43 = (f32[256]{0:T(256)}, f32[256]{0:T(256)S(1)}, u32[]{:S(2)}) copy-start(f32[256]{0:T(256)S(1)} %broadcast_multiply_fusion.5) | copy-start | bytes 3076
  193.5 155.2 %copy-start.48 = (f32[256]{0:T(256)}, f32[256]{0:T(256)S(1)}, u32[]{:S(2)}) copy-start(f32[256]{0:T(256)S(1)} %add_rsqrt_fusion.1) | copy-start | bytes 3076
  336.2 7.4 slice-start.2
  336.2 4.7 copy-start.25
  336.2 7.4 slice-start.3
  336.2 7.4 copy-start.56
  341.9 4.5 slice-start
  349.5 9.5 copy-start.9
  351.0 12.4 %all-to-all-start.4 = ((bf16[256,4,192]{0,2,1:T(8,128)(2,1)}), bf16[256,4,192]{0,2,1:T(8,128)(2,1)S(1)}, u32[]{:S(2)}, u32[]{:S(2)}) async-start(bf16[256,4,192]{0,2,1:T(8,128)(2,1)} %bitcast.19), calls=%async_computation.4 | async-start | bytes 786432 | tf_op jit(solution)/shard_map/all_to_all | solution.py:207
  356.9 94.4 %reduce-scatter.13.cloned.1.call-start = ((), (), s32[]{:S(2)}) async-start(), calls=%async_computation.20 | async-start | bytes 2654208 | tf_op jit(solution)/shard_map/reduce_scatter | solution.py:244
  359.0 140.8 %reduce-scatter.19.cloned.1.call-start = ((), (), s32[]{:S(2)}) async-start(), calls=%async_computation.23 | async-start | bytes 2654208
  369.9 4.4 copy-start.1
  384.1 4.7 copy-start.1
  393.1 12.5 %copy-start.14 = (bf16[1,256,768]{2,1,0:T(8,128)(2,1)S(1)}, bf16[1,256,768]{2,1,0:T(8,128)(2,1)}, u32[]{:S(2)}) copy-start(bf16[1,256,768]{2,1,0:T(8,128)(2,1)} %param.22) | copy-start | bytes 1179652
  408.1 164.1 %reduce-scatter.21.cloned.1.call-start = ((), (), s32[]{:S(2)}) async-start(), calls=%async_computation.24 | async-start | bytes 2654208
  421.7 222.8 %reduce-scatter.23.cloned.1.call-start = ((), (), s32[]{:S(2)}) async-start(), calls=%async_computation.25 | async-start | bytes 2654208
  436.2 374.1 %reduce-scatter.15.cloned.1.call-start = ((), (), s32[]{:S(2)}) async-start(), calls=%async_computation.21 | async-start | bytes 10616832 | tf_op jit(solution)/shard_map/reduce_scatter | solution.py:244
  442.8 532.1 %reduce-scatter.17.cloned.1.call-start = ((), (), s32[]{:S(2)}) async-start(), calls=%async_computation.22 | async-start | bytes 10616832 | tf_op jit(solution)/shard_map/reduce_scatter | solution.py:244
  449.5 578.7 %all-reduce.23.cloned.1.call-start = ((), (), s32[]{:S(2)}) async-start(), calls=%async_computation.26 | async-start | bytes 3833856 | tf_op jit(solution)/shard_map/psum | solution.py:245
  501.7 475.4 %copy-start.18 = (bf16[4,256,192]{1,2,0:T(8,128)(2,1)S(1)}, bf16[4,256,192]{1,2,0:T(8,128)(2,1)}, u32[]{:S(2)}) copy-start(bf16[4,256,192]{1,2,0:T(8,128)(2,1)} %copy-done.17) | copy-start | bytes 1179652
  574.0 403.5 %copy-start.45 = (f32[768]{0:T(1024)S(1)}, f32[768]{0:T(1024)}, u32[]{:S(2)}) copy-start(f32[768]{0:T(1024)} %get-tuple-element.323) | copy-start | bytes 9220
  574.0 403.5 %copy-start.46 = (f32[768]{0:T(1024)S(1)}, f32[768]{0:T(1024)}, u32[]{:S(2)}) copy-start(f32[768]{0:T(1024)} %get-tuple-element.398) | copy-start | bytes 9220
  574.0 403.5 %copy-start.47 = (f32[768]{0:T(1024)S(1)}, f32[768]{0:T(1024)}, u32[]{:S(2)}) copy-start(f32[768]{0:T(1024)} %get-tuple-element.400) | copy-start | bytes 9220
  574.0 403.5 %copy-start.50 = (f32[3072]{0:T(1024)S(1)}, f32[3072]{0:T(1024)}, u32[]{:S(2)}) copy-start(f32[3072]{0:T(1024)} %get-tuple-element.417) | copy-start | bytes 36868
  574.0 403.5 %copy-start.51 = (f32[768]{0:T(1024)S(1)}, f32[768]{0:T(1024)}, u32[]{:S(2)}) copy-start(f32[768]{0:T(1024)} %get-tuple-element.321) | copy-start | bytes 9220
  574.1 403.5 %copy-start.52 = (f32[768]{0:T(1024)S(1)}, f32[768]{0:T(1024)}, u32[]{:S(2)}) copy-start(f32[768]{0:T(1024)} %get-tuple-element.326) | copy-start | bytes 9220
  574.1 449.5 %copy-start.10 = (f32[256,768]{1,0:T(8,128)S(1)}, f32[256,768]{1,0:T(8,128)}, u32[]{:S(2)}) copy-start(f32[256,768]{1,0:T(8,128)} %copy-done.9) | copy-start | bytes 2359300
  977.1 48.4 %copy-start.21 = (bf16[768,768]{1,0:T(8,128)(2,1)S(1)}, bf16[768,768]{1,0:T(8,128)(2,1)}, u32[]{:S(2)}) copy-start(bf16[768,768]{1,0:T(8,128)(2,1)} %all-gather.11.cloned.1.call-done) | copy-start | bytes 3538948
  977.1 48.4 %copy-start.24 = (bf16[4,256,192]{1,2,0:T(8,128)(2,1)S(1)}, bf16[4,256,192]{1,2,0:T(8,128)(2,1)}, u32[]{:S(2)}) copy-start(bf16[4,256,192]{1,2,0:T(8,128)(2,1)} %copy-done.23) | copy-start | bytes 1179652
  1028.3 4.4 copy-start.36
  1028.3 5.1 copy-start.35
  1028.3 6.0 copy-start.34
  1028.3 6.9 copy-start.33
  (45 other events, 109.7 us)
Sparse Core Ops, SparseCore 0:
  10.2 40.9 all-gather.8
  53.4 39.8 all-gather.12
  95.4 39.8 all-gather.10
  137.3 39.8 all-gather.14
  179.1 77.2 all-gather.16
  258.5 77.6 all-gather.18
  361.2 66.2 reduce-scatter.12
  431.0 68.8 reduce-scatter.18
  503.4 68.8 reduce-scatter.20
  575.6 68.8 reduce-scatter.22
  648.1 162.0 reduce-scatter.14
  813.7 161.1 reduce-scatter.16
  978.9 49.3 all-reduce.22
where the time goes:
time: 1060 us; the launch traced here: 1040 us
  waiting for transfers between devices  725 us (68%)
  blocking collectives  126 us (12%)
  matrix products  77.4 us (7%)
  local copies, waits for them, and re-layouts  38.4 us (4%)
  other arithmetic  30.9 us (3%)
  starting transfers between devices  27.3 us (3%)
  between operations  17.1 us (2%)
    reduce_scatter x3, waiting for transfers between devices, body(): lax.psum_scatter(matrices + small_grads, 'fsdp', scatter_dimension=0, til...  327 us
    unnamed x16, waiting for transfers between devices  192 us
    all_gather x1, waiting for transfers between devices, body(): lax.all_gather(shards[5], 'fsdp', axis=0, tiled=True)  68.1 us
    all_gather x1, waiting for transfers between devices, body(): lax.all_gather(shards[4], 'fsdp', axis=0, tiled=True)  62.9 us
    unnamed x2, blocking collectives  56 us
    all_gather x1, waiting for transfers between devices, body(): lax.all_gather(shards[1], 'fsdp', axis=0, tiled=True)  34.4 us
    all_gather x1, waiting for transfers between devices, body(): lax.all_gather(shards[2], 'fsdp', axis=0, tiled=True)  32 us
    unnamed x131, local copies, waits for them, and re-layouts  27.9 us
  transfers between devices with their start and end apart: 18, of which 12 were waited for; matrix products, arithmetic and copies ran while one was open for 11% of the time, Pallas kernels for 0%

commit v1 on v0

v1 whole, which is shorter than its diff:
```python
from functools import partial

import jax
import jax.numpy as jnp
from jax import lax
from jax.experimental import pallas as pl
from jax.experimental.pallas import tpu as pltpu
from jax.sharding import PartitionSpec as P

HEAD_DIM = 64
LOW = jnp.bfloat16
FULL = jnp.float32
VMEM = pl.BlockSpec(memory_space=pltpu.VMEM)
SMEM = pl.BlockSpec(memory_space=pltpu.SMEM)
CORE_PAIRS = [(0, 1), (1, 0), (2, 3), (3, 2)]
CHIP_PAIRS = [(0, 2), (2, 0), (1, 3), (3, 1)]
EXTRA = 8
FAR = -1e9


def nn(a, b):
    return lax.dot_general(a, b, (((1,), (0,)), ((), ())), preferred_element_type=FULL)


def nt(a, b):
    return lax.dot_general(a, b, (((1,), (1,)), ((), ())), preferred_element_type=FULL)


def tn(a, b):
    return lax.dot_general(a, b, (((0,), (0,)), ((), ())), preferred_element_type=FULL)


def rows_at(block, size):
    return pl.ds(pl.multiple_of(block * size, size), size)


def call(kernel, name, outs, table, *args, scratch=(), flops=0, nbytes=0):
    return pl.pallas_call(
        kernel,
        name=name,
        out_shape=[jax.ShapeDtypeStruct(shape, dtype) for shape, dtype in outs],
        in_specs=[SMEM] + [VMEM] * len(args),
        out_specs=[VMEM] * len(outs),
        scratch_shapes=[pltpu.VMEM(shape, dtype) for shape, dtype in scratch],
        cost_estimate=pl.CostEstimate(
            flops=int(flops), bytes_accessed=int(nbytes), transcendentals=0
        ),
    )(table, *args)


def attend_kernel(parts, table, t0, t1, t2, t3, *refs):
    pieces, refs = refs[:parts], refs[parts:]
    tok, w, qp, kp, v, q_t, k_t, o_t, lse, keep, send, heads, v_t = refs
    seq, y = table[0], table[1]
    rows = t0.shape[0]
    width = w.shape[0]
    piece = width // parts
    length = tok.shape[0]
    for j, t in enumerate((t0, t1, t2, t3)):
        tok[rows_at(seq ^ j, rows), :] = t[...]
    bias = jnp.zeros((EXTRA, w.shape[1]), FULL)
    for p, ref in enumerate(pieces):
        w[rows_at(table[4 + p], piece), :] = ref[:piece, :]
        bias = bias + ref[piece : piece + EXTRA, :].astype(FULL)
    bias = bias[0:1, :]
    lane = lax.broadcasted_iota(jnp.int32, (rows, 256), 1)
    mark = (lane - 192).astype(FULL)
    for i in range(length // rows):
        here = slice(i * rows, (i + 1) * rows)
        x = nn(tok[here, :width], w[...]) + bias
        seg = tok[here, width : width + 128].astype(FULL)
        seg = jnp.concatenate([seg, seg], axis=1)
        q = x[:, :256].astype(LOW).astype(FULL) * 0.125
        q = jnp.where(lane < 192, q, jnp.where((lane < 196) & (mark != seg), FAR, 0.0))
        k = pltpu.roll(x[:, 128:384], 192, 1).astype(LOW).astype(FULL)
        k = jnp.where(lane < 192, k, jnp.where(mark == seg, 1.0, 0.0))
        vv = x[:, 384:640]
        qp[here, :] = q.astype(LOW)
        kp[here, :] = k.astype(LOW)
        v[here, :] = vv.astype(LOW)
        q_t[:, here] = q.T.astype(LOW)
        k_t[:, here] = k.T.astype(LOW)
        v_t[:, here] = vv.T.astype(LOW)
        for h in range(3):
            heads[h, here, :] = jnp.where(
                (lane // HEAD_DIM == h) | (lane >= 192), k, 0.0
            ).astype(LOW)
    lse[...] = jnp.zeros(lse.shape, FULL)

    @pl.loop(0, length // 256)
    def _(i):
        cols = rows_at(i, 256)
        for h in range(3):
            mine = slice(HEAD_DIM * h, HEAD_DIM * (h + 1))
            scores = nn(heads[h], q_t[:, cols])
            top = jnp.max(scores, axis=0, keepdims=True)
            expo = jnp.exp(scores - top)
            total = jnp.sum(expo, axis=0, keepdims=True)
            mixed = nn(v_t[mine, :], expo.astype(LOW))
            o_t[mine, cols] = mixed * (1.0 / total)
            lse[h : h + 1, cols] = top + jnp.log(total)

    half = length // 2
    keep[...] = o_t[:, rows_at(y, half)].astype(LOW)
    send[...] = o_t[:, rows_at(1 - y, half)].astype(LOW)


def gelu_parts(u):
    a = jnp.abs(u) * 0.7071067811865476
    t = 1.0 / (1.0 + 0.3275911 * a)
    poly = t * (
        0.254829592
        + t * (-0.284496736 + t * (1.421413741 + t * (-1.453152027 + t * 1.061405429)))
    )
    bell = jnp.exp(-0.5 * u * u)
    tail = 0.5 * poly * bell
    phi = jnp.where(u >= 0, 1.0 - tail, tail)
    return u * phi, phi + u * (bell * 0.3989422804014327)


def expand_kernel(parts, table, a0, a1, a2, a3, tok, other, *refs):
    em, refs = refs[:parts], refs[parts:]
    sh_in, refs = refs[:parts], refs[parts:]
    att, wm, e, sh, vec, normed, rstd, low, act, slope, part = refs
    seq, y, c = table[0], table[1], table[2]
    width = e.shape[0]
    piece = width // parts
    hidden = sh.shape[0]
    hidden_piece = hidden // parts
    half = width // 2
    for j, a in enumerate((a0, a1, a2, a3)):
        att[rows_at(seq ^ j, 192), :] = a[...]
    total = jnp.zeros(vec.shape, FULL)
    for p in range(parts):
        at = rows_at(table[4 + p], piece)
        wm[c, at, :] = em[p][:piece, :half]
        wm[1 - c, at, :] = other[p]
        e[at, :] = em[p][:piece, half:]
        total = total + em[p][piece : piece + EXTRA, :].astype(FULL)
        sh[rows_at(table[4 + p], hidden_piece), :] = sh_in[p][...]
    vec[...] = total
    count = normed.shape[0]
    branch = jnp.concatenate([tn(att[...], wm[0]), tn(att[...], wm[1])], axis=1)
    values = (
        tok[rows_at(y, count), :width].astype(FULL) + branch + vec[0:1, :width]
    )
    center = values - jnp.mean(values, axis=1, keepdims=True)
    scale = lax.rsqrt(jnp.mean(center * center, axis=1, keepdims=True) + 1e-12)
    center = center * scale
    normed[...] = center
    rstd[...] = jnp.broadcast_to(scale, rstd.shape)
    low[...] = (center * vec[1:2, :width] + vec[2:3, :width]).astype(LOW)

    @pl.loop(0, hidden // 256)
    def _(i):
        cols = rows_at(i, 256)
        pre = nn(low[...], e[:, cols]) + vec[6:7, cols]
        value, grad = gelu_parts(pre)
        act[:, cols] = value.astype(LOW)
        slope[:, cols] = grad.astype(LOW)

    part[...] = nn(act[...], sh[...]).astype(LOW)


def second_kernel(table, normed, vec, mine, theirs, cot_mine, cot_theirs, slope, e, sh, *refs):
    out, dsec, dz, dpre, dfp, sums, work = refs
    c = table[2]
    rows = cot_mine.shape[0]
    width = e.shape[0]
    hidden = sh.shape[0]
    first = normed[...] * vec[1:2, :width] + vec[2:3, :width]
    second = first + (mine[...].astype(FULL) + theirs[...].astype(FULL)) + vec[3:4, :width]
    center = second - jnp.mean(second, axis=1, keepdims=True)
    scale = lax.rsqrt(jnp.mean(center * center, axis=1, keepdims=True) + 1e-12)
    center = center * scale
    gain = vec[4:5, :width]
    work[...] = center * gain + vec[5:6, :width]
    out[...] = work[rows_at(c, rows), :].astype(LOW)
    work[rows_at(c, rows), :] = cot_mine[...].astype(FULL)
    work[rows_at(1 - c, rows), :] = cot_theirs[...].astype(FULL)
    up = work[...]
    sums[...] = jnp.zeros(sums.shape, FULL)
    sums[0:1, :width] = jnp.sum(up * center, axis=0, keepdims=True)
    sums[1:2, :width] = jnp.sum(up, axis=0, keepdims=True)
    scaled = up * gain
    grad = scale * (
        scaled
        - jnp.mean(scaled, axis=1, keepdims=True)
        - center * jnp.mean(scaled * center, axis=1, keepdims=True)
    )
    dsec[...] = grad
    dz[...] = grad.astype(LOW)
    sums[2:3, :width] = jnp.sum(dz[...].astype(FULL), axis=0, keepdims=True)

    @pl.loop(0, hidden // 256)
    def _(i):
        cols = rows_at(i, 256)
        value = nt(dz[...], sh[cols, :]) * slope[:, cols].astype(FULL)
        value = value.astype(LOW)
        dpre[:, cols] = value
        sums[3:4, cols] = jnp.sum(value.astype(FULL), axis=0, keepdims=True)

    dfp[...] = nt(dpre[...], e[...]).astype(LOW)


def shrink_grad_kernel(parts, table, act, dz, send, keep, work):
    block = work.shape[0] // parts
    work[...] = tn(act[...], dz[...]).astype(LOW)
    for b in range(parts // 2):
        send[b] = work[rows_at(table[4 + parts + b], block), :]
        keep[b] = work[rows_at(table[4 + parts + parts // 2 + b], block), :]


def first_kernel(table, mine, theirs, dsec, normed, rstd, vec, wm, dres, dbr, dkeep, dsend, sums, work):
    seq, c = table[0], table[2]
    width = normed.shape[1]
    half = width // 2
    rows = dres.shape[0]
    up = (mine[...].astype(FULL) + theirs[...].astype(FULL)) + dsec[...]
    center = normed[...]
    sums[...] = jnp.zeros(sums.shape, FULL)
    sums[0:1, :] = jnp.sum(up * center, axis=0, keepdims=True)
    sums[1:2, :] = jnp.sum(up, axis=0, keepdims=True)
    scaled = up * vec[1:2, :width]
    work[...] = rstd[:, 0:1] * (
        scaled
        - jnp.mean(scaled, axis=1, keepdims=True)
        - center * jnp.mean(scaled * center, axis=1, keepdims=True)
    )
    dbr[...] = work[...].astype(LOW)
    dres[...] = work[rows_at(c, rows), :]
    sums[2:3, :] = jnp.sum(dbr[...].astype(FULL), axis=0, keepdims=True)
    for j, ref in ((0, dkeep), (2, dsend)):
        at = rows_at(seq ^ j, 192)
        ref[...] = (
            nt(wm[0, at, :], dbr[:, :half]) + nt(wm[1, at, :], dbr[:, half:])
        ).astype(LOW)


def expand_grad_kernel(parts, table, low, dpre, att, dbr, sums_two, sums_one, send, keep, work, rows):
    c = table[2]
    width = low.shape[1]
    half = width // 2
    block = width // parts
    work[:, :half] = nn(att[...], dbr[:, rows_at(c, half)]).astype(LOW)
    work[:, half:] = tn(low[...], dpre[...]).astype(LOW)
    rows[...] = jnp.zeros(rows.shape, FULL)
    rows[0:1, :width] = sums_one[2:3, :]
    rows[1:3, :width] = sums_one[0:2, :]
    rows[3:4, :width] = sums_two[2:3, :width]
    rows[4:6, :width] = sums_two[0:2, :width]
    rows[6:7, : dpre.shape[1]] = sums_two[3:4, :]
    for b in range(parts // 2):
        for ref, at in ((send, b), (keep, parts // 2 + b)):
            ref[b, :block, :] = work[rows_at(table[4 + parts + at], block), :]
            ref[b, block:, :] = rows[...].astype(LOW)


def attend_back_kernel(
    parts, table, tok, qp, kp, v, q_t, k_t, o_t, lse, dkeep, dother, *refs
):
    send, keep, grads, probs, dscores, d_t, d_rows, q_rows, heads, v_heads, dq_t, work = refs
    y = table[1]
    length = tok.shape[0]
    width = work.shape[0]
    block = width // parts
    half = length // 2
    d_t[192:, :] = jnp.zeros((64, length), LOW)
    d_t[:192, rows_at(y, half)] = dkeep[...]
    d_t[:192, rows_at(1 - y, half)] = dother[...]
    lane = lax.broadcasted_iota(jnp.int32, (256, 256), 1)
    for i in range(length // 256):
        here = slice(i * 256, (i + 1) * 256)
        d = d_t[:, here].astype(FULL).T
        k = kp[here, :].astype(FULL)
        q = qp[here, :].astype(FULL)
        vv = v[here, :].astype(FULL)
        for h in range(3):
            own = lane // HEAD_DIM == h
            at = slice(h * length + i * 256, h * length + (i + 1) * 256)
            d_rows[at, :] = jnp.where(own, d, 0.0).astype(LOW)
            q_rows[at, :] = jnp.where(own, q, 0.0).astype(LOW)
            heads[h, here, :] = jnp.where(own | (lane >= 192), k, 0.0).astype(LOW)
            v_heads[h, here, :] = jnp.where(own, vv, 0.0).astype(LOW)
    dq_t[192:, :] = jnp.zeros((64, length), FULL)

    @pl.loop(0, length // 256)
    def _(i):
        cols = rows_at(i, 256)
        for h in range(3):
            mine = slice(HEAD_DIM * h, HEAD_DIM * (h + 1))
            out = pl.ds(pl.multiple_of(h * length + i * 256, 256), 256)
            prob = jnp.exp(nn(heads[h], q_t[:, cols]) - lse[h : h + 1, cols])
            probs[:, out] = prob.astype(LOW)
            delta = jnp.sum(
                d_t[mine, cols].astype(FULL) * o_t[mine, cols], axis=0, keepdims=True
            )
            grad = (prob * (nn(v_heads[h], d_t[:, cols]) - delta)).astype(LOW)
            dscores[:, out] = grad
            dq_t[mine, cols] = nn(k_t[mine, :], grad) * 0.125

    for i in range(length // 256):
        here = slice(i * 256, (i + 1) * 256)
        dv = nn(probs[here, :], d_rows[...])
        dk = pltpu.roll(nn(dscores[here, :], q_rows[...]), 192, 1)
        dq = dq_t[:, here].T
        grads[here, :256] = jnp.where(lane < 192, dq, dk).astype(LOW)
        grads[here, 256:384] = dk[:, :128].astype(LOW)
        grads[here, 384:] = dv.astype(LOW)
    work[...] = tn(tok[:, :width], grads[...]).astype(LOW)
    total = jnp.sum(grads[...].astype(FULL), axis=0, keepdims=True)
    total = jnp.broadcast_to(total, (EXTRA, total.shape[1])).astype(LOW)
    for b in range(parts // 2):
        for ref, at in ((send, b), (keep, parts // 2 + b)):
            ref[b, :block, :] = work[rows_at(table[4 + parts + at], block), :]
            ref[b, block:, :] = total


def input_grad_kernel(table, grads, w, send, keep, work):
    seq = table[0]
    rows = send.shape[1]
    work[...] = nt(grads[...], w[...]).astype(LOW)
    for b in range(2):
        send[b] = work[rows_at(seq ^ (1 + 2 * b), rows), :]
        keep[b] = work[rows_at(seq ^ (2 * b), rows), :]


def pair_kernel(table, keep, got, *outs):
    z = table[3]
    ring = keep.shape[0]
    for k, ref in enumerate(outs):
        at = lax.rem(z + k, ring)
        ref[...] = (keep[at].astype(FULL) + got[at].astype(FULL)).astype(LOW)


def swap_core(x):
    return lax.ppermute(x, "seq", CORE_PAIRS)


def swap_chip(x):
    return lax.ppermute(x, "seq", CHIP_PAIRS)


def swap_near(x):
    return lax.ppermute(x, "fsdp", [(i, i ^ 1) for i in range(8)])


def shift(x, k):
    return lax.ppermute(x, "fsdp", [(i, (i + 2 * k) % 8) for i in range(8)])


def gather(shard, count, extra):
    if count == 8:
        mine = [shard] + [shift(shard, k) for k in (1, 2, 3)]
        return mine + [swap_near(m) for m in mine]
    whole = lax.all_gather(shard, "fsdp", axis=0)
    rows = shard.shape[0] - extra
    main = whole[:, :rows].reshape(count * rows, shard.shape[1])
    if not extra:
        return [main]
    rest = jnp.sum(whole[:, rows:].astype(FULL), axis=0).astype(LOW)
    return [jnp.concatenate([main, rest], axis=0)]


def scatter(send, keep, table, count, extra):
    if count == 8:
        got = swap_near(send)
        shape = keep.shape[1:]
        parts = call(pair_kernel, "pair", [(shape, LOW)] * 4, table, keep, got)
        total = parts[0].astype(FULL)
        for k in (1, 2, 3):
            total = total + shift(parts[k], k).astype(FULL)
        return total
    both = jnp.concatenate([send, keep], axis=0)
    rows = both.shape[1] - extra
    main = both[:, :rows].reshape(count, -1, both.shape[2])
    rest = jnp.broadcast_to(both[:1, rows:], (count, extra, both.shape[2]))
    both = jnp.concatenate([main, rest], axis=1)
    return lax.psum_scatter(both, "fsdp", scatter_dimension=0).astype(FULL)


def body(
    count,
    tokens,
    segment_ids,
    query_weight,
    key_weight,
    value_weight,
    merge_weight,
    query_bias,
    value_bias,
    merge_bias,
    first_gain,
    first_shift,
    expand_weight,
    expand_bias,
    shrink_weight,
    shrink_bias,
    second_gain,
    second_shift,
    cotangent,
):
    rows, width = tokens.shape[1:]
    hidden = expand_weight.shape[1]
    share = width // count
    unit = hidden // count // 2
    slim = width // 4
    half = width // 2
    length = 4 * rows
    near = 2 * rows
    seq = lax.axis_index("seq")
    own = lax.axis_index("fsdp")
    c, y = seq % 2, seq // 2
    z, x = own // 2, own % 2
    if count == 8:
        parts, pad, rest = 8, EXTRA, 0
        mine = [((z - k) % 4) * 2 + x for k in range(4)]
        pieces = mine + [2 * (m // 2) + 1 - x for m in mine]
        blocks = [2 * k + 1 - x for k in range(4)] + [2 * k + x for k in range(4)]
    else:
        parts, pad = 2, EXTRA
        pieces, blocks = [0, 0], [0, 1]
    table = jnp.stack([seq, y, c, z] + pieces + blocks).astype(jnp.int32)
    pieces_in = parts if count == 8 else 1
    if count != 8:
        table_in = jnp.stack([seq, y, c, z, 0]).astype(jnp.int32)
    else:
        table_in = table

    def columns(weight):
        return lax.dynamic_slice(weight, (0, slim * seq), (share, slim))

    pair = jnp.stack([query_bias, value_bias])
    pair = lax.dynamic_update_slice(jnp.zeros((2, width), LOW), pair, (0, share * own))
    pair = lax.dynamic_slice(pair, (0, slim * seq), (2, slim))
    blank = jnp.zeros((1, slim), LOW)
    bias_row = jnp.concatenate(
        [pair[0:1], blank, pair[1:2], jnp.zeros((1, 64), LOW)], axis=1
    )
    shard = jnp.concatenate(
        [
            columns(query_weight),
            columns(key_weight),
            columns(value_weight),
            jnp.zeros((share, 64), LOW),
        ],
        axis=1,
    )
    shard = jnp.concatenate([shard, jnp.pad(bias_row, ((0, EXTRA - 1), (0, 0)))], axis=0)
    w_pieces = gather(shard, count, EXTRA)

    inputs = tokens.reshape(rows, width)
    marks = jnp.broadcast_to(segment_ids.reshape(rows, 1).astype(LOW), (rows, 128))
    inputs = jnp.concatenate([inputs, marks], axis=1)
    t_two = swap_chip(inputs)
    t_one = swap_core(inputs)
    t_three = swap_core(t_two)

    vectors = jnp.zeros((EXTRA, half + hidden // 2), LOW)
    stack = jnp.stack(
        [merge_bias, first_gain, first_shift, shrink_bias, second_gain, second_shift]
    )
    vectors = lax.dynamic_update_slice(vectors, stack, (0, share * own))
    chunk = lax.dynamic_slice(expand_bias, (unit * c,), (unit,)).reshape(1, unit)
    vectors = lax.dynamic_update_slice(vectors, chunk, (6, unit * own))
    wide = expand_weight.reshape(share, count, 2, unit)
    wide = jnp.where(c == 0, wide[:, :, 0], wide[:, :, 1]).reshape(share, hidden // 2)
    em = jnp.concatenate(
        [lax.dynamic_slice(merge_weight, (0, half * c), (share, half)), wide], axis=1
    )
    em = jnp.concatenate([em, vectors], axis=0)
    em_pieces = gather(em, count, EXTRA)
    low_shard = lax.dynamic_slice(shrink_weight, (unit * c, 0), (unit, width))
    sh_pieces = gather(low_shard, count, 0)

    tok, w, qp, kp, v, q_t, k_t, o_t, lse, keep, send = call(
        partial(attend_kernel, pieces_in),
        "attend",
        [
            ((length, width + 128), LOW),
            ((width, 640), LOW),
            ((length, 256), LOW),
            ((length, 256), LOW),
            ((length, 256), LOW),
            ((256, length), LOW),
            ((256, length), LOW),
            ((slim, length), FULL),
            ((8, length), FULL),
            ((slim, near), LOW),
            ((slim, near), LOW),
        ],
        table_in,
        inputs,
        t_one,
        t_two,
        t_three,
        *w_pieces,
        scratch=[((3, length, 256), LOW), ((256, length), LOW)],
        flops=4e9,
        nbytes=1e7,
    )
    a_two = swap_chip(send)
    a_one = swap_core(keep)
    a_three = swap_core(a_two)
    merge_other = swap_core(jnp.stack([p[: width // pieces_in, :half] for p in em_pieces]))
    cot = cotangent.reshape(rows, width)
    cot_other = swap_core(cot)

    att, wm, e, sh, vec, normed, rstd, low, act, slope, part = call(
        partial(expand_kernel, pieces_in),
        "expand",
        [
            ((width, near), LOW),
            ((2, width, half), LOW),
            ((width, hidden // 2), LOW),
            ((hidden // 2, width), LOW),
            ((EXTRA, half + hidden // 2), FULL),
            ((near, width), FULL),
            ((near, 128), FULL),
            ((near, width), LOW),
            ((near, hidden // 2), LOW),
            ((near, hidden // 2), LOW),
            ((near, width), LOW),
        ],
        table_in,
        keep,
        a_one,
        a_two,
        a_three,
        tok,
        merge_other,
        *em_pieces,
        *sh_pieces,
        flops=4e9,
        nbytes=2e7,
    )
    part_other = swap_core(part)
    out, dsec, dz, dpre, dfp, sums_two = call(
        second_kernel,
        "second",
        [
            ((rows, width), LOW),
            ((near, width), FULL),
            ((near, width), LOW),
            ((near, hidden // 2), LOW),
            ((near, width), LOW),
            ((EXTRA, hidden // 2), FULL),
        ],
        table,
        normed,
        vec,
        part,
        part_other,
        cot,
        cot_other,
        slope,
        e,
        sh,
        scratch=[((near, width), FULL)],
        flops=3e9,
        nbytes=2e7,
    )
    dfp_other = swap_core(dfp)
    sh_send, sh_keep = call(
        partial(shrink_grad_kernel, parts),
        "shrink_grad",
        [((parts // 2, hidden // 2 // parts, width), LOW)] * 2,
        table,
        act,
        dz,
        scratch=[((hidden // 2, width), LOW)],
        flops=1.2e9,
        nbytes=5e6,
    )
    dres, dbr, dkeep, dsend, sums_one = call(
        first_kernel,
        "first",
        [
            ((rows, width), FULL),
            ((near, width), LOW),
            ((slim, near), LOW),
            ((slim, near), LOW),
            ((EXTRA, width), FULL),
        ],
        table,
        dfp,
        dfp_other,
        dsec,
        normed,
        rstd,
        vec,
        wm,
        scratch=[((near, width), FULL)],
        flops=1e9,
        nbytes=8e6,
    )
    dother = swap_chip(dsend)
    shrink_own = scatter(sh_send, sh_keep, table, count, 0)
    em_send, em_keep = call(
        partial(expand_grad_kernel, parts),
        "expand_grad",
        [((parts // 2, width // parts + EXTRA, half + hidden // 2), LOW)] * 2,
        table,
        low,
        dpre,
        att,
        dbr,
        sums_two,
        sums_one,
        scratch=[((width, half + hidden // 2), LOW), ((EXTRA, half + hidden // 2), FULL)],
        flops=1.5e9,
        nbytes=8e6,
    )
    em_own = scatter(em_send, em_keep, table, count, EXTRA)
    w_send, w_keep, grads = call(
        partial(attend_back_kernel, parts),
        "attend_back",
        [((parts // 2, width // parts + EXTRA, 640), LOW)] * 2 + [((length, 640), LOW)],
        table,
        tok,
        qp,
        kp,
        v,
        q_t,
        k_t,
        o_t,
        lse,
        dkeep,
        dother,
        scratch=[
            ((length, 3 * length), LOW),
            ((length, 3 * length), LOW),
            ((256, length), LOW),
            ((3 * length, 256), LOW),
            ((3 * length, 256), LOW),
            ((3, length, 256), LOW),
            ((3, length, 256), LOW),
            ((256, length), FULL),
            ((width, 640), LOW),
        ],
        flops=8e9,
        nbytes=1e7,
    )
    w_own = scatter(w_send, w_keep, table, count, EXTRA).astype(LOW)
    x_send, x_keep = call(
        input_grad_kernel,
        "input_grad",
        [((2, rows, width), LOW)] * 2,
        table,
        grads,
        w,
        scratch=[((length, width), LOW)],
        flops=1e9,
        nbytes=5e6,
    )
    x_sum = x_keep.astype(FULL) + swap_core(x_send).astype(FULL)
    x_other = swap_chip(x_sum[1].astype(LOW))
    in_grad = dres + x_sum[0] + x_other.astype(FULL)

    def over_chips(part):
        part = part.astype(LOW)
        return part.astype(FULL) + swap_chip(part).astype(FULL)

    def both_cores(part):
        other = swap_core(part)
        return jnp.where(c == 0, part, other), jnp.where(c == 0, other, part)

    sh_low, sh_high = both_cores(over_chips(shrink_own))
    d_shrink = jnp.concatenate([sh_low, sh_high], axis=0)
    em_low, em_high = both_cores(over_chips(em_own))
    d_merge = jnp.concatenate([em_low[:share, :half], em_high[:share, :half]], axis=1)
    d_expand = jnp.stack(
        [
            em_low[:share, half:].reshape(share, count, unit),
            em_high[:share, half:].reshape(share, count, unit),
        ],
        axis=2,
    ).reshape(share, hidden)
    small = lax.dynamic_slice(em_low[share:], (0, share * own), (6, share))
    d_b_expand = jnp.concatenate(
        [
            lax.dynamic_slice(part[share:], (6, unit * own), (1, unit)).reshape(unit)
            for part in (em_low, em_high)
        ]
    )

    w_two = swap_chip(w_own)
    w_one = swap_core(w_own)
    w_three = swap_core(w_two)
    near_low = jnp.where(c == 0, w_own, w_one)
    near_high = jnp.where(c == 0, w_one, w_own)
    far_low = jnp.where(c == 0, w_two, w_three)
    far_high = jnp.where(c == 0, w_three, w_two)
    ordered = [
        jnp.where(y == 0, near_low, far_low),
        jnp.where(y == 0, near_high, far_high),
        jnp.where(y == 0, far_low, near_low),
        jnp.where(y == 0, far_high, near_high),
    ]
    d_q, d_k, d_v = [
        jnp.concatenate([o[:, slim * i : slim * (i + 1)] for o in ordered], axis=1).astype(FULL)
        for i in range(3)
    ]
    d_b_query = lax.dynamic_slice(d_q[share], (share * own,), (share,))
    d_b_value = lax.dynamic_slice(d_v[share], (share * own,), (share,))

    return (
        out.reshape(1, rows, width),
        in_grad.astype(LOW).reshape(1, rows, width),
        d_q[:share],
        d_k[:share],
        d_v[:share],
        d_merge,
        d_b_query,
        d_b_value,
        small[0],
        small[1],
        small[2],
        d_expand,
        d_b_expand,
        d_shrink,
        small[3],
        small[4],
        small[5],
    )


def solution(mesh):
    row, flat = P("fsdp", None), P("fsdp")
    cube = P("fsdp", "seq", None)
    return jax.shard_map(
        partial(body, mesh.shape["fsdp"]),
        mesh=mesh,
        in_specs=(cube, P("fsdp", "seq"))
        + (row,) * 4
        + (flat,) * 5
        + (row, flat, row)
        + (flat,) * 3
        + (cube,),
        out_specs=(cube, cube) + (row,) * 4 + (flat,) * 5 + (row, flat, row) + (flat,) * 3,
        check_vma=False,
    )
```

time: 1060 us -> 330 us (0.31); the launches traced: 1040 us -> 324 us
  waiting for transfers between devices: 725 us -> 130 us
  blocking collectives: 126 us -> 0 us
  Pallas kernels: 0 us -> 83.1 us
  matrix products: 77.4 us -> 0 us
  starting transfers between devices: 27.3 us -> 61.5 us
  other arithmetic: 30.9 us -> 13.4 us
  between operations: 17.1 us -> 2.1 us
    reduce_scatter x3 -> x0, waiting for transfers between devices: 327 us -> none  [body(): lax.psum_scatter(matrices + small_grads, 'fsdp', scatter_dimension=0, til...]
    all_gather x6 -> x0, waiting for transfers between devices: 201 us -> none  [the longest x1 68.1 us: body(): lax.all_gather(shards[5], 'fsdp', axis=0, tiled=True)]
    unnamed x16 -> x0, waiting for transfers between devices: 192 us -> none
    ppermute x0 -> x53, waiting for transfers between devices: none -> 130 us  [the longest x18 73.4 us: shift(): return lax.ppermute(x, 'fsdp', [(i, (i + 2 * k) % 8) for i in range(8)])]
    pallas_call x0 -> x11, Pallas kernels: none -> 83.1 us  [call(): pl.pallas_call(kernel, name=name, out_shape=[jax.ShapeDtypeStruct(shape,...]
    dot_general x32 -> x0, matrix products: 77.4 us -> none  [the longest x6 13.6 us: inner_rows(): lax.dot_general(left, right, (((0,), (0,)), ((), ())), preferred_element_...]
    ppermute x0 -> x53, starting transfers between devices: none -> 61.5 us  [the longest x13 21.2 us: swap_core(): return lax.ppermute(x, 'seq', CORE_PAIRS)]
    unnamed x2 -> x0, blocking collectives: 56 us -> none
  transfers between devices with their start and end apart: 18 -> 53, of which waited for: 12 -> 23; matrix products, arithmetic and copies ran while one was open for 11% -> 8% of each run, Pallas kernels for 0% -> 16%
where the time goes in v1:
time: 330 us; the launch traced here: 324 us
  waiting for transfers between devices  130 us (39%)
  Pallas kernels  83.1 us (25%)
  starting transfers between devices  61.5 us (19%)
  local copies, waits for them, and re-layouts  33.9 us (10%)
  other arithmetic  13.4 us (4%)
    pallas_call x11, Pallas kernels, call(): pl.pallas_call(kernel, name=name, out_shape=[jax.ShapeDtypeStruct(shape,...  83.1 us
    ppermute x18, waiting for transfers between devices, shift(): return lax.ppermute(x, 'fsdp', [(i, (i + 2 * k) % 8) for i in range(8)])  73.4 us
    ppermute x15, waiting for transfers between devices, swap_near(): return lax.ppermute(x, 'fsdp', [(i, i ^ 1) for i in range(8)])  40.5 us
    ppermute x13, starting transfers between devices, swap_core(): return lax.ppermute(x, 'seq', CORE_PAIRS)  21.2 us
    ppermute x18, starting transfers between devices, shift(): return lax.ppermute(x, 'fsdp', [(i, (i + 2 * k) % 8) for i in range(8)])  20 us
    ppermute x15, starting transfers between devices, swap_near(): return lax.ppermute(x, 'fsdp', [(i, i ^ 1) for i in range(8)])  13.5 us
    unnamed x117, local copies, waits for them, and re-layouts  13 us
    ppermute x7, waiting for transfers between devices, swap_chip(): return lax.ppermute(x, 'seq', CHIP_PAIRS)  11.2 us
  transfers between devices with their start and end apart: 53, of which 23 were waited for; matrix products, arithmetic and copies ran while one was open for 8% of the time, Pallas kernels for 16%

profile of v1, /device:TPU:9, one launch (start us, length us, event | category | flops | bytes accessed | tf_op | source)
XLA Modules:
  0.0 323.8 jit_solution(6885888468641855201)
XLA Ops:
  1.5 2.9 reshape.79
  18.2 2.8 collective-permute-start.4
  21.7 23.9 %collective-permute-done.14.refs_2_ = bf16[104,1920]{1,0:T(8,128)(2,1)S(1)} collective-permute-done((bf16[104,1920]{1,0:T(8,128)(2,1)S(1)}, bf16[104,1920]{1,0:T(8,128)(2,1)S(1)}, u32[]{:S(2)}, u32[]{:S(2)}) %collective-permute-start.14) | collective-permute-done | bytes 399392 | tf_op jit(solution)/shard_map/ppermute | solution.py:349
  47.4 4.0 %collective-permute-done.15.refs_3_ = bf16[104,1920]{1,0:T(8,128)(2,1)S(1)} collective-permute-done((bf16[104,1920]{1,0:T(8,128)(2,1)S(1)}, bf16[104,1920]{1,0:T(8,128)(2,1)S(1)}, u32[]{:S(2)}, u32[]{:S(2)}) %collective-permute-start.15) | collective-permute-done | bytes 399392 | tf_op jit(solution)/shard_map/ppermute | solution.py:349
  53.6 1.5 fusion.11
  57.7 1.7 collective-permute-start
  59.5 2.1 collective-permute-done.17.refs_5_
  61.7 2.5 collective-permute-start.2
  64.8 8.3 %collective-permute-done.6.refs_4_ = bf16[104,640]{1,0:T(8,128)(2,1)S(1)} collective-permute-done((bf16[104,640]{1,0:T(8,128)(2,1)S(1)}, bf16[104,640]{1,0:T(8,128)(2,1)S(1)}, u32[]{:S(2)}, u32[]{:S(2)}) %collective-permute-start.6) | collective-permute-done | bytes 133152 | tf_op jit(solution)/shard_map/ppermute | solution.py:345
  75.2 9.3 %collective-permute-done.7.refs_5_ = bf16[104,640]{1,0:T(8,128)(2,1)S(1)} collective-permute-done((bf16[104,640]{1,0:T(8,128)(2,1)S(1)}, bf16[104,640]{1,0:T(8,128)(2,1)S(1)}, u32[]{:S(2)}, u32[]{:S(2)}) %collective-permute-start.7) | collective-permute-done | bytes 133152 | tf_op jit(solution)/shard_map/ppermute | solution.py:345
  86.6 1.7 collective-permute-done.8.refs_6_
  88.3 2.7 collective-permute-done.9.refs_7_
  94.2 2.6 collective-permute-start.20
  96.8 14.4 %attend.1 = (bf16[1024,896]{1,0:T(8,128)(2,1)}, bf16[768,640]{1,0:T(8,128)(2,1)}, bf16[1024,256]{1,0:T(8,128)(2,1)}, bf16[1024,256]{1,0:T(8,128)(2,1)}, bf16[102...) custom-call(s32[20]{0:T(128)} %stack.143.table, ...), custom_call_target="tpu_custom_call" | custom-call | flops 4000000000 | bytes 10000000 | tf_op jit(solution)/shard_map/attend/pallas_call | solution.py:38
  114.9 3.1 collective-permute-done.11.a2
  118.9 2.2 collective-permute-done.26.refs_14_
  121.1 6.3 %collective-permute-done.27.refs_15_ = bf16[192,768]{1,0:T(8,128)(2,1)S(1)} collective-permute-done((bf16[192,768]{1,0:T(8,128)(2,1)}, bf16[192,768]{1,0:T(8,128)(2,1)S(1)}, u32[]{:S(2)}, u32[]{:S(2)}) %collective-permute-start.27) | collective-permute-done | bytes 294944 | tf_op jit(solution)/shard_map/ppermute | solution.py:345
  128.5 14.1 %expand.1 = (bf16[768,512]{1,0:T(8,128)(2,1)}, bf16[2,768,384]{2,1,0:T(8,128)(2,1)}, bf16[768,1536]{1,0:T(8,128)(2,1)}, bf16[1536,768]{1,0:T(8,128)(2,1)}, f32[8...) custom-call(s32[20]{0:T(128)} %stack.143.table, ...), custom_call_target="tpu_custom_call" | custom-call | flops 4000000000 | bytes 20000000 | tf_op jit(solution)/shard_map/expand/pallas_call | solution.py:38
  143.8 2.6 collective-permute-done.29.cot_theirs
  147.5 10.8 %second.1 = (bf16[256,768]{1,0:T(8,128)(2,1)}, f32[512,768]{1,0:T(8,128)}, bf16[512,768]{1,0:T(8,128)(2,1)}, bf16[512,1536]{1,0:T(8,128)(2,1)}, bf16[512,768]{1,0:T(8,128)(2,1)}, /*index=5*/f32[8,1536]{1,0:T(8,128)}) custom-call(s32[20]{0:T(128)} %stack.143.table, f32[512,768]{1,0:T(8,128)} %get-tuple-element.74.normed, f32[8,1920]{1,0:T(8,128)} %get-tuple-element.75.vec, ...), custom_call_target="tpu_custom_call" | custom-call | flops 3000000000 | bytes 20000000 | tf_op jit(solution)/shard_map/second/pallas_call | solution.py:38
  158.6 2.1 collective-permute-done.30.theirs
  161.7 5.2 %first.1 = (f32[256,768]{1,0:T(8,128)}, bf16[512,768]{1,0:T(8,128)(2,1)}, bf16[192,512]{1,0:T(8,128)(2,1)}, bf16[192,512]{1,0:T(8,128)(2,1)}, f32[8,768]{1,0:T(8,128)}) custom-call(s32[20]{0:T(128)} %stack.143.table, bf16[512,768]{1,0:T(8,128)(2,1)} %get-tuple-element.81.mine, bf16[512,768]{1,0:T(8,128)(2,1)} %copy-done.7, ...), custom_call_target="tpu_custom_call" | custom-call | flops 1000000000 | bytes 8000000 | tf_op jit(solution)/shard_map/first/pallas_call | solution.py:38
  167.1 4.5 %shrink_grad.1 = (bf16[4,192,768]{2,1,0:T(8,128)(2,1)}, bf16[4,192,768]{2,1,0:T(8,128)(2,1)}) custom-call(s32[20]{0:T(128)} %stack.143.table, bf16[512,1536]{1,0:T(8,128)(2,1)} %get-tuple-element.117.act, bf16[512,768]{1,0:T(8,128)(2,1)} %get-tuple-element.118.dz), custom_call_target="tpu_custom_call" | custom-call | flops 1200000000 | bytes 5000000 | tf_op jit(solution)/shard_map/shrink_grad/pallas_call | solution.py:38
  173.9 16.0 %attend_back.1 = (bf16[4,104,640]{2,1,0:T(8,128)(2,1)}, bf16[4,104,640]{2,1,0:T(8,128)(2,1)}, bf16[1024,640]{1,0:T(8,128)(2,1)}) custom-call(s32[20]{0:T(128)} %stack.143.table, bf16[1024,896]{1,0:T(8,128)(2,1)} %get-tuple-element.73.tok, bf16[1024,256]{1,0:T(8,128)(2,1)} %get-tuple-element.86.qp, bf16[1024,256]{1,0:T(8,128)(2,1)} %get-tuple-element.87.kp, ...), custom_call_target="tpu_custom_call" | custom-call | flops 8000000000 | bytes 10000000 | tf_op jit(solution)/shard_map/attend_back/pallas_call | solution.py:38
  190.9 7.8 %collective-permute-done.47.got = bf16[4,192,768]{2,1,0:T(8,128)(2,1)S(1)} collective-permute-done((bf16[4,192,768]{2,1,0:T(8,128)(2,1)}, bf16[4,192,768]{2,1,0:T(8,128)(2,1)S(1)}, u32[]{:S(2)}, u32[]{:S(2)}) %collective-permute-start.47) | collective-permute-done | bytes 1179680 | tf_op jit(solution)/shard_map/ppermute | solution.py:345
  199.8 2.8 pair.5
  202.6 1.7 collective-permute-start.48
  204.3 3.0 collective-permute-start.49
  207.5 5.7 %expand_grad.1 = (bf16[4,104,1920]{2,1,0:T(8,128)(2,1)}, bf16[4,104,1920]{2,1,0:T(8,128)(2,1)}) custom-call(s32[20]{0:T(128)} %stack.143.table, bf16[512,768]{1,0:T(8,128)(2,1)} %get-tuple-element.105.low, bf16[512,1536]{1,0:T(8,128)(2,1)} %get-tuple-element.106.dpre, bf16[768,512]{1,0:T(8,128)(2,1)} %get-tuple-element.107.att, ...), custom_call_target="tpu_custom_call" | custom-call | flops 1500000000 | bytes 8000000 | tf_op jit(solution)/shard_map/expand_grad/pallas_call | solution.py:38
  214.2 4.3 %input_grad.1 = (bf16[2,256,768]{2,1,0:T(8,128)(2,1)}, bf16[2,256,768]{2,1,0:T(8,128)(2,1)}) custom-call(s32[20]{0:T(128)} %stack.143.table, bf16[1024,640]{1,0:T(8,128)(2,1)} %get-tuple-element.95.grads, bf16[768,640]{1,0:T(8,128)(2,1)} %get-tuple-element.96.w), custom_call_target="tpu_custom_call" | custom-call | flops 1000000000 | bytes 5000000 | tf_op jit(solution)/shard_map/input_grad/pallas_call | solution.py:38
  218.5 3.5 %collective-permute-start.32 = (bf16[2,256,768]{2,1,0:T(8,128)(2,1)}, bf16[2,256,768]{2,1,0:T(8,128)(2,1)}, u32[]{:S(2)}, u32[]{:S(2)}) collective-permute-start(bf16[2,256,768]{2,1,0:T(8,128)(2,1)} %get-tuple-element.98), channel_id=1, source_target_pairs={{0,8},{8,0},{16,24},{24,16},{1,9},{9,1},{17,25},{25,17},{2,10},{10... | collective-permute-start | bytes 2359304 | tf_op jit(solution)/shard_map/ppermute | solution.py:337
  222.0 2.0 pair.3
  224.0 1.8 collective-permute-start.35
  225.8 1.5 collective-permute-done.49
  227.3 3.0 collective-permute-start.36
  230.3 6.2 %collective-permute-done.50 = bf16[192,768]{1,0:T(8,128)(2,1)S(1)} collective-permute-done((bf16[192,768]{1,0:T(8,128)(2,1)}, bf16[192,768]{1,0:T(8,128)(2,1)S(1)}, u32[]{:S(2)}, u32[]{:S(2)}) %collective-permute-start.50) | collective-permute-done | bytes 294944 | tf_op jit(solution)/shard_map/ppermute | solution.py:349
  237.9 3.8 %collective-permute-done.37 = bf16[104,640]{1,0:T(8,128)(2,1)} collective-permute-done((bf16[104,640]{1,0:T(8,128)(2,1)}, bf16[104,640]{1,0:T(8,128)(2,1)}, u32[]{:S(2)}, u32[]{:S(2)}) %collective-permute-start.37) | collective-permute-done | bytes 133152 | tf_op jit(solution)/shard_map/ppermute | solution.py:349
  244.1 5.0 %collective-permute-start.38 = (bf16[104,640]{1,0:T(8,128)(2,1)S(1)}, bf16[104,640]{1,0:T(8,128)(2,1)S(1)}, u32[]{:S(2)}, u32[]{:S(2)}) collective-permute-start(bf16[104,640]{1,0:T(8,128)(2,1)S(1)} %add_convert_fusion.2), channel_id=1, source_target_pairs={{0,8},{8,0},{16,24},{24,16},{1,9},{9,1},{17,25},{25,17},{2,10},{10... | collective-permute-start | bytes 399368 | tf_op jit(solution)/shard_map/ppermute | solution.py:337
  250.5 1.5 convert_add_fusion
  257.3 3.2 pair.4
  260.5 2.8 collective-permute-start.43
  265.9 5.2 %collective-permute-done.42 = bf16[104,1920]{1,0:T(8,128)(2,1)S(1)} collective-permute-done((bf16[104,1920]{1,0:T(8,128)(2,1)}, bf16[104,1920]{1,0:T(8,128)(2,1)S(1)}, u32[]{:S(2)}, u32[]{:S(2)}) %collective-permute-start.42) | collective-permute-done | bytes 399392 | tf_op jit(solution)/shard_map/ppermute | solution.py:349
  271.2 23.2 %collective-permute-done.43 = bf16[104,1920]{1,0:T(8,128)(2,1)S(1)} collective-permute-done((bf16[104,1920]{1,0:T(8,128)(2,1)}, bf16[104,1920]{1,0:T(8,128)(2,1)S(1)}, u32[]{:S(2)}, u32[]{:S(2)}) %collective-permute-start.43) | collective-permute-done | bytes 399392 | tf_op jit(solution)/shard_map/ppermute | solution.py:349
  294.4 4.2 %collective-permute-done.44 = bf16[104,1920]{1,0:T(8,128)(2,1)S(1)} collective-permute-done((bf16[104,1920]{1,0:T(8,128)(2,1)}, bf16[104,1920]{1,0:T(8,128)(2,1)S(1)}, u32[]{:S(2)}, u32[]{:S(2)}) %collective-permute-start.44) | collective-permute-done | bytes 399392 | tf_op jit(solution)/shard_map/ppermute | solution.py:349
  302.5 7.6 %collective-permute-done.45 = bf16[104,1920]{1,0:T(8,128)(2,1)S(1)} collective-permute-done((bf16[104,1920]{1,0:T(8,128)(2,1)S(1)}, bf16[104,1920]{1,0:T(8,128)(2,1)S(1)}, u32[]{:S(2)}, u32[]{:S(2)}) %collective-permute-start.45) | collective-permute-done | bytes 399392 | tf_op jit(solution)/shard_map/ppermute | solution.py:341
  310.2 1.6 collective-permute-start.46
  312.3 1.9 fusion.3
  318.8 2.6 reshape.84
  (254 shorter events, 68.5 us)
Async XLA Ops:
  8.0 10.3 %collective-permute-start.13 = (bf16[104,1920]{1,0:T(8,128)(2,1)S(1)}, bf16[104,1920]{1,0:T(8,128)(2,1)S(1)}, u32[]{:S(2)}, u32[]{:S(2)}) collective-permute-start(bf16[104,1920]{1,0:T(8,128)(2,1)S(1)} %pad_maximum_fusion.3.refs_0_), channel_id=1, source_target_pairs={{0,2},{1,3},{2,4},{3,5},{4,6},{5,7},{6,0},{7,1},{8,10},{9,11},{10,... | collective-permute-start | bytes 1198088 | tf_op jit(solution)/shard_map/ppermute | solution.py:349
  9.1 36.5 %collective-permute-start.14 = (bf16[104,1920]{1,0:T(8,128)(2,1)S(1)}, bf16[104,1920]{1,0:T(8,128)(2,1)S(1)}, u32[]{:S(2)}, u32[]{:S(2)}) collective-permute-start(bf16[104,1920]{1,0:T(8,128)(2,1)S(1)} %pad_maximum_fusion.3.refs_0_), channel_id=1, source_target_pairs={{0,4},{1,5},{2,6},{3,7},{4,0},{5,1},{6,2},{7,3},{8,12},{9,13},{10,... | collective-permute-start | bytes 1198088 | tf_op jit(solution)/shard_map/ppermute | solution.py:349
  10.4 41.1 %collective-permute-start.15 = (bf16[104,1920]{1,0:T(8,128)(2,1)S(1)}, bf16[104,1920]{1,0:T(8,128)(2,1)S(1)}, u32[]{:S(2)}, u32[]{:S(2)}) collective-permute-start(bf16[104,1920]{1,0:T(8,128)(2,1)S(1)} %pad_maximum_fusion.3.refs_0_), channel_id=1, source_target_pairs={{0,6},{1,7},{2,0},{3,1},{4,2},{5,3},{6,4},{7,5},{8,14},{9,15},{10,... | collective-permute-start | bytes 1198088 | tf_op jit(solution)/shard_map/ppermute | solution.py:349
  11.8 41.7 %collective-permute-start.16 = (bf16[104,1920]{1,0:T(8,128)(2,1)S(1)}, bf16[104,1920]{1,0:T(8,128)(2,1)}, u32[]{:S(2)}, u32[]{:S(2)}) collective-permute-start(bf16[104,1920]{1,0:T(8,128)(2,1)S(1)} %pad_maximum_fusion.3.refs_0_), channel_id=1, source_target_pairs={{0,1},{1,0},{2,3},{3,2},{4,5},{5,4},{6,7},{7,6},{8,9},{9,8},{10,11... | collective-permute-start | bytes 1198088 | tf_op jit(solution)/shard_map/ppermute | solution.py:345
  16.8 36.7 %collective-permute-start.3 = (bf16[104,640]{1,0:T(8,128)(2,1)S(1)}, bf16[104,640]{1,0:T(8,128)(2,1)S(1)}, u32[]{:S(2)}, u32[]{:S(2)}) collective-permute-start(bf16[104,640]{1,0:T(8,128)(2,1)S(1)} %fusion.7.refs_0_), channel_id=1, source_target_pairs={{0,2},{1,3},{2,4},{3,5},{4,6},{5,7},{6,0},{7,1},{8,10},{9,11},{10,... | collective-permute-start | bytes 399368 | tf_op jit(solution)/shard_map/ppermute | solution.py:349
  18.2 36.9 %collective-permute-start.4 = (bf16[104,640]{1,0:T(8,128)(2,1)S(1)}, bf16[104,640]{1,0:T(8,128)(2,1)S(1)}, u32[]{:S(2)}, u32[]{:S(2)}) collective-permute-start(bf16[104,640]{1,0:T(8,128)(2,1)S(1)} %fusion.7.refs_0_), channel_id=1, source_target_pairs={{0,4},{1,5},{2,6},{3,7},{4,0},{5,1},{6,2},{7,3},{8,12},{9,13},{10,... | collective-permute-start | bytes 399368 | tf_op jit(solution)/shard_map/ppermute | solution.py:349
  45.5 13.9 %collective-permute-start.1 = (bf16[256,896]{1,0:T(8,128)(2,1)S(1)}, bf16[256,896]{1,0:T(8,128)(2,1)S(1)}, u32[]{:S(2)}, u32[]{:S(2)}) collective-permute-start(bf16[256,896]{1,0:T(8,128)(2,1)S(1)} %pad_maximum_fusion.2.t0), channel_id=1, source_target_pairs={{0,16},{16,0},{8,24},{24,8},{1,17},{17,1},{9,25},{25,9},{2,18},{18... | collective-permute-start | bytes 1376264 | tf_op jit(solution)/shard_map/ppermute | solution.py:341
  51.4 10.2 %collective-permute-start.17 = (bf16[104,1920]{1,0:T(8,128)(2,1)S(1)}, bf16[104,1920]{1,0:T(8,128)(2,1)S(1)}, u32[]{:S(2)}, u32[]{:S(2)}) collective-permute-start(bf16[104,1920]{1,0:T(8,128)(2,1)S(1)} %collective-permute-done.13.refs_1_), channel_id=1, source_target_pairs={{0,1},{1,0},{2,3},{3,2},{4,5},{5,4},{6,7},{7,6},{8,9},{9,8},{10,11... | collective-permute-start | bytes 1198088 | tf_op jit(solution)/shard_map/ppermute | solution.py:345
  53.4 4.2 %collective-permute-start.5 = (bf16[104,640]{1,0:T(8,128)(2,1)S(1)}, bf16[104,640]{1,0:T(8,128)(2,1)S(1)}, u32[]{:S(2)}, u32[]{:S(2)}) collective-permute-start(bf16[104,640]{1,0:T(8,128)(2,1)S(1)} %fusion.7.refs_0_), channel_id=1, source_target_pairs={{0,6},{1,7},{2,0},{3,1},{4,2},{5,3},{6,4},{7,5},{8,14},{9,15},{10,... | collective-permute-start | bytes 399368 | tf_op jit(solution)/shard_map/ppermute | solution.py:349
  53.5 19.6 %collective-permute-start.18 = (bf16[104,1920]{1,0:T(8,128)(2,1)S(1)}, bf16[104,1920]{1,0:T(8,128)(2,1)S(1)}, u32[]{:S(2)}, u32[]{:S(2)}) collective-permute-start(bf16[104,1920]{1,0:T(8,128)(2,1)S(1)} %collective-permute-done.14.refs_2_), channel_id=1, source_target_pairs={{0,1},{1,0},{2,3},{3,2},{4,5},{5,4},{6,7},{7,6},{8,9},{9,8},{10,11... | collective-permute-start | bytes 1198088 | tf_op jit(solution)/shard_map/ppermute | solution.py:345
  55.2 17.9 %collective-permute-start.6 = (bf16[104,640]{1,0:T(8,128)(2,1)S(1)}, bf16[104,640]{1,0:T(8,128)(2,1)S(1)}, u32[]{:S(2)}, u32[]{:S(2)}) collective-permute-start(bf16[104,640]{1,0:T(8,128)(2,1)S(1)} %fusion.7.refs_0_), channel_id=1, source_target_pairs={{0,1},{1,0},{2,3},{3,2},{4,5},{5,4},{6,7},{7,6},{8,9},{9,8},{10,11... | collective-permute-start | bytes 399368 | tf_op jit(solution)/shard_map/ppermute | solution.py:345
  57.7 34.9 %collective-permute-start = (bf16[256,896]{1,0:T(8,128)(2,1)S(1)}, bf16[256,896]{1,0:T(8,128)(2,1)S(1)}, u32[]{:S(2)}, u32[]{:S(2)}) collective-permute-start(bf16[256,896]{1,0:T(8,128)(2,1)S(1)} %pad_maximum_fusion.2.t0), channel_id=1, source_target_pairs={{0,8},{8,0},{16,24},{24,16},{1,9},{9,1},{17,25},{25,17},{2,10},{10... | collective-permute-start | bytes 1376264 | tf_op jit(solution)/shard_map/ppermute | solution.py:337
  59.4 26.4 %collective-permute-start.19 = (bf16[104,1920]{1,0:T(8,128)(2,1)S(1)}, bf16[104,1920]{1,0:T(8,128)(2,1)S(1)}, u32[]{:S(2)}, u32[]{:S(2)}) collective-permute-start(bf16[104,1920]{1,0:T(8,128)(2,1)S(1)} %collective-permute-done.15.refs_3_), channel_id=1, source_target_pairs={{0,1},{1,0},{2,3},{3,2},{4,5},{5,4},{6,7},{7,6},{8,9},{9,8},{10,11... | collective-permute-start | bytes 1198088 | tf_op jit(solution)/shard_map/ppermute | solution.py:345
  61.7 31.7 %collective-permute-start.2 = (bf16[256,896]{1,0:T(8,128)(2,1)S(1)}, bf16[256,896]{1,0:T(8,128)(2,1)S(1)}, u32[]{:S(2)}, u32[]{:S(2)}) collective-permute-start(bf16[256,896]{1,0:T(8,128)(2,1)S(1)} %collective-permute-done.1.t2), channel_id=1, source_target_pairs={{0,8},{8,0},{16,24},{24,16},{1,9},{9,1},{17,25},{25,17},{2,10},{10... | collective-permute-start | bytes 1376264 | tf_op jit(solution)/shard_map/ppermute | solution.py:337
  73.1 18.1 %collective-permute-start.21 = (bf16[192,768]{1,0:T(8,128)(2,1)S(1)}, bf16[192,768]{1,0:T(8,128)(2,1)}, u32[]{:S(2)}, u32[]{:S(2)}) collective-permute-start(bf16[192,768]{1,0:T(8,128)(2,1)S(1)} %constant_dynamic-slice_fusion.10.refs_8_), channel_id=1, source_target_pairs={{0,2},{1,3},{2,4},{3,5},{4,6},{5,7},{6,0},{7,1},{8,10},{9,11},{10,... | collective-permute-start | bytes 884744 | tf_op jit(solution)/shard_map/ppermute | solution.py:349
  73.1 11.4 %collective-permute-start.7 = (bf16[104,640]{1,0:T(8,128)(2,1)S(1)}, bf16[104,640]{1,0:T(8,128)(2,1)S(1)}, u32[]{:S(2)}, u32[]{:S(2)}) collective-permute-start(bf16[104,640]{1,0:T(8,128)(2,1)S(1)} %collective-permute-done.3.refs_1_), channel_id=1, source_target_pairs={{0,1},{1,0},{2,3},{3,2},{4,5},{5,4},{6,7},{7,6},{8,9},{9,8},{10,11... | collective-permute-start | bytes 399368 | tf_op jit(solution)/shard_map/ppermute | solution.py:345
  85.8 5.2 %collective-permute-start.9 = (bf16[104,640]{1,0:T(8,128)(2,1)S(1)}, bf16[104,640]{1,0:T(8,128)(2,1)S(1)}, u32[]{:S(2)}, u32[]{:S(2)}) collective-permute-start(bf16[104,640]{1,0:T(8,128)(2,1)S(1)} %collective-permute-done.5.refs_3_), channel_id=1, source_target_pairs={{0,1},{1,0},{2,3},{3,2},{4,5},{5,4},{6,7},{7,6},{8,9},{9,8},{10,11... | collective-permute-start | bytes 399368 | tf_op jit(solution)/shard_map/ppermute | solution.py:345
  88.3 23.0 %collective-permute-start.22 = (bf16[192,768]{1,0:T(8,128)(2,1)S(1)}, bf16[192,768]{1,0:T(8,128)(2,1)}, u32[]{:S(2)}, u32[]{:S(2)}) collective-permute-start(bf16[192,768]{1,0:T(8,128)(2,1)S(1)} %constant_dynamic-slice_fusion.10.refs_8_), channel_id=1, source_target_pairs={{0,4},{1,5},{2,6},{3,7},{4,0},{5,1},{6,2},{7,3},{8,12},{9,13},{10,... | collective-permute-start | bytes 884744 | tf_op jit(solution)/shard_map/ppermute | solution.py:349
  91.0 21.6 %collective-permute-start.23 = (bf16[192,768]{1,0:T(8,128)(2,1)S(1)}, bf16[192,768]{1,0:T(8,128)(2,1)}, u32[]{:S(2)}, u32[]{:S(2)}) collective-permute-start(bf16[192,768]{1,0:T(8,128)(2,1)S(1)} %constant_dynamic-slice_fusion.10.refs_8_), channel_id=1, source_target_pairs={{0,6},{1,7},{2,0},{3,1},{4,2},{5,3},{6,4},{7,5},{8,14},{9,15},{10,... | collective-permute-start | bytes 884744 | tf_op jit(solution)/shard_map/ppermute | solution.py:349
  91.2 22.5 %collective-permute-start.24 = (bf16[192,768]{1,0:T(8,128)(2,1)S(1)}, bf16[192,768]{1,0:T(8,128)(2,1)}, u32[]{:S(2)}, u32[]{:S(2)}) collective-permute-start(bf16[192,768]{1,0:T(8,128)(2,1)S(1)} %constant_dynamic-slice_fusion.10.refs_8_), channel_id=1, source_target_pairs={{0,1},{1,0},{2,3},{3,2},{4,5},{5,4},{6,7},{7,6},{8,9},{9,8},{10,11... | collective-permute-start | bytes 884744 | tf_op jit(solution)/shard_map/ppermute | solution.py:345
  92.6 21.5 %collective-permute-start.25 = (bf16[192,768]{1,0:T(8,128)(2,1)}, bf16[192,768]{1,0:T(8,128)(2,1)}, u32[]{:S(2)}, u32[]{:S(2)}) collective-permute-start(bf16[192,768]{1,0:T(8,128)(2,1)} %collective-permute-done.21.refs_9_), channel_id=1, source_target_pairs={{0,1},{1,0},{2,3},{3,2},{4,5},{5,4},{6,7},{7,6},{8,9},{9,8},{10,11... | collective-permute-start | bytes 884744 | tf_op jit(solution)/shard_map/ppermute | solution.py:345
  94.2 33.2 %collective-permute-start.20 = (bf16[8,96,384]{2,1,0:T(8,128)(2,1)}, bf16[8,96,384]{2,1,0:T(8,128)(2,1)S(1)}, u32[]{:S(2)}, u32[]{:S(2)}) collective-permute-start(bf16[8,96,384]{2,1,0:T(8,128)(2,1)} %fusion.8), channel_id=1, source_target_pairs={{0,8},{8,0},{16,24},{24,16},{1,9},{9,1},{17,25},{25,17},{2,10},{10... | collective-permute-start | bytes 1769480 | tf_op jit(solution)/shard_map/ppermute | solution.py:337
  111.3 6.7 %collective-permute-start.11 = (bf16[192,512]{1,0:T(8,128)(2,1)}, bf16[192,512]{1,0:T(8,128)(2,1)S(1)}, u32[]{:S(2)}, u32[]{:S(2)}) collective-permute-start(bf16[192,512]{1,0:T(8,128)(2,1)} %get-tuple-element.72), channel_id=1, source_target_pairs={{0,16},{16,0},{8,24},{24,8},{1,17},{17,1},{9,25},{25,9},{2,18},{18... | collective-permute-start | bytes 589832 | tf_op jit(solution)/shard_map/ppermute | solution.py:341
  112.6 8.5 %collective-permute-start.26 = (bf16[192,768]{1,0:T(8,128)(2,1)}, bf16[192,768]{1,0:T(8,128)(2,1)S(1)}, u32[]{:S(2)}, u32[]{:S(2)}) collective-permute-start(bf16[192,768]{1,0:T(8,128)(2,1)} %collective-permute-done.22.refs_10_), channel_id=1, source_target_pairs={{0,1},{1,0},{2,3},{3,2},{4,5},{5,4},{6,7},{7,6},{8,9},{9,8},{10,11... | collective-permute-start | bytes 884744 | tf_op jit(solution)/shard_map/ppermute | solution.py:345
  113.7 13.7 %collective-permute-start.27 = (bf16[192,768]{1,0:T(8,128)(2,1)}, bf16[192,768]{1,0:T(8,128)(2,1)S(1)}, u32[]{:S(2)}, u32[]{:S(2)}) collective-permute-start(bf16[192,768]{1,0:T(8,128)(2,1)} %collective-permute-done.23.refs_11_), channel_id=1, source_target_pairs={{0,1},{1,0},{2,3},{3,2},{4,5},{5,4},{6,7},{7,6},{8,9},{9,8},{10,11... | collective-permute-start | bytes 884744 | tf_op jit(solution)/shard_map/ppermute | solution.py:345
  114.1 13.3 %collective-permute-start.10 = (bf16[192,512]{1,0:T(8,128)(2,1)}, bf16[192,512]{1,0:T(8,128)(2,1)S(1)}, u32[]{:S(2)}, u32[]{:S(2)}) collective-permute-start(bf16[192,512]{1,0:T(8,128)(2,1)} %get-tuple-element.71.a0), channel_id=1, source_target_pairs={{0,8},{8,0},{16,24},{24,16},{1,9},{9,1},{17,25},{25,17},{2,10},{10... | collective-permute-start | bytes 589832 | tf_op jit(solution)/shard_map/ppermute | solution.py:337
  118.0 9.4 %collective-permute-start.12 = (bf16[192,512]{1,0:T(8,128)(2,1)S(1)}, bf16[192,512]{1,0:T(8,128)(2,1)S(1)}, u32[]{:S(2)}, u32[]{:S(2)}) collective-permute-start(bf16[192,512]{1,0:T(8,128)(2,1)S(1)} %collective-permute-done.11.a2), channel_id=1, source_target_pairs={{0,8},{8,0},{16,24},{24,16},{1,9},{9,1},{17,25},{25,17},{2,10},{10... | collective-permute-start | bytes 589832 | tf_op jit(solution)/shard_map/ppermute | solution.py:337
  166.9 6.3 %collective-permute-start.31 = (bf16[192,512]{1,0:T(8,128)(2,1)}, bf16[192,512]{1,0:T(8,128)(2,1)S(1)}, u32[]{:S(2)}, u32[]{:S(2)}) collective-permute-start(bf16[192,512]{1,0:T(8,128)(2,1)} %get-tuple-element.94), channel_id=1, source_target_pairs={{0,16},{16,0},{8,24},{24,8},{1,17},{17,1},{9,25},{25,9},{2,18},{18... | collective-permute-start | bytes 589832 | tf_op jit(solution)/shard_map/ppermute | solution.py:341
  171.7 27.1 %collective-permute-start.47 = (bf16[4,192,768]{2,1,0:T(8,128)(2,1)}, bf16[4,192,768]{2,1,0:T(8,128)(2,1)S(1)}, u32[]{:S(2)}, u32[]{:S(2)}) collective-permute-start(bf16[4,192,768]{2,1,0:T(8,128)(2,1)} %get-tuple-element.120), channel_id=1, source_target_pairs={{0,1},{1,0},{2,3},{3,2},{4,5},{5,4},{6,7},{7,6},{8,9},{9,8},{10,11... | collective-permute-start | bytes 3538952 | tf_op jit(solution)/shard_map/ppermute | solution.py:345
  189.9 28.6 %collective-permute-start.34 = (bf16[4,104,640]{2,1,0:T(8,128)(2,1)}, bf16[4,104,640]{2,1,0:T(8,128)(2,1)S(1)}, u32[]{:S(2)}, u32[]{:S(2)}) collective-permute-start(bf16[4,104,640]{2,1,0:T(8,128)(2,1)} %get-tuple-element.100), channel_id=1, source_target_pairs={{0,1},{1,0},{2,3},{3,2},{4,5},{5,4},{6,7},{7,6},{8,9},{9,8},{10,11... | collective-permute-start | bytes 1597448 | tf_op jit(solution)/shard_map/ppermute | solution.py:345
  202.6 21.4 %collective-permute-start.48 = (bf16[192,768]{1,0:T(8,128)(2,1)}, bf16[192,768]{1,0:T(8,128)(2,1)S(1)}, u32[]{:S(2)}, u32[]{:S(2)}) collective-permute-start(bf16[192,768]{1,0:T(8,128)(2,1)} %get-tuple-element.122), channel_id=1, source_target_pairs={{0,2},{1,3},{2,4},{3,5},{4,6},{5,7},{6,0},{7,1},{8,10},{9,11},{10,... | collective-permute-start | bytes 884744 | tf_op jit(solution)/shard_map/ppermute | solution.py:349
  204.3 23.0 %collective-permute-start.49 = (bf16[192,768]{1,0:T(8,128)(2,1)}, bf16[192,768]{1,0:T(8,128)(2,1)S(1)}, u32[]{:S(2)}, u32[]{:S(2)}) collective-permute-start(bf16[192,768]{1,0:T(8,128)(2,1)} %get-tuple-element.123), channel_id=1, source_target_pairs={{0,4},{1,5},{2,6},{3,7},{4,0},{5,1},{6,2},{7,3},{8,12},{9,13},{10,... | collective-permute-start | bytes 884744 | tf_op jit(solution)/shard_map/ppermute | solution.py:349
  207.3 29.2 %collective-permute-start.50 = (bf16[192,768]{1,0:T(8,128)(2,1)}, bf16[192,768]{1,0:T(8,128)(2,1)S(1)}, u32[]{:S(2)}, u32[]{:S(2)}) collective-permute-start(bf16[192,768]{1,0:T(8,128)(2,1)} %get-tuple-element.124), channel_id=1, source_target_pairs={{0,6},{1,7},{2,0},{3,1},{4,2},{5,3},{6,4},{7,5},{8,14},{9,15},{10,... | collective-permute-start | bytes 884744 | tf_op jit(solution)/shard_map/ppermute | solution.py:349
  213.2 43.0 %collective-permute-start.41 = (bf16[4,104,1920]{2,1,0:T(8,128)(2,1)}, bf16[4,104,1920]{2,1,0:T(8,128)(2,1)S(1)}, u32[]{:S(2)}, u32[]{:S(2)}) collective-permute-start(bf16[4,104,1920]{2,1,0:T(8,128)(2,1)} %get-tuple-element.112), channel_id=1, source_target_pairs={{0,1},{1,0},{2,3},{3,2},{4,5},{5,4},{6,7},{7,6},{8,9},{9,8},{10,11... | collective-permute-start | bytes 4792328 | tf_op jit(solution)/shard_map/ppermute | solution.py:345
  218.5 32.0 %collective-permute-start.32 = (bf16[2,256,768]{2,1,0:T(8,128)(2,1)}, bf16[2,256,768]{2,1,0:T(8,128)(2,1)}, u32[]{:S(2)}, u32[]{:S(2)}) collective-permute-start(bf16[2,256,768]{2,1,0:T(8,128)(2,1)} %get-tuple-element.98), channel_id=1, source_target_pairs={{0,8},{8,0},{16,24},{24,16},{1,9},{9,1},{17,25},{25,17},{2,10},{10... | collective-permute-start | bytes 2359304 | tf_op jit(solution)/shard_map/ppermute | solution.py:337
  224.0 12.6 %collective-permute-start.35 = (bf16[104,640]{1,0:T(8,128)(2,1)}, bf16[104,640]{1,0:T(8,128)(2,1)S(1)}, u32[]{:S(2)}, u32[]{:S(2)}) collective-permute-start(bf16[104,640]{1,0:T(8,128)(2,1)} %get-tuple-element.102), channel_id=1, source_target_pairs={{0,2},{1,3},{2,4},{3,5},{4,6},{5,7},{6,0},{7,1},{8,10},{9,11},{10,... | collective-permute-start | bytes 399368 | tf_op jit(solution)/shard_map/ppermute | solution.py:349
  227.3 10.7 %collective-permute-start.36 = (bf16[104,640]{1,0:T(8,128)(2,1)}, bf16[104,640]{1,0:T(8,128)(2,1)}, u32[]{:S(2)}, u32[]{:S(2)}) collective-permute-start(bf16[104,640]{1,0:T(8,128)(2,1)} %get-tuple-element.103), channel_id=1, source_target_pairs={{0,4},{1,5},{2,6},{3,7},{4,0},{5,1},{6,2},{7,3},{8,12},{9,13},{10,... | collective-permute-start | bytes 399368 | tf_op jit(solution)/shard_map/ppermute | solution.py:349
  236.4 5.3 %collective-permute-start.37 = (bf16[104,640]{1,0:T(8,128)(2,1)}, bf16[104,640]{1,0:T(8,128)(2,1)}, u32[]{:S(2)}, u32[]{:S(2)}) collective-permute-start(bf16[104,640]{1,0:T(8,128)(2,1)} %get-tuple-element.104), channel_id=1, source_target_pairs={{0,6},{1,7},{2,0},{3,1},{4,2},{5,3},{6,4},{7,5},{8,14},{9,15},{10,... | collective-permute-start | bytes 399368 | tf_op jit(solution)/shard_map/ppermute | solution.py:349
  236.6 12.5 %collective-permute-start.51 = (bf16[192,768]{1,0:T(8,128)(2,1)S(1)}, bf16[192,768]{1,0:T(8,128)(2,1)S(1)}, u32[]{:S(2)}, u32[]{:S(2)}) collective-permute-start(bf16[192,768]{1,0:T(8,128)(2,1)S(1)} %add_convert_fusion.1), channel_id=1, source_target_pairs={{0,16},{16,0},{8,24},{24,8},{1,17},{17,1},{9,25},{25,9},{2,18},{18... | collective-permute-start | bytes 884744 | tf_op jit(solution)/shard_map/ppermute | solution.py:341
  242.8 9.2 %collective-permute-start.39 = (bf16[104,640]{1,0:T(8,128)(2,1)S(1)}, bf16[104,640]{1,0:T(8,128)(2,1)S(1)}, u32[]{:S(2)}, u32[]{:S(2)}) collective-permute-start(bf16[104,640]{1,0:T(8,128)(2,1)S(1)} %add_convert_fusion.2), channel_id=1, source_target_pairs={{0,16},{16,0},{8,24},{24,8},{1,17},{17,1},{9,25},{25,9},{2,18},{18... | collective-permute-start | bytes 399368 | tf_op jit(solution)/shard_map/ppermute | solution.py:341
  244.1 10.5 %collective-permute-start.38 = (bf16[104,640]{1,0:T(8,128)(2,1)S(1)}, bf16[104,640]{1,0:T(8,128)(2,1)S(1)}, u32[]{:S(2)}, u32[]{:S(2)}) collective-permute-start(bf16[104,640]{1,0:T(8,128)(2,1)S(1)} %add_convert_fusion.2), channel_id=1, source_target_pairs={{0,8},{8,0},{16,24},{24,16},{1,9},{9,1},{17,25},{25,17},{2,10},{10... | collective-permute-start | bytes 399368 | tf_op jit(solution)/shard_map/ppermute | solution.py:337
  250.0 64.2 %collective-permute-start.52 = (f32[192,768]{1,0:T(8,128)}, f32[192,768]{1,0:T(8,128)}, u32[]{:S(2)}, u32[]{:S(2)}) collective-permute-start(f32[192,768]{1,0:T(8,128)} %convert_add_fusion.2), channel_id=1, source_target_pairs={{0,8},{8,0},{16,24},{24,16},{1,9},{9,1},{17,25},{25,17},{2,10},{10... | collective-permute-start | bytes 1769480 | tf_op jit(solution)/shard_map/ppermute | solution.py:337
  253.4 59.0 %collective-permute-start.33 = (bf16[256,768]{1,0:T(8,128)(2,1)}, bf16[256,768]{1,0:T(8,128)(2,1)}, u32[]{:S(2)}, u32[]{:S(2)}) collective-permute-start(bf16[256,768]{1,0:T(8,128)(2,1)} %fusion.4), channel_id=1, source_target_pairs={{0,16},{16,0},{8,24},{24,8},{1,17},{17,1},{9,25},{25,9},{2,18},{18... | collective-permute-start | bytes 1179656 | tf_op jit(solution)/shard_map/ppermute | solution.py:341
  260.5 10.7 %collective-permute-start.42 = (bf16[104,1920]{1,0:T(8,128)(2,1)}, bf16[104,1920]{1,0:T(8,128)(2,1)S(1)}, u32[]{:S(2)}, u32[]{:S(2)}) collective-permute-start(bf16[104,1920]{1,0:T(8,128)(2,1)} %get-tuple-element.114), channel_id=1, source_target_pairs={{0,2},{1,3},{2,4},{3,5},{4,6},{5,7},{6,0},{7,1},{8,10},{9,11},{10,... | collective-permute-start | bytes 1198088 | tf_op jit(solution)/shard_map/ppermute | solution.py:349
  260.5 33.9 %collective-permute-start.43 = (bf16[104,1920]{1,0:T(8,128)(2,1)}, bf16[104,1920]{1,0:T(8,128)(2,1)S(1)}, u32[]{:S(2)}, u32[]{:S(2)}) collective-permute-start(bf16[104,1920]{1,0:T(8,128)(2,1)} %get-tuple-element.115), channel_id=1, source_target_pairs={{0,4},{1,5},{2,6},{3,7},{4,0},{5,1},{6,2},{7,3},{8,12},{9,13},{10,... | collective-permute-start | bytes 1198088 | tf_op jit(solution)/shard_map/ppermute | solution.py:349
  263.3 35.3 %collective-permute-start.44 = (bf16[104,1920]{1,0:T(8,128)(2,1)}, bf16[104,1920]{1,0:T(8,128)(2,1)S(1)}, u32[]{:S(2)}, u32[]{:S(2)}) collective-permute-start(bf16[104,1920]{1,0:T(8,128)(2,1)} %get-tuple-element.116), channel_id=1, source_target_pairs={{0,6},{1,7},{2,0},{3,1},{4,2},{5,3},{6,4},{7,5},{8,14},{9,15},{10,... | collective-permute-start | bytes 1198088 | tf_op jit(solution)/shard_map/ppermute | solution.py:349
  299.8 10.2 %collective-permute-start.45 = (bf16[104,1920]{1,0:T(8,128)(2,1)S(1)}, bf16[104,1920]{1,0:T(8,128)(2,1)S(1)}, u32[]{:S(2)}, u32[]{:S(2)}) collective-permute-start(bf16[104,1920]{1,0:T(8,128)(2,1)S(1)} %add_convert_fusion), channel_id=1, source_target_pairs={{0,16},{16,0},{8,24},{24,8},{1,17},{17,1},{9,25},{25,9},{2,18},{18... | collective-permute-start | bytes 1198088 | tf_op jit(solution)/shard_map/ppermute | solution.py:341
  310.2 6.3 %collective-permute-start.46 = (f32[104,1920]{1,0:T(8,128)S(1)}, f32[104,1920]{1,0:T(8,128)S(1)}, u32[]{:S(2)}, u32[]{:S(2)}) collective-permute-start(f32[104,1920]{1,0:T(8,128)S(1)} %convert_add_fusion.1), channel_id=1, source_target_pairs={{0,8},{8,0},{16,24},{24,16},{1,9},{9,1},{17,25},{25,17},{2,10},{10... | collective-permute-start | bytes 2396168 | tf_op jit(solution)/shard_map/ppermute | solution.py:337
  (60 other events, 1060.8 us)

commit v2 on v1

v2 whole, which is shorter than its diff:
```python
from functools import partial

import jax
import jax.numpy as jnp
from jax import lax
from jax.experimental import pallas as pl
from jax.experimental.pallas import tpu as pltpu
from jax.sharding import PartitionSpec as P

HEAD_DIM = 64
LOW = jnp.bfloat16
FULL = jnp.float32
VMEM = pl.BlockSpec(memory_space=pltpu.VMEM)
SMEM = pl.BlockSpec(memory_space=pltpu.SMEM)
CORE_PAIRS = [(0, 1), (1, 0), (2, 3), (3, 2)]
CHIP_PAIRS = [(0, 2), (2, 0), (1, 3), (3, 1)]
EXTRA = 8
HEADER = 16
FAR = -1e9


def nn(a, b):
    return lax.dot_general(a, b, (((1,), (0,)), ((), ())), preferred_element_type=FULL)


def nt(a, b):
    return lax.dot_general(a, b, (((1,), (1,)), ((), ())), preferred_element_type=FULL)


def tn(a, b):
    return lax.dot_general(a, b, (((0,), (0,)), ((), ())), preferred_element_type=FULL)


def rows_at(block, size):
    return pl.ds(pl.multiple_of(block * size, size), size)


def call(kernel, name, outs, table, *args, scratch=(), flops=0, nbytes=0):
    return pl.pallas_call(
        kernel,
        name=name,
        out_shape=[jax.ShapeDtypeStruct(shape, dtype) for shape, dtype in outs],
        in_specs=[SMEM] + [VMEM] * len(args),
        out_specs=[VMEM] * len(outs),
        scratch_shapes=[pltpu.VMEM(shape, dtype) for shape, dtype in scratch],
        cost_estimate=pl.CostEstimate(
            flops=0, bytes_accessed=0, transcendentals=0
        ),
    )(table, *args)


def attend_kernel(parts, table, t0, t1, t2, t3, *refs):
    pieces, refs = refs[:parts], refs[parts:]
    tok, w, wm, vec, qp, kp, v, q_t, k_t, o_t, lse, keep, send, heads, v_t = refs
    seq, y = table[0], table[1]
    rows = t0.shape[0]
    width = w.shape[0]
    piece = width // parts
    length = tok.shape[0]
    for j, t in enumerate((t0, t1, t2, t3)):
        tok[rows_at(seq ^ j, rows), :] = t[...]
    total = jnp.zeros(vec.shape, FULL)
    for p, ref in enumerate(pieces):
        at = rows_at(table[4 + p], piece)
        w[at, :] = ref[:piece, :640]
        wm[at, :] = ref[:piece, 640:]
        total = total + ref[piece : piece + HEADER, :].astype(FULL)
    vec[...] = total
    bias = vec[8:9, :640]
    lane = lax.broadcasted_iota(jnp.int32, (rows, 256), 1)
    mark = (lane - 192).astype(FULL)
    for i in range(length // rows):
        here = slice(i * rows, (i + 1) * rows)
        x = nn(tok[here, :width], w[...]) + bias
        seg = tok[here, width : width + 128].astype(FULL)
        seg = jnp.concatenate([seg, seg], axis=1)
        q = x[:, :256].astype(LOW).astype(FULL) * 0.125
        q = jnp.where(lane < 192, q, jnp.where((lane < 196) & (mark != seg), FAR, 0.0))
        k = pltpu.roll(x[:, 128:384], 192, 1).astype(LOW).astype(FULL)
        k = jnp.where(lane < 192, k, jnp.where(mark == seg, 1.0, 0.0))
        vv = x[:, 384:640]
        qp[here, :] = q.astype(LOW)
        kp[here, :] = k.astype(LOW)
        v[here, :] = vv.astype(LOW)
        q_t[:, here] = q.T.astype(LOW)
        k_t[:, here] = k.T.astype(LOW)
        v_t[:, here] = vv.T.astype(LOW)
        for h in range(3):
            heads[h, here, :] = jnp.where(
                (lane // HEAD_DIM == h) | (lane >= 192), k, 0.0
            ).astype(LOW)
    lse[...] = jnp.zeros(lse.shape, FULL)

    @pl.loop(0, length // 256)
    def _(i):
        cols = rows_at(i, 256)
        for h in range(3):
            mine = slice(HEAD_DIM * h, HEAD_DIM * (h + 1))
            scores = nn(heads[h], q_t[:, cols])
            top = jnp.max(scores, axis=0, keepdims=True)
            expo = jnp.exp(scores - top)
            total = jnp.sum(expo, axis=0, keepdims=True)
            mixed = nn(v_t[mine, :], expo.astype(LOW))
            o_t[mine, cols] = mixed * (1.0 / total)
            lse[h : h + 1, cols] = top + jnp.log(total)

    half = length // 2
    keep[...] = o_t[:, rows_at(y, half)].astype(LOW)
    send[...] = o_t[:, rows_at(1 - y, half)].astype(LOW)


def gelu_parts(u):
    phi = 0.5 + 0.5 * lax.erf(u * 0.7071067811865476)
    bell = jnp.exp(-0.5 * u * u)
    return u * phi, phi + u * (bell * 0.3989422804014327)


def merge_kernel(table, a0, a1, a2, a3, tok, vec, mine, theirs, att, normed, rstd, low, bias, work):
    seq, y, c = table[0], table[1], table[2]
    count, width = normed.shape
    half = width // 2
    for j, a in enumerate((a0, a1, a2, a3)):
        att[rows_at(seq ^ j, 192), :] = a[...]
    bias[...] = jnp.broadcast_to(
        jnp.concatenate([vec[6:7, :width], vec[7:8, :width]], axis=1), bias.shape
    )
    work[:, rows_at(c, half)] = tn(att[...], mine[...])
    work[:, rows_at(1 - c, half)] = tn(att[...], theirs[...])
    values = tok[rows_at(y, count), :width].astype(FULL) + work[...] + vec[0:1, :width]
    center = values - jnp.mean(values, axis=1, keepdims=True)
    scale = lax.rsqrt(jnp.mean(center * center, axis=1, keepdims=True) + 1e-12)
    center = center * scale
    normed[...] = center
    rstd[...] = jnp.broadcast_to(scale, rstd.shape)
    low[...] = (center * vec[1:2, :width] + vec[2:3, :width]).astype(LOW)


def gelu_kernel(parts, table, low, bias, *refs):
    pieces, (e, act, slope) = refs[:parts], refs[parts:]
    piece = e.shape[0] // parts
    for p, ref in enumerate(pieces):
        e[rows_at(table[4 + p], piece), :] = ref[...]

    @pl.loop(0, act.shape[1] // 256)
    def _(i):
        cols = rows_at(i, 256)
        pre = nn(low[...], e[:, cols]) + bias[0:1, cols]
        value, grad = gelu_parts(pre)
        act[:, cols] = value.astype(LOW)
        slope[:, cols] = grad.astype(LOW)


def shrink_kernel(parts, table, act, *refs):
    pieces, (sh, part) = refs[:parts], refs[parts:]
    piece = sh.shape[0] // parts
    for p, ref in enumerate(pieces):
        sh[rows_at(table[4 + p], piece), :] = ref[...]
    part[...] = nn(act[...], sh[...]).astype(LOW)


def second_kernel(table, normed, vec, mine, theirs, cot_mine, cot_theirs, *refs):
    out, dsec, dz, sums, work = refs
    c = table[2]
    rows = cot_mine.shape[0]
    width = normed.shape[1]
    first = normed[...] * vec[1:2, :width] + vec[2:3, :width]
    second = first + (mine[...].astype(FULL) + theirs[...].astype(FULL)) + vec[3:4, :width]
    center = second - jnp.mean(second, axis=1, keepdims=True)
    scale = lax.rsqrt(jnp.mean(center * center, axis=1, keepdims=True) + 1e-12)
    center = center * scale
    gain = vec[4:5, :width]
    work[...] = center * gain + vec[5:6, :width]
    out[...] = work[rows_at(c, rows), :].astype(LOW)
    work[rows_at(c, rows), :] = cot_mine[...].astype(FULL)
    work[rows_at(1 - c, rows), :] = cot_theirs[...].astype(FULL)
    up = work[...]
    sums[...] = jnp.zeros(sums.shape, FULL)
    sums[0:1, :] = jnp.sum(up * center, axis=0, keepdims=True)
    sums[1:2, :] = jnp.sum(up, axis=0, keepdims=True)
    scaled = up * gain
    grad = scale * (
        scaled
        - jnp.mean(scaled, axis=1, keepdims=True)
        - center * jnp.mean(scaled * center, axis=1, keepdims=True)
    )
    dsec[...] = grad
    dz[...] = grad.astype(LOW)
    sums[2:3, :] = jnp.sum(dz[...].astype(FULL), axis=0, keepdims=True)


def hidden_kernel(table, dz, slope, e, sh, dpre, dfp, sums):
    hidden = sh.shape[0]
    sums[...] = jnp.zeros(sums.shape, FULL)

    @pl.loop(0, hidden // 256)
    def _(i):
        cols = rows_at(i, 256)
        value = nt(dz[...], sh[cols, :]) * slope[:, cols].astype(FULL)
        value = value.astype(LOW)
        dpre[:, cols] = value
        sums[0:1, cols] = jnp.sum(value.astype(FULL), axis=0, keepdims=True)

    dfp[...] = nt(dpre[...], e[...]).astype(LOW)


def put_blocks(parts, table, work, block, outs, extra=None):
    for i, ref in enumerate(outs):
        for j in range(parts // 4):
            at = table[4 + parts + i * (parts // 4) + j]
            ref[j, :block, :] = work[rows_at(at, block), :]
            if extra is not None:
                ref[j, block:, :] = extra


def shrink_grad_kernel(parts, table, act, dz, *refs):
    outs, work = refs[:4], refs[4]
    work[...] = tn(act[...], dz[...]).astype(LOW)
    put_blocks(parts, table, work, work.shape[0] // parts, outs)


def first_kernel(
    table, mine, theirs, dsec, normed, rstd, vec, wm, wm_other, dres, dbr, dkeep, dsend, sums, work
):
    seq, c = table[0], table[2]
    width = normed.shape[1]
    half = width // 2
    rows = dres.shape[0]
    up = (mine[...].astype(FULL) + theirs[...].astype(FULL)) + dsec[...]
    center = normed[...]
    sums[...] = jnp.zeros(sums.shape, FULL)
    sums[0:1, :] = jnp.sum(up * center, axis=0, keepdims=True)
    sums[1:2, :] = jnp.sum(up, axis=0, keepdims=True)
    scaled = up * vec[1:2, :width]
    work[...] = rstd[:, 0:1] * (
        scaled
        - jnp.mean(scaled, axis=1, keepdims=True)
        - center * jnp.mean(scaled * center, axis=1, keepdims=True)
    )
    dbr[...] = work[...].astype(LOW)
    dres[...] = work[rows_at(c, rows), :]
    sums[2:3, :] = jnp.sum(dbr[...].astype(FULL), axis=0, keepdims=True)
    for j, ref in ((0, dkeep), (2, dsend)):
        at = rows_at(seq ^ j, 192)
        ref[...] = (
            nt(wm[at, :], dbr[:, rows_at(c, half)])
            + nt(wm_other[at, :], dbr[:, rows_at(1 - c, half)])
        ).astype(LOW)


def expand_grad_kernel(parts, table, low, dpre, att, dbr, sums_two, sums_hid, sums_one, *refs):
    outs, (work, rows) = refs[:4], refs[4:]
    c = table[2]
    width = low.shape[1]
    half = width // 2
    work[:, :half] = nn(att[...], dbr[:, rows_at(c, half)]).astype(LOW)
    work[:, half:] = tn(low[...], dpre[...]).astype(LOW)
    rows[...] = jnp.zeros(rows.shape, FULL)
    rows[0:1, :width] = sums_one[2:3, :]
    rows[1:3, :width] = sums_one[0:2, :]
    rows[3:4, :width] = sums_two[2:3, :]
    rows[4:6, :width] = sums_two[0:2, :]
    rows[6:7, : dpre.shape[1]] = sums_hid[0:1, :]
    put_blocks(parts, table, work, width // parts, outs, rows[...].astype(LOW))


def attend_back_kernel(
    parts, table, tok, qp, kp, v, q_t, k_t, o_t, lse, dkeep, dother, *refs
):
    outs, refs = refs[:4], refs[4:]
    grads, probs, dscores, d_t, d_rows, q_rows, heads, v_heads, dq_t, work = refs
    y = table[1]
    length = tok.shape[0]
    width = work.shape[0]
    block = width // parts
    half = length // 2
    d_t[192:, :] = jnp.zeros((64, length), LOW)
    d_t[:192, rows_at(y, half)] = dkeep[...]
    d_t[:192, rows_at(1 - y, half)] = dother[...]
    lane = lax.broadcasted_iota(jnp.int32, (256, 256), 1)
    for i in range(length // 256):
        here = slice(i * 256, (i + 1) * 256)
        d = d_t[:, here].astype(FULL).T
        k = kp[here, :].astype(FULL)
        q = qp[here, :].astype(FULL)
        vv = v[here, :].astype(FULL)
        for h in range(3):
            own = lane // HEAD_DIM == h
            at = slice(h * length + i * 256, h * length + (i + 1) * 256)
            d_rows[at, :] = jnp.where(own, d, 0.0).astype(LOW)
            q_rows[at, :] = jnp.where(own, q, 0.0).astype(LOW)
            heads[h, here, :] = jnp.where(own | (lane >= 192), k, 0.0).astype(LOW)
            v_heads[h, here, :] = jnp.where(own, vv, 0.0).astype(LOW)
    dq_t[192:, :] = jnp.zeros((64, length), FULL)

    @pl.loop(0, length // 256)
    def _(i):
        cols = rows_at(i, 256)
        for h in range(3):
            mine = slice(HEAD_DIM * h, HEAD_DIM * (h + 1))
            out = pl.ds(pl.multiple_of(h * length + i * 256, 256), 256)
            prob = jnp.exp(nn(heads[h], q_t[:, cols]) - lse[h : h + 1, cols])
            probs[:, out] = prob.astype(LOW)
            delta = jnp.sum(
                d_t[mine, cols].astype(FULL) * o_t[mine, cols], axis=0, keepdims=True
            )
            grad = (prob * (nn(v_heads[h], d_t[:, cols]) - delta)).astype(LOW)
            dscores[:, out] = grad
            dq_t[mine, cols] = nn(k_t[mine, :], grad) * 0.125

    for i in range(length // 256):
        here = slice(i * 256, (i + 1) * 256)
        dv = nn(probs[here, :], d_rows[...])
        dk = pltpu.roll(nn(dscores[here, :], q_rows[...]), 192, 1)
        dq = dq_t[:, here].T
        grads[here, :256] = jnp.where(lane < 192, dq, dk).astype(LOW)
        grads[here, 256:384] = dk[:, :128].astype(LOW)
        grads[here, 384:] = dv.astype(LOW)
    work[...] = tn(tok[:, :width], grads[...]).astype(LOW)
    total = jnp.sum(grads[...].astype(FULL), axis=0, keepdims=True)
    total = jnp.broadcast_to(total, (EXTRA, total.shape[1])).astype(LOW)
    put_blocks(parts, table, work, block, outs, total)


def input_grad_kernel(table, grads, w, send, keep, work):
    seq = table[0]
    rows = send.shape[1]
    work[...] = nt(grads[...], w[...]).astype(LOW)
    for b in range(2):
        send[b] = work[rows_at(seq ^ (1 + 2 * b), rows), :]
        keep[b] = work[rows_at(seq ^ (2 * b), rows), :]


def pair_kernel(keep, got, *outs):
    for k, ref in enumerate(outs):
        ref[...] = (keep[k].astype(FULL) + got[k].astype(FULL)).astype(LOW)


def projection_kernel(table, wq, wk, wv, merge, rest, out):
    seq, c = table[0], table[2]
    share, width = wq.shape
    slim, half = width // 4, width // 2
    for s in range(4):

        @pl.when(seq == s)
        def _():
            cols = slice(slim * s, slim * (s + 1))
            for i, ref in enumerate((wq, wk, wv)):
                out[:share, slim * i : slim * (i + 1)] = ref[:, cols]

    out[:share, 3 * slim : 640] = jnp.zeros((share, 640 - 3 * slim), LOW)
    out[:share, 640:] = merge[:, rows_at(c, half)]
    out[share:, :] = rest[...]


def wide_kernel(unit, table, wide, out):
    c = table[2]
    for s in range(2):

        @pl.when(c == s)
        def _():
            for f in range(out.shape[1] // unit):
                start = 2 * unit * f + unit * s
                out[:, unit * f : unit * (f + 1)] = wide[:, start : start + unit]


def final_projection_kernel(table, p0, p1, p2, p3, dq, dk, dv, rows, stack):
    seq = table[0]
    share = dq.shape[0]
    slim = dq.shape[1] // 4
    for j, p in enumerate((p0, p1, p2, p3)):
        stack[j] = p[...].astype(FULL)
    for i in range(4):
        part = stack[seq ^ i]
        cols = slice(slim * i, slim * (i + 1))
        for g, ref in enumerate((dq, dk, dv)):
            ref[:, cols] = part[:share, slim * g : slim * (g + 1)]
            if g != 1:
                rows[4 * g : 4 * g + 8, cols] = part[share : share + 8, slim * g : slim * (g + 1)]


def final_wide_kernel(table, mine, theirs, merge, wide, rows, both):
    c = table[2]
    share, half = merge.shape[0], merge.shape[1] // 2
    hidden = wide.shape[1]
    unit = hidden // 16
    both[c] = mine[...]
    both[1 - c] = theirs[...]
    for s in range(2):
        merge[:, half * s : half * (s + 1)] = both[s, :share, :half]
        for f in range(8):
            start = half + unit * f
            at = 2 * unit * f + unit * s
            wide[:, at : at + unit] = both[s, :share, start : start + unit]
        rows[s] = both[s, share:, :]


def after(x, *others):
    return lax.optimization_barrier((x,) + others)[0]


class Link:
    def __init__(self, window=2):
        self.window = window
        self.done = []

    def send(self, x, axis, pairs, *others):
        if len(self.done) >= self.window:
            others = others + (self.done[-self.window],)
        if others:
            x = after(x, *others)
        self.done.append(lax.ppermute(x, axis, pairs))
        return self.done[-1]


NEAR_PAIRS = [(i, i ^ 1) for i in range(8)]
SHIFTS = {k: [(i, (i + 2 * k) % 8) for i in range(8)] for k in (1, 2, 3)}


def swap_core(x):
    return lax.ppermute(x, "seq", CORE_PAIRS)


def gather_whole(shard, count, extra):
    whole = lax.all_gather(shard, "fsdp", axis=0)
    rows = shard.shape[0] - extra
    main = whole[:, :rows].reshape(count * rows, shard.shape[1])
    if not extra:
        return [main]
    rest = jnp.sum(whole[:, rows:].astype(FULL), axis=0).astype(LOW)
    return [jnp.concatenate([main, rest], axis=0)]


def scatter_whole(send, keep, count, extra):
    both = jnp.concatenate([send, keep], axis=0)
    rows = both.shape[1] - extra
    main = both[:, :rows].reshape(count, -1, both.shape[2])
    rest = jnp.broadcast_to(both[:1, rows:], (count, extra, both.shape[2]))
    both = jnp.concatenate([main, rest], axis=1)
    return lax.psum_scatter(both, "fsdp", scatter_dimension=0).astype(FULL)


def pair_sum(keep, got):
    shape = keep.shape[1:]
    return pl.pallas_call(
        pair_kernel,
        name="pair",
        out_shape=[jax.ShapeDtypeStruct(shape, LOW)] * keep.shape[0],
        in_specs=[VMEM, VMEM],
        out_specs=[VMEM] * keep.shape[0],
        cost_estimate=pl.CostEstimate(
            flops=0, bytes_accessed=0, transcendentals=0
        ),
    )(keep, got)


def body(
    count,
    tokens,
    segment_ids,
    query_weight,
    key_weight,
    value_weight,
    merge_weight,
    query_bias,
    value_bias,
    merge_bias,
    first_gain,
    first_shift,
    expand_weight,
    expand_bias,
    shrink_weight,
    shrink_bias,
    second_gain,
    second_shift,
    cotangent,
):
    rows, width = tokens.shape[1:]
    hidden = expand_weight.shape[1]
    share = width // count
    unit = hidden // count // 2
    slim = width // 4
    half = width // 2
    length = 4 * rows
    near_rows = 2 * rows
    seq = lax.axis_index("seq")
    own = lax.axis_index("fsdp")
    c, y = seq % 2, seq // 2
    z, x = own // 2, own % 2
    ring = count == 8
    if ring:
        parts = parts_in = 8
        mine = [((z - k) % 4) * 2 + x for k in (0, 1, 3, 2)]
        pieces = mine + [2 * (m // 2) + 1 - x for m in mine]
        there = [2 * ((z + k) % 4) for k in (2, 1, 3, 0)]
        blocks = [t + 1 - x for t in there] + [t + x for t in there]
    else:
        parts, parts_in = 4, 1
        pieces, blocks = [0], [0, 1, 2, 3]
    pieces = pieces + [0] * (parts - parts_in)
    table = jnp.stack([seq, y, c, z] + pieces + blocks).astype(jnp.int32)
    x_link, y_link, z_link = Link(), Link(), Link()

    def near(v, *others):
        return x_link.send(v, "fsdp", NEAR_PAIRS, *others)

    def along(v, k, *others):
        return z_link.send(v, "fsdp", SHIFTS[k], *others)

    def across(v, *others):
        return y_link.send(v, "seq", CHIP_PAIRS, *others)

    pair = jnp.stack([query_bias, value_bias])
    pair = lax.dynamic_update_slice(jnp.zeros((2, width), LOW), pair, (0, share * own))
    pair = lax.dynamic_slice(pair, (0, slim * seq), (2, slim))
    bias_row = jnp.concatenate([pair[0:1], jnp.zeros((1, slim), LOW), pair[1:2]], axis=1)
    rest = jnp.zeros((HEADER, 640 + half), LOW)
    stack = jnp.stack(
        [merge_bias, first_gain, first_shift, shrink_bias, second_gain, second_shift]
    )
    rest = lax.dynamic_update_slice(rest, stack, (0, share * own))
    chunk = lax.dynamic_slice(expand_bias, (unit * c,), (unit,)).reshape(1, unit)
    rest = lax.dynamic_update_slice(
        rest, chunk, (6 + unit * own // width, unit * own % width)
    )
    rest = lax.dynamic_update_slice(rest, bias_row, (8, 0))
    (shard,) = call(
        projection_kernel,
        "projection",
        [((share + HEADER, 640 + half), LOW)],
        table,
        query_weight,
        key_weight,
        value_weight,
        merge_weight,
        rest,
    )
    inputs = tokens.reshape(rows, width)
    marks = jnp.broadcast_to(segment_ids.reshape(rows, 1).astype(LOW), (rows, 128))

    def wide_shard(dep):
        weight = after(expand_weight, dep)
        if ring:
            return call(
                partial(wide_kernel, unit),
                "wide",
                [((share, hidden // 2), LOW)],
                table,
                weight,
            )[0]
        wide = weight.reshape(share, count, 2, unit)
        return jnp.where(c == 0, wide[:, :, 0], wide[:, :, 1]).reshape(share, hidden // 2)

    low_shard = lax.dynamic_slice(shrink_weight, (unit * c, 0), (unit, width))
    if ring:
        q1 = along(shard, 1)
        q3 = along(shard, 3)
        q2 = along(shard, 2)
        qx0 = near(shard)
        inputs = jnp.concatenate([inputs, marks], axis=1)
        t_two = across(inputs)
        t_one = swap_core(inputs)
        qx1 = near(q1)
        e0 = wide_shard(q1)
        ex0 = near(e0)
        qx3 = near(q3)
        qx2 = near(q2)
        w_pieces = [shard, q1, q3, q2, qx0, qx1, qx3, qx2]
        t_three = swap_core(t_two)
        e1 = along(e0, 1)
        e3 = along(e0, 3)
        ex1 = near(e1)
        s0 = after(low_shard, q3)
        sx0 = near(s0)
        e2 = along(e0, 2)
        w_pieces[-1] = after(qx2, e1)
    else:
        w_pieces = gather_whole(shard, count, HEADER)
        inputs = jnp.concatenate([inputs, marks], axis=1)
        t_two = across(inputs)
        t_one = swap_core(inputs)
        t_three = swap_core(t_two)
        e_pieces = gather_whole(wide_shard(shard), count, 0)
        sh_pieces = gather_whole(low_shard, count, 0)

    tok, w, wm, vec, qp, kp, v, q_t, k_t, o_t, lse, keep, send = call(
        partial(attend_kernel, parts_in),
        "attend",
        [
            ((length, width + 128), LOW),
            ((width, 640), LOW),
            ((width, half), LOW),
            ((HEADER, 640 + half), FULL),
            ((length, 256), LOW),
            ((length, 256), LOW),
            ((length, 256), LOW),
            ((256, length), LOW),
            ((256, length), LOW),
            ((slim, length), FULL),
            ((8, length), FULL),
            ((slim, near_rows), LOW),
            ((slim, near_rows), LOW),
        ],
        table,
        inputs,
        t_one,
        t_two,
        t_three,
        *w_pieces,
        scratch=[((3, length, 256), LOW), ((256, length), LOW)],
        flops=14e9,
        nbytes=1e7,
    )
    a_two = across(send)
    a_one = swap_core(keep)
    wm_other = swap_core(wm)
    a_three = swap_core(a_two)
    cot = cotangent.reshape(rows, width)
    cot_other = swap_core(after(cot, keep))
    if ring:
        ex3 = near(e3, keep)
        s1 = along(s0, 1, keep)
        ex2 = near(e2)
        s3 = along(s0, 3)
        s2 = along(s0, 2)
        sx1 = near(s1)
        sx3 = near(s3)
        sx2 = near(s2)
        e_pieces = [e0, e1, e3, e2, ex0, ex1, ex3, ex2]
        sh_pieces = [s0, s1, s3, s2, sx0, sx1, sx3, sx2]

    att, normed, rstd, low, e_bias = call(
        merge_kernel,
        "merge",
        [
            ((width, near_rows), LOW),
            ((near_rows, width), FULL),
            ((near_rows, 128), FULL),
            ((near_rows, width), LOW),
            ((EXTRA, hidden // 2), FULL),
        ],
        table,
        keep,
        a_one,
        a_two,
        a_three,
        tok,
        vec,
        wm,
        wm_other,
        scratch=[((near_rows, width), FULL)],
        flops=5e9,
        nbytes=1e7,
    )
    if ring:
        e_pieces[-1] = after(e_pieces[-1], low)
    e, act, slope = call(
        partial(gelu_kernel, parts_in),
        "gelu",
        [
            ((width, hidden // 2), LOW),
            ((near_rows, hidden // 2), LOW),
            ((near_rows, hidden // 2), LOW),
        ],
        table,
        low,
        e_bias,
        *e_pieces,
        flops=8e9,
        nbytes=1e7,
    )
    sh, part = call(
        partial(shrink_kernel, parts_in),
        "shrink",
        [((hidden // 2, width), LOW), ((near_rows, width), LOW)],
        table,
        act,
        *sh_pieces,
        flops=4e9,
        nbytes=1e7,
    )
    part_other = swap_core(part)
    out, dsec, dz, sums_two = call(
        second_kernel,
        "second",
        [
            ((rows, width), LOW),
            ((near_rows, width), FULL),
            ((near_rows, width), LOW),
            ((EXTRA, width), FULL),
        ],
        table,
        normed,
        vec,
        part,
        part_other,
        cot,
        cot_other,
        scratch=[((near_rows, width), FULL)],
        flops=5e9,
        nbytes=8e6,
    )
    sh_blocks = call(
        partial(shrink_grad_kernel, parts),
        "shrink_grad",
        [((parts // 4, hidden // 2 // parts, width), LOW)] * 4,
        table,
        act,
        dz,
        scratch=[((hidden // 2, width), LOW)],
        flops=5e9,
        nbytes=5e6,
    )
    dpre, dfp, sums_hid = call(
        hidden_kernel,
        "hidden",
        [
            ((near_rows, hidden // 2), LOW),
            ((near_rows, width), LOW),
            ((EXTRA, hidden // 2), FULL),
        ],
        table,
        after(dz, sh_blocks[0]),
        slope,
        e,
        sh,
        flops=6e9,
        nbytes=8e6,
    )
    dfp_other = swap_core(dfp)
    dres, dbr, dkeep, dsend, sums_one = call(
        first_kernel,
        "first",
        [
            ((rows, width), FULL),
            ((near_rows, width), LOW),
            ((slim, near_rows), LOW),
            ((slim, near_rows), LOW),
            ((EXTRA, width), FULL),
        ],
        table,
        dfp,
        dfp_other,
        dsec,
        normed,
        rstd,
        vec,
        wm,
        wm_other,
        scratch=[((near_rows, width), FULL)],
        flops=5e9,
        nbytes=8e6,
    )
    dother = across(dsend)
    em_blocks = call(
        partial(expand_grad_kernel, parts),
        "expand_grad",
        [((parts // 4, width // parts + EXTRA, half + hidden // 2), LOW)] * 4,
        table,
        low,
        dpre,
        att,
        dbr,
        sums_two,
        sums_hid,
        sums_one,
        scratch=[((width, half + hidden // 2), LOW), ((EXTRA, half + hidden // 2), FULL)],
        flops=5e9,
        nbytes=8e6,
    )
    def finish_half(blocks, got, i):
        if i == 0:
            p2, p1 = pair_sum(blocks[2], got)
            return along(p2, 2), along(p1, 1), p1
        p3, p0 = pair_sum(blocks[3], got)
        return along(p3, 3), p0

    if ring:
        sh_got = [near(sh_blocks[0]), near(sh_blocks[1])]
        em_got = [near(em_blocks[0])]
        r2, r1, mark = finish_half(sh_blocks, after(sh_got[0], em_blocks[0]), 0)
        sh_sums = [r2, r1]
        gate = mark
    else:
        gate = em_blocks[0]
    *w_blocks, grads = call(
        partial(attend_back_kernel, parts),
        "attend_back",
        [((parts // 4, width // parts + EXTRA, 640), LOW)] * 4 + [((length, 640), LOW)],
        table,
        tok,
        qp,
        kp,
        v,
        q_t,
        k_t,
        o_t,
        lse,
        dkeep,
        after(dother, gate),
        scratch=[
            ((length, 3 * length), LOW),
            ((length, 3 * length), LOW),
            ((256, length), LOW),
            ((3 * length, 256), LOW),
            ((3 * length, 256), LOW),
            ((3, length, 256), LOW),
            ((3, length, 256), LOW),
            ((256, length), FULL),
            ((width, 640), LOW),
        ],
        flops=16e9,
        nbytes=1e7,
    )
    if ring:
        sh_sums += list(finish_half(sh_blocks, after(sh_got[1], grads), 1))
        gate = sh_sums[-1]
    else:
        gate = w_blocks[0]
    x_send, x_keep = call(
        input_grad_kernel,
        "input_grad",
        [((2, rows, width), LOW)] * 2,
        table,
        after(grads, gate),
        w,
        scratch=[((length, width), LOW)],
        flops=4e9,
        nbytes=5e6,
    )
    x_sum = x_keep.astype(FULL) + swap_core(x_send).astype(FULL)
    x_other = across(x_sum[1].astype(LOW))
    in_grad = dres + x_sum[0] + x_other.astype(FULL)


    if ring:
        em_got.append(near(em_blocks[1]))
        r2, r1, mark = finish_half(em_blocks, after(em_got[0], x_send), 0)
        em_sums = [r2, r1]
        w_got = [near(w_blocks[0])]
        em_sums += list(finish_half(em_blocks, after(em_got[1], mark), 1))
        w_got.append(near(w_blocks[1]))
        r2, r1, mark = finish_half(w_blocks, after(w_got[0], em_sums[-1]), 0)
        w_sums = [r2, r1] + list(finish_half(w_blocks, after(w_got[1], mark), 1))
        shrink_own, em_own, w_own = [
            g[0].astype(FULL) + g[1].astype(FULL) + g[2].astype(FULL) + g[3].astype(FULL)
            for g in (sh_sums, em_sums, w_sums)
        ]
    else:
        shrink_own, em_own, w_own = [
            scatter_whole(
                jnp.concatenate(g[:2], axis=0), jnp.concatenate(g[2:], axis=0), count, extra
            )
            for g, extra in ((sh_blocks, 0), (em_blocks, EXTRA), (w_blocks, EXTRA))
        ]
    w_own = w_own.astype(LOW)

    def over_chips(part):
        part = part.astype(LOW)
        return part.astype(FULL) + across(part).astype(FULL)

    def both_cores(part):
        other = swap_core(part)
        return jnp.where(c == 0, part, other), jnp.where(c == 0, other, part)

    sh_low, sh_high = both_cores(over_chips(shrink_own))
    d_shrink = jnp.concatenate([sh_low, sh_high], axis=0)
    em_own = over_chips(em_own)
    w_two = across(w_own)
    w_one = swap_core(w_own)
    w_three = swap_core(w_two)
    em_other = swap_core(em_own)
    d_merge, d_expand, em_rows = final_wide(
        ring, table, c, em_own, em_other, share, half, hidden, unit, count
    )
    small = lax.dynamic_slice(em_rows[0], (0, share * own), (6, share))
    d_b_expand = jnp.concatenate(
        [
            lax.dynamic_slice(em_rows[i], (6, unit * own), (1, unit)).reshape(unit)
            for i in range(2)
        ]
    )
    d_q, d_k, d_v, w_rows = call(
        final_projection_kernel,
        "final_projection",
        [((share, width), FULL)] * 3 + [((16, width), FULL)],
        table,
        w_own,
        w_one,
        w_two,
        w_three,
        scratch=[((4, share + EXTRA, 640), FULL)],
    )
    w_rows = lax.dynamic_slice(w_rows, (0, share * own), (16, share))

    return (
        out.reshape(1, rows, width),
        in_grad.astype(LOW).reshape(1, rows, width),
        d_q,
        d_k,
        d_v,
        d_merge,
        w_rows[0],
        w_rows[8],
        small[0],
        small[1],
        small[2],
        d_expand,
        d_b_expand,
        d_shrink,
        small[3],
        small[4],
        small[5],
    )


def final_wide(ring, table, c, mine, theirs, share, half, hidden, unit, count):
    if ring:
        return call(
            final_wide_kernel,
            "final_wide",
            [
                ((share, 2 * half), FULL),
                ((share, hidden), FULL),
                ((2, EXTRA, half + hidden // 2), FULL),
            ],
            table,
            mine,
            theirs,
            scratch=[((2, share + EXTRA, half + hidden // 2), FULL)],
        )
    low, high = jnp.where(c == 0, mine, theirs), jnp.where(c == 0, theirs, mine)
    merge = jnp.concatenate([low[:share, :half], high[:share, :half]], axis=1)
    wide = jnp.stack(
        [part[:share, half:].reshape(share, count, unit) for part in (low, high)], axis=2
    ).reshape(share, hidden)
    return merge, wide, jnp.stack([low[share:], high[share:]])


def solution(mesh):
    row, flat = P("fsdp", None), P("fsdp")
    cube = P("fsdp", "seq", None)
    return jax.shard_map(
        partial(body, mesh.shape["fsdp"]),
        mesh=mesh,
        in_specs=(cube, P("fsdp", "seq"))
        + (row,) * 4
        + (flat,) * 5
        + (row, flat, row)
        + (flat,) * 3
        + (cube,),
        out_specs=(cube, cube) + (row,) * 4 + (flat,) * 5 + (row, flat, row) + (flat,) * 3,
        check_vma=False,
    )
```

time: 330 us -> 284 us (0.86); the launches traced: 324 us -> 282 us
  waiting for transfers between devices: 130 us -> 54.2 us
  starting transfers between devices: 61.5 us -> 94.9 us
  Pallas kernels: 83.1 us -> 103 us
  local copies, waits for them, and re-layouts: 33.9 us -> 16.5 us
    ppermute x40 -> x43, waiting for transfers between devices: 125 us -> 49.4 us  [send(): self.done.append(lax.ppermute(x, axis, pairs))]
    ppermute x40 -> x43, starting transfers between devices: 40.3 us -> 61.1 us  [send(): self.done.append(lax.ppermute(x, axis, pairs))]
    ppermute x13, starting transfers between devices: 21.2 us -> 33.8 us  [swap_core(): return lax.ppermute(x, 'seq', CORE_PAIRS)]
    pallas_call x0 -> x6, Pallas kernels: none -> 12.5 us  [pair_sum(): pl.pallas_call(pair_kernel, name='pair', out_shape=[jax.ShapeDtypeStruct(...]
    pallas_call x11 -> x15, Pallas kernels: 83.1 us -> 90.2 us  [call(): pl.pallas_call(kernel, name=name, out_shape=[jax.ShapeDtypeStruct(shape,...]
    reshape x2 -> x0, local copies, waits for them, and re-layouts: 5.47 us -> none  [the longest x1 2.85 us: body(): wide = expand_weight.reshape(share, count, 2, unit)]
    slice x13 -> x1, local copies, waits for them, and re-layouts: 5.42 us -> 0.87 us  [body(): em_rows[i]]
    unnamed x117 -> x98, local copies, waits for them, and re-layouts: 13 us -> 9.89 us
  transfers between devices with their start and end apart: 53 -> 56, of which waited for: 23 -> 21; matrix products, arithmetic and copies ran while one was open for 8% -> 4% of each run, Pallas kernels for 16% -> 27%
where the time goes in v2:
time: 284 us; the launch traced here: 282 us
  Pallas kernels  103 us (36%)
  starting transfers between devices  94.9 us (33%)
  waiting for transfers between devices  54.2 us (19%)
  local copies, waits for them, and re-layouts  16.5 us (6%)
  other arithmetic  12.3 us (4%)
    pallas_call x15, Pallas kernels, call(): pl.pallas_call(kernel, name=name, out_shape=[jax.ShapeDtypeStruct(shape,...  90.2 us
    ppermute x43, starting transfers between devices, send(): self.done.append(lax.ppermute(x, axis, pairs))  61.1 us
    ppermute x43, waiting for transfers between devices, send(): self.done.append(lax.ppermute(x, axis, pairs))  49.4 us
    ppermute x13, starting transfers between devices, swap_core(): return lax.ppermute(x, 'seq', CORE_PAIRS)  33.8 us
    pallas_call x6, Pallas kernels, pair_sum(): pl.pallas_call(pair_kernel, name='pair', out_shape=[jax.ShapeDtypeStruct(...  12.5 us
    unnamed x98, local copies, waits for them, and re-layouts  9.89 us
  transfers between devices with their start and end apart: 56, of which 21 were waited for; matrix products, arithmetic and copies ran while one was open for 4% of the time, Pallas kernels for 27%

profile of v2, /device:TPU:9, one launch (start us, length us, event | category | flops | bytes accessed | tf_op | source)
XLA Modules:
  0.0 282.0 jit_solution(14989459804282847353)
XLA Ops:
  5.4 1.9 projection.1.refs_0_
  10.5 1.7 collective-permute-start.6
  12.3 1.7 collective-permute-done.3.refs_1_
  15.4 2.3 collective-permute-start.5
  17.7 1.9 wide.1.refs_0_
  24.8 7.7 %collective-permute-start = (bf16[256,896]{1,0:T(8,128)(2,1)S(1)}, bf16[256,896]{1,0:T(8,128)(2,1)S(1)}, u32[]{:S(2)}, u32[]{:S(2)}) collective-permute-start(bf16[256,896]{1,0:T(8,128)(2,1)S(1)} %pad_maximum_fusion.1.t0), channel_id=1, source_target_pairs={{0,8},{8,0},{16,24},{24,16},{1,9},{9,1},{17,25},{25,17},{2,10},{10... | collective-permute-start | bytes 1376264 | tf_op jit(solution)/shard_map/ppermute | solution.py:420
  33.6 6.6 %collective-permute-start.16 = (bf16[96,1536]{1,0:T(8,128)(2,1)}, bf16[96,1536]{1,0:T(8,128)(2,1)}, u32[]{:S(2)}, u32[]{:S(2)}) collective-permute-start(bf16[96,1536]{1,0:T(8,128)(2,1)} %wide.1.refs_0_), channel_id=1, source_target_pairs={{0,6},{1,7},{2,0},{3,1},{4,2},{5,3},{6,4},{7,5},{8,14},{9,15},{10,... | collective-permute-start | bytes 884744 | tf_op jit(solution)/shard_map/ppermute | solution.py:411
  41.6 1.7 collective-permute-start.17
  45.1 14.8 %attend.1 = (bf16[1024,896]{1,0:T(8,128)(2,1)}, bf16[768,640]{1,0:T(8,128)(2,1)}, bf16[768,384]{1,0:T(8,128)(2,1)}, f32[16,1024]{1,0:T(8,128)}, bf16[1024,256]{1...) custom-call(s32[20]{0:T(128)} %stack.110.table, ...), custom_call_target="tpu_custom_call" | custom-call | tf_op jit(solution)/shard_map/attend/pallas_call | solution.py:39
  59.9 5.0 %collective-permute-start.22 = (bf16[192,768]{1,0:T(8,128)(2,1)S(1)}, bf16[192,768]{1,0:T(8,128)(2,1)S(1)}, u32[]{:S(2)}, u32[]{:S(2)}) collective-permute-start(bf16[192,768]{1,0:T(8,128)(2,1)S(1)} %constant_dynamic-slice_fusion.5.refs_0_), channel_id=1, source_target_pairs={{0,2},{1,3},{2,4},{3,5},{4,6},{5,7},{6,0},{7,1},{8,10},{9,11},{10,... | collective-permute-start | bytes 884744 | tf_op jit(solution)/shard_map/ppermute | solution.py:411
  65.6 2.9 %collective-permute-start.15 = (bf16[768,384]{1,0:T(8,128)(2,1)}, bf16[768,384]{1,0:T(8,128)(2,1)S(1)}, u32[]{:S(2)}, u32[]{:S(2)}) collective-permute-start(bf16[768,384]{1,0:T(8,128)(2,1)} %get-tuple-element.148.mine.wm), channel_id=1, source_target_pairs={{0,8},{8,0},{16,24},{24,16},{1,9},{9,1},{17,25},{25,17},{2,10},{10... | collective-permute-start | bytes 1769480 | tf_op jit(solution)/shard_map/ppermute | solution.py:420
  71.9 9.5 %collective-permute-done.23.refs_2_ = bf16[192,768]{1,0:T(8,128)(2,1)S(1)} collective-permute-done((bf16[192,768]{1,0:T(8,128)(2,1)S(1)}, bf16[192,768]{1,0:T(8,128)(2,1)S(1)}, u32[]{:S(2)}, u32[]{:S(2)}) %collective-permute-start.23) | collective-permute-done | bytes 294944 | tf_op jit(solution)/shard_map/ppermute | solution.py:411
  85.1 9.4 %collective-permute-start.12 = (bf16[192,512]{1,0:T(8,128)(2,1)}, bf16[192,512]{1,0:T(8,128)(2,1)S(1)}, u32[]{:S(2)}, u32[]{:S(2)}) collective-permute-start(bf16[192,512]{1,0:T(8,128)(2,1)} %get-tuple-element.144.a0), channel_id=1, source_target_pairs={{0,8},{8,0},{16,24},{24,16},{1,9},{9,1},{17,25},{25,17},{2,10},{10... | collective-permute-start | bytes 589832 | tf_op jit(solution)/shard_map/ppermute | solution.py:420
  97.5 5.5 %merge.3 = (bf16[768,512]{1,0:T(8,128)(2,1)}, f32[512,768]{1,0:T(8,128)}, f32[512,128]{1,0:T(8,128)}, bf16[512,768]{1,0:T(8,128)(2,1)}, f32[8,1536]{1,0:T(8,128)}) custom-call(s32[20]{0:T(128)} %stack.110.table, bf16[192,512]{1,0:T(8,128)(2,1)} %get-tuple-element.144.a0, bf16[192,512]{1,0:T(8,128)(2,1)} %copy-done.39, bf16[192,512]{1,0:T(8,128)(2,1)} %copy-done.37, ...), custom_call_target="tpu_custom_call" | custom-call | tf_op jit(solution)/shard_map/merge/pallas_call | solution.py:39
  103.0 7.0 %gelu.1 = (bf16[768,1536]{1,0:T(8,128)(2,1)}, bf16[512,1536]{1,0:T(8,128)(2,1)}, bf16[512,1536]{1,0:T(8,128)(2,1)}) custom-call(s32[20]{0:T(128)} %stack.110.table, bf16[512,768]{1,0:T(8,128)(2,1)} %get-tuple-element.150.low, f32[8,1536]{1,0:T(8,128)} %get-tuple-element.151.bias, bf16[96,1536]{1,0:T(8,128)(2,1)} %wide.1.refs_0_, ...), custom_call_target="tpu_custom_call" | custom-call | tf_op jit(solution)/shard_map/gelu/pallas_call | solution.py:39
  110.8 4.5 %shrink.1 = (bf16[1536,768]{1,0:T(8,128)(2,1)}, bf16[512,768]{1,0:T(8,128)(2,1)}) custom-call(s32[20]{0:T(128)} %stack.110.table, bf16[512,1536]{1,0:T(8,128)(2,1)} %get-tuple-element.160.act, bf16[192,768]{1,0:T(8,128)(2,1)} %copy-done.5, bf16[192,768]{1,0:T(8,128)(2,1)} %copy-done.22, bf16[192,768]{1,0:T(8,128)(2,1)} %copy-done.23, ...), custom_call_target="tpu_custom_call" | custom-call | tf_op jit(solution)/shard_map/shrink/pallas_call | solution.py:39
  115.9 2.5 collective-permute-done.29.cot_theirs
  119.4 5.4 %second.1 = (bf16[256,768]{1,0:T(8,128)(2,1)}, f32[512,768]{1,0:T(8,128)}, bf16[512,768]{1,0:T(8,128)(2,1)}, f32[8,768]{1,0:T(8,128)}) custom-call(s32[20]{0:T(128)} %stack.110.table, f32[512,768]{1,0:T(8,128)} %get-tuple-element.149.normed, f32[16,1024]{1,0:T(8,128)} %get-tuple-element.147.vec, bf16[512,768]{1,0:T(8,128)(2,1)} %get-tuple-element.167.mine, ...), custom_call_target="tpu_custom_call" | custom-call | tf_op jit(solution)/shard_map/second/pallas_call | solution.py:39
  124.8 4.6 %shrink_grad.1 = (bf16[2,192,768]{2,1,0:T(8,128)(2,1)}, bf16[2,192,768]{2,1,0:T(8,128)(2,1)}, bf16[2,192,768]{2,1,0:T(8,128)(2,1)}, bf16[2,192,768]{2,1,0:T(8,128)(2,1)}) custom-call(s32[20]{0:T(128)} %stack.110.table, bf16[512,1536]{1,0:T(8,128)(2,1)} %get-tuple-element.160.act, bf16[512,768]{1,0:T(8,128)(2,1)} %get-tuple-element.172.dz), custom_call_target="tpu_custom_call" | custom-call | tf_op jit(solution)/shard_map/shrink_grad/pallas_call | solution.py:39
  129.4 8.0 %hidden.1 = (bf16[512,1536]{1,0:T(8,128)(2,1)}, bf16[512,768]{1,0:T(8,128)(2,1)}, f32[8,1536]{1,0:T(8,128)}) custom-call(s32[20]{0:T(128)} %stack.110.table, bf16[512,768]{1,0:T(8,128)(2,1)} %get-tuple-element.172.dz, bf16[512,1536]{1,0:T(8,128)(2,1)} %get-tuple-element.173.slope, bf16[768,1536]{1,0:T(8,128)(2,1)} %get-tuple-element.174.e, ...), custom_call_target="tpu_custom_call" | custom-call | tf_op jit(solution)/shard_map/hidden/pallas_call | solution.py:39
  140.8 5.4 %first.1 = (f32[256,768]{1,0:T(8,128)}, bf16[512,768]{1,0:T(8,128)(2,1)}, bf16[192,512]{1,0:T(8,128)(2,1)}, bf16[192,512]{1,0:T(8,128)(2,1)}, f32[8,768]{1,0:T(8,128)}) custom-call(s32[20]{0:T(128)} %stack.110.table, bf16[512,768]{1,0:T(8,128)(2,1)} %get-tuple-element.176.mine, bf16[512,768]{1,0:T(8,128)(2,1)} %copy-done.8, ...), custom_call_target="tpu_custom_call" | custom-call | tf_op jit(solution)/shard_map/first/pallas_call | solution.py:39
  146.1 5.7 %expand_grad.1 = (bf16[2,104,1920]{2,1,0:T(8,128)(2,1)}, bf16[2,104,1920]{2,1,0:T(8,128)(2,1)}, bf16[2,104,1920]{2,1,0:T(8,128)(2,1)}, bf16[2,104,1920]{2,1,0:T(8,128)(2,1)}) custom-call(s32[20]{0:T(128)} %stack.110.table, bf16[512,768]{1,0:T(8,128)(2,1)} %get-tuple-element.150.low, bf16[512,1536]{1,0:T(8,128)(2,1)} %get-tuple-element.192.dpre, ...), custom_call_target="tpu_custom_call" | custom-call | tf_op jit(solution)/shard_map/expand_grad/pallas_call | solution.py:39
  154.7 2.1 pair.6
  156.8 2.1 collective-permute-start.39
  158.9 6.3 %collective-permute-done.33.got = bf16[2,192,768]{2,1,0:T(8,128)(2,1)S(1)} collective-permute-done((bf16[2,192,768]{2,1,0:T(8,128)(2,1)}, bf16[2,192,768]{2,1,0:T(8,128)(2,1)S(1)}, u32[]{:S(2)}, u32[]{:S(2)}) %collective-permute-start.33) | collective-permute-done | bytes 589856 | tf_op jit(solution)/shard_map/ppermute | solution.py:411
  166.9 16.1 %attend_back.1 = (bf16[2,104,640]{2,1,0:T(8,128)(2,1)}, bf16[2,104,640]{2,1,0:T(8,128)(2,1)}, bf16[2,104,640]{2,1,0:T(8,128)(2,1)}, bf16[2,104,640]{2,1,0:T(8,128)(2,1)}, bf16[1024,640]{1,0:T(8,128)(2,1)}) custom-call(s32[20]{0:T(128)} %stack.110.table, bf16[1024,896]{1,0:T(8,128)(2,1)} %get-tuple-element.146.tok, bf16[1024,256]{1,0:T(8,128)(2,1)} %get-tuple-element.180.qp, ...), custom_call_target="tpu_custom_call" | custom-call | tf_op jit(solution)/shard_map/attend_back/pallas_call | solution.py:39
  183.0 2.2 pair.7
  185.2 4.3 %input_grad.1 = (bf16[2,256,768]{2,1,0:T(8,128)(2,1)}, bf16[2,256,768]{2,1,0:T(8,128)(2,1)}) custom-call(s32[20]{0:T(128)} %stack.110.table, bf16[1024,640]{1,0:T(8,128)(2,1)} %get-tuple-element.208.grads, bf16[768,640]{1,0:T(8,128)(2,1)} %get-tuple-element.209.w), custom_call_target="tpu_custom_call" | custom-call | tf_op jit(solution)/shard_map/input_grad/pallas_call | solution.py:39
  189.5 1.8 collective-permute-start.34
  192.3 1.7 collective-permute-start.40
  194.9 2.4 pair.8
  197.3 4.1 %collective-permute-done.43 = bf16[192,768]{1,0:T(8,128)(2,1)} collective-permute-done((bf16[192,768]{1,0:T(8,128)(2,1)S(1)}, bf16[192,768]{1,0:T(8,128)(2,1)}, u32[]{:S(2)}, u32[]{:S(2)}) %collective-permute-start.43) | collective-permute-done | bytes 294944 | tf_op jit(solution)/shard_map/ppermute | solution.py:411
  202.4 4.9 %collective-permute-done.40 = bf16[192,768]{1,0:T(8,128)(2,1)} collective-permute-done((bf16[192,768]{1,0:T(8,128)(2,1)}, bf16[192,768]{1,0:T(8,128)(2,1)}, u32[]{:S(2)}, u32[]{:S(2)}) %collective-permute-start.40) | collective-permute-done | bytes 294944 | tf_op jit(solution)/shard_map/ppermute | solution.py:411
  210.6 2.6 collective-permute-start.41
  213.2 2.4 pair.9
  215.6 8.5 %collective-permute-done.44 = bf16[104,1920]{1,0:T(8,128)(2,1)S(1)} collective-permute-done((bf16[104,1920]{1,0:T(8,128)(2,1)}, bf16[104,1920]{1,0:T(8,128)(2,1)S(1)}, u32[]{:S(2)}, u32[]{:S(2)}) %collective-permute-start.44) | collective-permute-done | bytes 399392 | tf_op jit(solution)/shard_map/ppermute | solution.py:411
  224.0 9.6 %collective-permute-start.45 = (bf16[104,1920]{1,0:T(8,128)(2,1)}, bf16[104,1920]{1,0:T(8,128)(2,1)S(1)}, u32[]{:S(2)}, u32[]{:S(2)}) collective-permute-start(bf16[104,1920]{1,0:T(8,128)(2,1)} %get-tuple-element.238), channel_id=1, source_target_pairs={{0,6},{1,7},{2,0},{3,1},{4,2},{5,3},{6,4},{7,5},{8,14},{9,15},{10,... | collective-permute-start | bytes 1198088 | tf_op jit(solution)/shard_map/ppermute | solution.py:411
  236.3 4.5 %collective-permute-done.45 = bf16[104,1920]{1,0:T(8,128)(2,1)S(1)} collective-permute-done((bf16[104,1920]{1,0:T(8,128)(2,1)}, bf16[104,1920]{1,0:T(8,128)(2,1)S(1)}, u32[]{:S(2)}, u32[]{:S(2)}) %collective-permute-start.45) | collective-permute-done | bytes 399392 | tf_op jit(solution)/shard_map/ppermute | solution.py:411
  242.0 1.8 collective-permute-done.35
  245.8 1.8 pair.10
  249.6 3.2 %collective-permute-start.55 = (f32[192,768]{1,0:T(8,128)}, f32[192,768]{1,0:T(8,128)}, u32[]{:S(2)}, u32[]{:S(2)}) collective-permute-start(f32[192,768]{1,0:T(8,128)} %convert_add_fusion.2), channel_id=1, source_target_pairs={{0,8},{8,0},{16,24},{24,16},{1,9},{9,1},{17,25},{25,17},{2,10},{10... | collective-permute-start | bytes 1769480 | tf_op jit(solution)/shard_map/ppermute | solution.py:420
  253.5 1.8 pair.11
  257.9 2.7 collective-permute-start.54
  260.5 2.1 fusion.3
  265.5 2.2 collective-permute-start.49
  268.0 3.0 %collective-permute-start.52 = (bf16[104,640]{1,0:T(8,128)(2,1)S(1)}, bf16[104,640]{1,0:T(8,128)(2,1)S(1)}, u32[]{:S(2)}, u32[]{:S(2)}) collective-permute-start(bf16[104,640]{1,0:T(8,128)(2,1)S(1)} %collective-permute-done.51.p2), channel_id=1, source_target_pairs={{0,8},{8,0},{16,24},{24,16},{1,9},{9,1},{17,25},{25,17},{2,10},{10... | collective-permute-start | bytes 399368 | tf_op jit(solution)/shard_map/ppermute | solution.py:420
  273.4 2.3 final_projection.1
  276.9 2.9 %final_wide.1 = (f32[96,768]{1,0:T(8,128)}, f32[96,3072]{1,0:T(8,128)}, f32[2,8,1920]{2,1,0:T(8,128)}) custom-call(s32[20]{0:T(128)} %stack.110.table, f32[104,1920]{1,0:T(8,128)} %copy-done.2, f32[104,1920]{1,0:T(8,128)} %collective-permute-done.54.theirs), custom_call_target="tpu_custom_call" | custom-call | tf_op jit(solution)/shard_map/final_wide/pallas_call | solution.py:39
  (218 shorter events, 65.8 us)
Async XLA Ops:
  7.3 6.7 %collective-permute-start.3 = (bf16[112,1024]{1,0:T(8,128)(2,1)}, bf16[112,1024]{1,0:T(8,128)(2,1)S(1)}, u32[]{:S(2)}, u32[]{:S(2)}) collective-permute-start(bf16[112,1024]{1,0:T(8,128)(2,1)} %projection.1.refs_0_), channel_id=1, source_target_pairs={{0,2},{1,3},{2,4},{3,5},{4,6},{5,7},{6,0},{7,1},{8,10},{9,11},{10,... | collective-permute-start | bytes 688136 | tf_op jit(solution)/shard_map/ppermute | solution.py:411
  9.2 23.3 %collective-permute-start.1 = (bf16[256,896]{1,0:T(8,128)(2,1)S(1)}, bf16[256,896]{1,0:T(8,128)(2,1)S(1)}, u32[]{:S(2)}, u32[]{:S(2)}) collective-permute-start(bf16[256,896]{1,0:T(8,128)(2,1)S(1)} %pad_maximum_fusion.1.t0), channel_id=1, source_target_pairs={{0,16},{16,0},{8,24},{24,8},{1,17},{17,1},{9,25},{25,9},{2,18},{18... | collective-permute-start | bytes 1376264 | tf_op jit(solution)/shard_map/ppermute | solution.py:411
  10.5 9.1 %collective-permute-start.6 = (bf16[112,1024]{1,0:T(8,128)(2,1)}, bf16[112,1024]{1,0:T(8,128)(2,1)S(1)}, u32[]{:S(2)}, u32[]{:S(2)}) collective-permute-start(bf16[112,1024]{1,0:T(8,128)(2,1)} %projection.1.refs_0_), channel_id=1, source_target_pairs={{0,1},{1,0},{2,3},{3,2},{4,5},{5,4},{6,7},{7,6},{8,9},{9,8},{10,11... | collective-permute-start | bytes 688136 | tf_op jit(solution)/shard_map/ppermute | solution.py:411
  12.2 8.4 %collective-permute-start.4 = (bf16[112,1024]{1,0:T(8,128)(2,1)}, bf16[112,1024]{1,0:T(8,128)(2,1)S(1)}, u32[]{:S(2)}, u32[]{:S(2)}) collective-permute-start(bf16[112,1024]{1,0:T(8,128)(2,1)} %projection.1.refs_0_), channel_id=1, source_target_pairs={{0,6},{1,7},{2,0},{3,1},{4,2},{5,3},{6,4},{7,5},{8,14},{9,15},{10,... | collective-permute-start | bytes 688136 | tf_op jit(solution)/shard_map/ppermute | solution.py:411
  14.0 8.0 %collective-permute-start.7 = (bf16[112,1024]{1,0:T(8,128)(2,1)S(1)}, bf16[112,1024]{1,0:T(8,128)(2,1)S(1)}, u32[]{:S(2)}, u32[]{:S(2)}) collective-permute-start(bf16[112,1024]{1,0:T(8,128)(2,1)S(1)} %collective-permute-done.3.refs_1_), channel_id=1, source_target_pairs={{0,1},{1,0},{2,3},{3,2},{4,5},{5,4},{6,7},{7,6},{8,9},{9,8},{10,11... | collective-permute-start | bytes 688136 | tf_op jit(solution)/shard_map/ppermute | solution.py:411
  15.4 9.4 %collective-permute-start.5 = (bf16[112,1024]{1,0:T(8,128)(2,1)}, bf16[112,1024]{1,0:T(8,128)(2,1)}, u32[]{:S(2)}, u32[]{:S(2)}) collective-permute-start(bf16[112,1024]{1,0:T(8,128)(2,1)} %projection.1.refs_0_), channel_id=1, source_target_pairs={{0,4},{1,5},{2,6},{3,7},{4,0},{5,1},{6,2},{7,3},{8,12},{9,13},{10,... | collective-permute-start | bytes 688136 | tf_op jit(solution)/shard_map/ppermute | solution.py:411
  19.6 12.9 %collective-permute-start.9 = (bf16[96,1536]{1,0:T(8,128)(2,1)}, bf16[96,1536]{1,0:T(8,128)(2,1)S(1)}, u32[]{:S(2)}, u32[]{:S(2)}) collective-permute-start(bf16[96,1536]{1,0:T(8,128)(2,1)} %wide.1.refs_0_), channel_id=1, source_target_pairs={{0,1},{1,0},{2,3},{3,2},{4,5},{5,4},{6,7},{7,6},{8,9},{9,8},{10,11... | collective-permute-start | bytes 884744 | tf_op jit(solution)/shard_map/ppermute | solution.py:411
  20.5 13.0 %collective-permute-start.11 = (bf16[96,1536]{1,0:T(8,128)(2,1)}, bf16[96,1536]{1,0:T(8,128)(2,1)}, u32[]{:S(2)}, u32[]{:S(2)}) collective-permute-start(bf16[96,1536]{1,0:T(8,128)(2,1)} %wide.1.refs_0_), channel_id=1, source_target_pairs={{0,2},{1,3},{2,4},{3,5},{4,6},{5,7},{6,0},{7,1},{8,10},{9,11},{10,... | collective-permute-start | bytes 884744 | tf_op jit(solution)/shard_map/ppermute | solution.py:411
  22.0 18.2 %collective-permute-start.8 = (bf16[112,1024]{1,0:T(8,128)(2,1)S(1)}, bf16[112,1024]{1,0:T(8,128)(2,1)S(1)}, u32[]{:S(2)}, u32[]{:S(2)}) collective-permute-start(bf16[112,1024]{1,0:T(8,128)(2,1)S(1)} %collective-permute-done.4.refs_2_), channel_id=1, source_target_pairs={{0,1},{1,0},{2,3},{3,2},{4,5},{5,4},{6,7},{7,6},{8,9},{9,8},{10,11... | collective-permute-start | bytes 688136 | tf_op jit(solution)/shard_map/ppermute | solution.py:411
  24.8 18.6 %collective-permute-start = (bf16[256,896]{1,0:T(8,128)(2,1)S(1)}, bf16[256,896]{1,0:T(8,128)(2,1)S(1)}, u32[]{:S(2)}, u32[]{:S(2)}) collective-permute-start(bf16[256,896]{1,0:T(8,128)(2,1)S(1)} %pad_maximum_fusion.1.t0), channel_id=1, source_target_pairs={{0,8},{8,0},{16,24},{24,16},{1,9},{9,1},{17,25},{25,17},{2,10},{10... | collective-permute-start | bytes 1376264 | tf_op jit(solution)/shard_map/ppermute | solution.py:420
  32.5 11.9 %collective-permute-start.2 = (bf16[256,896]{1,0:T(8,128)(2,1)S(1)}, bf16[256,896]{1,0:T(8,128)(2,1)S(1)}, u32[]{:S(2)}, u32[]{:S(2)}) collective-permute-start(bf16[256,896]{1,0:T(8,128)(2,1)S(1)} %collective-permute-done.1.t2), channel_id=1, source_target_pairs={{0,8},{8,0},{16,24},{24,16},{1,9},{9,1},{17,25},{25,17},{2,10},{10... | collective-permute-start | bytes 1376264 | tf_op jit(solution)/shard_map/ppermute | solution.py:420
  32.5 7.8 %collective-permute-start.10 = (bf16[112,1024]{1,0:T(8,128)(2,1)}, bf16[112,1024]{1,0:T(8,128)(2,1)S(1)}, u32[]{:S(2)}, u32[]{:S(2)}) collective-permute-start(bf16[112,1024]{1,0:T(8,128)(2,1)} %collective-permute-done.5.refs_3_), channel_id=1, source_target_pairs={{0,1},{1,0},{2,3},{3,2},{4,5},{5,4},{6,7},{7,6},{8,9},{9,8},{10,11... | collective-permute-start | bytes 688136 | tf_op jit(solution)/shard_map/ppermute | solution.py:411
  33.6 26.3 %collective-permute-start.16 = (bf16[96,1536]{1,0:T(8,128)(2,1)}, bf16[96,1536]{1,0:T(8,128)(2,1)}, u32[]{:S(2)}, u32[]{:S(2)}) collective-permute-start(bf16[96,1536]{1,0:T(8,128)(2,1)} %wide.1.refs_0_), channel_id=1, source_target_pairs={{0,6},{1,7},{2,0},{3,1},{4,2},{5,3},{6,4},{7,5},{8,14},{9,15},{10,... | collective-permute-start | bytes 884744 | tf_op jit(solution)/shard_map/ppermute | solution.py:411
  40.2 24.7 %collective-permute-start.18 = (bf16[96,1536]{1,0:T(8,128)(2,1)}, bf16[96,1536]{1,0:T(8,128)(2,1)}, u32[]{:S(2)}, u32[]{:S(2)}) collective-permute-start(bf16[96,1536]{1,0:T(8,128)(2,1)} %collective-permute-done.11.refs_1_), channel_id=1, source_target_pairs={{0,1},{1,0},{2,3},{3,2},{4,5},{5,4},{6,7},{7,6},{8,9},{9,8},{10,11... | collective-permute-start | bytes 884744 | tf_op jit(solution)/shard_map/ppermute | solution.py:411
  41.6 24.0 %collective-permute-start.17 = (bf16[96,1536]{1,0:T(8,128)(2,1)}, bf16[96,1536]{1,0:T(8,128)(2,1)}, u32[]{:S(2)}, u32[]{:S(2)}) collective-permute-start(bf16[96,1536]{1,0:T(8,128)(2,1)} %wide.1.refs_0_), channel_id=1, source_target_pairs={{0,4},{1,5},{2,6},{3,7},{4,0},{5,1},{6,2},{7,3},{8,12},{9,13},{10,... | collective-permute-start | bytes 884744 | tf_op jit(solution)/shard_map/ppermute | solution.py:411
  43.4 25.1 %collective-permute-start.20 = (bf16[192,768]{1,0:T(8,128)(2,1)S(1)}, bf16[192,768]{1,0:T(8,128)(2,1)S(1)}, u32[]{:S(2)}, u32[]{:S(2)}) collective-permute-start(bf16[192,768]{1,0:T(8,128)(2,1)S(1)} %constant_dynamic-slice_fusion.5.refs_0_), channel_id=1, source_target_pairs={{0,1},{1,0},{2,3},{3,2},{4,5},{5,4},{6,7},{7,6},{8,9},{9,8},{10,11... | collective-permute-start | bytes 884744 | tf_op jit(solution)/shard_map/ppermute | solution.py:411
  59.9 9.6 %collective-permute-start.22 = (bf16[192,768]{1,0:T(8,128)(2,1)S(1)}, bf16[192,768]{1,0:T(8,128)(2,1)S(1)}, u32[]{:S(2)}, u32[]{:S(2)}) collective-permute-start(bf16[192,768]{1,0:T(8,128)(2,1)S(1)} %constant_dynamic-slice_fusion.5.refs_0_), channel_id=1, source_target_pairs={{0,2},{1,3},{2,4},{3,5},{4,6},{5,7},{6,0},{7,1},{8,10},{9,11},{10,... | collective-permute-start | bytes 884744 | tf_op jit(solution)/shard_map/ppermute | solution.py:411
  65.6 15.8 %collective-permute-start.23 = (bf16[192,768]{1,0:T(8,128)(2,1)S(1)}, bf16[192,768]{1,0:T(8,128)(2,1)S(1)}, u32[]{:S(2)}, u32[]{:S(2)}) collective-permute-start(bf16[192,768]{1,0:T(8,128)(2,1)S(1)} %constant_dynamic-slice_fusion.5.refs_0_), channel_id=1, source_target_pairs={{0,6},{1,7},{2,0},{3,1},{4,2},{5,3},{6,4},{7,5},{8,14},{9,15},{10,... | collective-permute-start | bytes 884744 | tf_op jit(solution)/shard_map/ppermute | solution.py:411
  65.6 30.4 %collective-permute-start.15 = (bf16[768,384]{1,0:T(8,128)(2,1)}, bf16[768,384]{1,0:T(8,128)(2,1)S(1)}, u32[]{:S(2)}, u32[]{:S(2)}) collective-permute-start(bf16[768,384]{1,0:T(8,128)(2,1)} %get-tuple-element.148.mine.wm), channel_id=1, source_target_pairs={{0,8},{8,0},{16,24},{24,16},{1,9},{9,1},{17,25},{25,17},{2,10},{10... | collective-permute-start | bytes 1769480 | tf_op jit(solution)/shard_map/ppermute | solution.py:420
  68.5 14.1 %collective-permute-start.21 = (bf16[96,1536]{1,0:T(8,128)(2,1)}, bf16[96,1536]{1,0:T(8,128)(2,1)}, u32[]{:S(2)}, u32[]{:S(2)}) collective-permute-start(bf16[96,1536]{1,0:T(8,128)(2,1)} %collective-permute-done.17.refs_3_), channel_id=1, source_target_pairs={{0,1},{1,0},{2,3},{3,2},{4,5},{5,4},{6,7},{7,6},{8,9},{9,8},{10,11... | collective-permute-start | bytes 884744 | tf_op jit(solution)/shard_map/ppermute | solution.py:411
  69.6 14.8 %collective-permute-start.24 = (bf16[192,768]{1,0:T(8,128)(2,1)S(1)}, bf16[192,768]{1,0:T(8,128)(2,1)S(1)}, u32[]{:S(2)}, u32[]{:S(2)}) collective-permute-start(bf16[192,768]{1,0:T(8,128)(2,1)S(1)} %constant_dynamic-slice_fusion.5.refs_0_), channel_id=1, source_target_pairs={{0,4},{1,5},{2,6},{3,7},{4,0},{5,1},{6,2},{7,3},{8,12},{9,13},{10,... | collective-permute-start | bytes 884744 | tf_op jit(solution)/shard_map/ppermute | solution.py:411
  71.0 13.4 %collective-permute-start.25 = (bf16[192,768]{1,0:T(8,128)(2,1)S(1)}, bf16[192,768]{1,0:T(8,128)(2,1)S(1)}, u32[]{:S(2)}, u32[]{:S(2)}) collective-permute-start(bf16[192,768]{1,0:T(8,128)(2,1)S(1)} %collective-permute-done.22.refs_1_), channel_id=1, source_target_pairs={{0,1},{1,0},{2,3},{3,2},{4,5},{5,4},{6,7},{7,6},{8,9},{9,8},{10,11... | collective-permute-start | bytes 884744 | tf_op jit(solution)/shard_map/ppermute | solution.py:411
  81.4 13.0 %collective-permute-start.13 = (bf16[192,512]{1,0:T(8,128)(2,1)}, bf16[192,512]{1,0:T(8,128)(2,1)S(1)}, u32[]{:S(2)}, u32[]{:S(2)}) collective-permute-start(bf16[192,512]{1,0:T(8,128)(2,1)} %get-tuple-element.145), channel_id=1, source_target_pairs={{0,16},{16,0},{8,24},{24,8},{1,17},{17,1},{9,25},{25,9},{2,18},{18... | collective-permute-start | bytes 589832 | tf_op jit(solution)/shard_map/ppermute | solution.py:411
  82.6 27.4 %collective-permute-start.26 = (bf16[192,768]{1,0:T(8,128)(2,1)S(1)}, bf16[192,768]{1,0:T(8,128)(2,1)S(1)}, u32[]{:S(2)}, u32[]{:S(2)}) collective-permute-start(bf16[192,768]{1,0:T(8,128)(2,1)S(1)} %collective-permute-done.23.refs_2_), channel_id=1, source_target_pairs={{0,1},{1,0},{2,3},{3,2},{4,5},{5,4},{6,7},{7,6},{8,9},{9,8},{10,11... | collective-permute-start | bytes 884744 | tf_op jit(solution)/shard_map/ppermute | solution.py:411
  84.4 25.6 %collective-permute-start.27 = (bf16[192,768]{1,0:T(8,128)(2,1)S(1)}, bf16[192,768]{1,0:T(8,128)(2,1)S(1)}, u32[]{:S(2)}, u32[]{:S(2)}) collective-permute-start(bf16[192,768]{1,0:T(8,128)(2,1)S(1)} %collective-permute-done.24.refs_3_), channel_id=1, source_target_pairs={{0,1},{1,0},{2,3},{3,2},{4,5},{5,4},{6,7},{7,6},{8,9},{9,8},{10,11... | collective-permute-start | bytes 884744 | tf_op jit(solution)/shard_map/ppermute | solution.py:411
  85.1 10.6 %collective-permute-start.12 = (bf16[192,512]{1,0:T(8,128)(2,1)}, bf16[192,512]{1,0:T(8,128)(2,1)S(1)}, u32[]{:S(2)}, u32[]{:S(2)}) collective-permute-start(bf16[192,512]{1,0:T(8,128)(2,1)} %get-tuple-element.144.a0), channel_id=1, source_target_pairs={{0,8},{8,0},{16,24},{24,16},{1,9},{9,1},{17,25},{25,17},{2,10},{10... | collective-permute-start | bytes 589832 | tf_op jit(solution)/shard_map/ppermute | solution.py:420
  137.7 14.7 %collective-permute-start.32 = (bf16[2,192,768]{2,1,0:T(8,128)(2,1)S(1)}, bf16[2,192,768]{2,1,0:T(8,128)(2,1)S(1)}, u32[]{:S(2)}, u32[]{:S(2)}) collective-permute-start(bf16[2,192,768]{2,1,0:T(8,128)(2,1)S(1)} %copy-done.46), channel_id=1, source_target_pairs={{0,1},{1,0},{2,3},{3,2},{4,5},{5,4},{6,7},{7,6},{8,9},{9,8},{10,11... | collective-permute-start | bytes 1769480 | tf_op jit(solution)/shard_map/ppermute | solution.py:411
  138.7 26.5 %collective-permute-start.33 = (bf16[2,192,768]{2,1,0:T(8,128)(2,1)}, bf16[2,192,768]{2,1,0:T(8,128)(2,1)S(1)}, u32[]{:S(2)}, u32[]{:S(2)}) collective-permute-start(bf16[2,192,768]{2,1,0:T(8,128)(2,1)} %get-tuple-element.205), channel_id=1, source_target_pairs={{0,1},{1,0},{2,3},{3,2},{4,5},{5,4},{6,7},{7,6},{8,9},{9,8},{10,11... | collective-permute-start | bytes 1769480 | tf_op jit(solution)/shard_map/ppermute | solution.py:411
  152.5 41.6 %collective-permute-start.36 = (bf16[2,104,1920]{2,1,0:T(8,128)(2,1)}, bf16[2,104,1920]{2,1,0:T(8,128)(2,1)S(1)}, u32[]{:S(2)}, u32[]{:S(2)}) collective-permute-start(bf16[2,104,1920]{2,1,0:T(8,128)(2,1)} %get-tuple-element.215), channel_id=1, source_target_pairs={{0,1},{1,0},{2,3},{3,2},{4,5},{5,4},{6,7},{7,6},{8,9},{9,8},{10,11... | collective-permute-start | bytes 2396168 | tf_op jit(solution)/shard_map/ppermute | solution.py:411
  153.4 12.7 %collective-permute-start.31 = (bf16[192,512]{1,0:T(8,128)(2,1)S(1)}, bf16[192,512]{1,0:T(8,128)(2,1)S(1)}, u32[]{:S(2)}, u32[]{:S(2)}) collective-permute-start(bf16[192,512]{1,0:T(8,128)(2,1)S(1)} %copy-done.48), channel_id=1, source_target_pairs={{0,16},{16,0},{8,24},{24,8},{1,17},{17,1},{9,25},{25,9},{2,18},{18... | collective-permute-start | bytes 589832 | tf_op jit(solution)/shard_map/ppermute | solution.py:411
  156.8 35.5 %collective-permute-start.39 = (bf16[192,768]{1,0:T(8,128)(2,1)}, bf16[192,768]{1,0:T(8,128)(2,1)}, u32[]{:S(2)}, u32[]{:S(2)}) collective-permute-start(bf16[192,768]{1,0:T(8,128)(2,1)} %get-tuple-element.229), channel_id=1, source_target_pairs={{0,4},{1,5},{2,6},{3,7},{4,0},{5,1},{6,2},{7,3},{8,12},{9,13},{10,... | collective-permute-start | bytes 884744 | tf_op jit(solution)/shard_map/ppermute | solution.py:411
  165.2 45.4 %collective-permute-start.38 = (bf16[2,104,1920]{2,1,0:T(8,128)(2,1)}, bf16[2,104,1920]{2,1,0:T(8,128)(2,1)S(1)}, u32[]{:S(2)}, u32[]{:S(2)}) collective-permute-start(bf16[2,104,1920]{2,1,0:T(8,128)(2,1)} %get-tuple-element.219), channel_id=1, source_target_pairs={{0,1},{1,0},{2,3},{3,2},{4,5},{5,4},{6,7},{7,6},{8,9},{9,8},{10,11... | collective-permute-start | bytes 2396168 | tf_op jit(solution)/shard_map/ppermute | solution.py:411
  189.5 44.2 %collective-permute-start.34 = (bf16[2,256,768]{2,1,0:T(8,128)(2,1)}, bf16[2,256,768]{2,1,0:T(8,128)(2,1)}, u32[]{:S(2)}, u32[]{:S(2)}) collective-permute-start(bf16[2,256,768]{2,1,0:T(8,128)(2,1)} %get-tuple-element.211), channel_id=1, source_target_pairs={{0,8},{8,0},{16,24},{24,16},{1,9},{9,1},{17,25},{25,17},{2,10},{10... | collective-permute-start | bytes 2359304 | tf_op jit(solution)/shard_map/ppermute | solution.py:420
  191.2 10.2 %collective-permute-start.43 = (bf16[192,768]{1,0:T(8,128)(2,1)S(1)}, bf16[192,768]{1,0:T(8,128)(2,1)}, u32[]{:S(2)}, u32[]{:S(2)}) collective-permute-start(bf16[192,768]{1,0:T(8,128)(2,1)S(1)} %copy-done.47), channel_id=1, source_target_pairs={{0,2},{1,3},{2,4},{3,5},{4,6},{5,7},{6,0},{7,1},{8,10},{9,11},{10,... | collective-permute-start | bytes 884744 | tf_op jit(solution)/shard_map/ppermute | solution.py:411
  192.3 15.0 %collective-permute-start.40 = (bf16[192,768]{1,0:T(8,128)(2,1)}, bf16[192,768]{1,0:T(8,128)(2,1)}, u32[]{:S(2)}, u32[]{:S(2)}) collective-permute-start(bf16[192,768]{1,0:T(8,128)(2,1)} %get-tuple-element.230), channel_id=1, source_target_pairs={{0,6},{1,7},{2,0},{3,1},{4,2},{5,3},{6,4},{7,5},{8,14},{9,15},{10,... | collective-permute-start | bytes 884744 | tf_op jit(solution)/shard_map/ppermute | solution.py:411
  201.4 22.6 %collective-permute-start.44 = (bf16[104,1920]{1,0:T(8,128)(2,1)}, bf16[104,1920]{1,0:T(8,128)(2,1)S(1)}, u32[]{:S(2)}, u32[]{:S(2)}) collective-permute-start(bf16[104,1920]{1,0:T(8,128)(2,1)} %get-tuple-element.237), channel_id=1, source_target_pairs={{0,4},{1,5},{2,6},{3,7},{4,0},{5,1},{6,2},{7,3},{8,12},{9,13},{10,... | collective-permute-start | bytes 1198088 | tf_op jit(solution)/shard_map/ppermute | solution.py:411
  208.6 40.2 %collective-permute-start.50 = (bf16[192,768]{1,0:T(8,128)(2,1)S(1)}, bf16[192,768]{1,0:T(8,128)(2,1)S(1)}, u32[]{:S(2)}, u32[]{:S(2)}) collective-permute-start(bf16[192,768]{1,0:T(8,128)(2,1)S(1)} %add_convert_fusion.1), channel_id=1, source_target_pairs={{0,16},{16,0},{8,24},{24,8},{1,17},{17,1},{9,25},{25,9},{2,18},{18... | collective-permute-start | bytes 884744 | tf_op jit(solution)/shard_map/ppermute | solution.py:411
  209.9 35.9 %collective-permute-start.37 = (bf16[2,104,640]{2,1,0:T(8,128)(2,1)}, bf16[2,104,640]{2,1,0:T(8,128)(2,1)}, u32[]{:S(2)}, u32[]{:S(2)}) collective-permute-start(bf16[2,104,640]{2,1,0:T(8,128)(2,1)} %get-tuple-element.216), channel_id=1, source_target_pairs={{0,1},{1,0},{2,3},{3,2},{4,5},{5,4},{6,7},{7,6},{8,9},{9,8},{10,11... | collective-permute-start | bytes 798728 | tf_op jit(solution)/shard_map/ppermute | solution.py:411
  210.6 25.7 %collective-permute-start.41 = (bf16[104,1920]{1,0:T(8,128)(2,1)}, bf16[104,1920]{1,0:T(8,128)(2,1)}, u32[]{:S(2)}, u32[]{:S(2)}) collective-permute-start(bf16[104,1920]{1,0:T(8,128)(2,1)} %get-tuple-element.231), channel_id=1, source_target_pairs={{0,2},{1,3},{2,4},{3,5},{4,6},{5,7},{6,0},{7,1},{8,10},{9,11},{10,... | collective-permute-start | bytes 1198088 | tf_op jit(solution)/shard_map/ppermute | solution.py:411
  224.0 16.8 %collective-permute-start.45 = (bf16[104,1920]{1,0:T(8,128)(2,1)}, bf16[104,1920]{1,0:T(8,128)(2,1)S(1)}, u32[]{:S(2)}, u32[]{:S(2)}) collective-permute-start(bf16[104,1920]{1,0:T(8,128)(2,1)} %get-tuple-element.238), channel_id=1, source_target_pairs={{0,6},{1,7},{2,0},{3,1},{4,2},{5,3},{6,4},{7,5},{8,14},{9,15},{10,... | collective-permute-start | bytes 1198088 | tf_op jit(solution)/shard_map/ppermute | solution.py:411
  235.0 8.8 %collective-permute-start.35 = (bf16[256,768]{1,0:T(8,128)(2,1)S(1)}, bf16[256,768]{1,0:T(8,128)(2,1)}, u32[]{:S(2)}, u32[]{:S(2)}) collective-permute-start(bf16[256,768]{1,0:T(8,128)(2,1)S(1)} %fusion.4), channel_id=1, source_target_pairs={{0,16},{16,0},{8,24},{24,8},{1,17},{17,1},{9,25},{25,9},{2,18},{18... | collective-permute-start | bytes 1179656 | tf_op jit(solution)/shard_map/ppermute | solution.py:411
  243.8 12.9 %collective-permute-start.53 = (bf16[104,1920]{1,0:T(8,128)(2,1)S(1)}, bf16[104,1920]{1,0:T(8,128)(2,1)}, u32[]{:S(2)}, u32[]{:S(2)}) collective-permute-start(bf16[104,1920]{1,0:T(8,128)(2,1)S(1)} %add_convert_fusion), channel_id=1, source_target_pairs={{0,16},{16,0},{8,24},{24,8},{1,17},{17,1},{9,25},{25,9},{2,18},{18... | collective-permute-start | bytes 1198088 | tf_op jit(solution)/shard_map/ppermute | solution.py:411
  245.0 7.8 %collective-permute-start.47 = (bf16[2,104,640]{2,1,0:T(8,128)(2,1)}, bf16[2,104,640]{2,1,0:T(8,128)(2,1)S(1)}, u32[]{:S(2)}, u32[]{:S(2)}) collective-permute-start(bf16[2,104,640]{2,1,0:T(8,128)(2,1)} %get-tuple-element.242), channel_id=1, source_target_pairs={{0,1},{1,0},{2,3},{3,2},{4,5},{5,4},{6,7},{7,6},{8,9},{9,8},{10,11... | collective-permute-start | bytes 798728 | tf_op jit(solution)/shard_map/ppermute | solution.py:411
  247.5 7.8 %collective-permute-start.42 = (bf16[104,640]{1,0:T(8,128)(2,1)}, bf16[104,640]{1,0:T(8,128)(2,1)S(1)}, u32[]{:S(2)}, u32[]{:S(2)}) collective-permute-start(bf16[104,640]{1,0:T(8,128)(2,1)} %get-tuple-element.232), channel_id=1, source_target_pairs={{0,4},{1,5},{2,6},{3,7},{4,0},{5,1},{6,2},{7,3},{8,12},{9,13},{10,... | collective-permute-start | bytes 399368 | tf_op jit(solution)/shard_map/ppermute | solution.py:411
  249.6 14.7 %collective-permute-start.55 = (f32[192,768]{1,0:T(8,128)}, f32[192,768]{1,0:T(8,128)}, u32[]{:S(2)}, u32[]{:S(2)}) collective-permute-start(f32[192,768]{1,0:T(8,128)} %convert_add_fusion.2), channel_id=1, source_target_pairs={{0,8},{8,0},{16,24},{24,16},{1,9},{9,1},{17,25},{25,17},{2,10},{10... | collective-permute-start | bytes 1769480 | tf_op jit(solution)/shard_map/ppermute | solution.py:420
  255.3 7.4 %collective-permute-start.48 = (bf16[104,640]{1,0:T(8,128)(2,1)}, bf16[104,640]{1,0:T(8,128)(2,1)S(1)}, u32[]{:S(2)}, u32[]{:S(2)}) collective-permute-start(bf16[104,640]{1,0:T(8,128)(2,1)} %get-tuple-element.245), channel_id=1, source_target_pairs={{0,6},{1,7},{2,0},{3,1},{4,2},{5,3},{6,4},{7,5},{8,14},{9,15},{10,... | collective-permute-start | bytes 399368 | tf_op jit(solution)/shard_map/ppermute | solution.py:411
  255.3 8.6 %collective-permute-start.46 = (bf16[104,640]{1,0:T(8,128)(2,1)}, bf16[104,640]{1,0:T(8,128)(2,1)S(1)}, u32[]{:S(2)}, u32[]{:S(2)}) collective-permute-start(bf16[104,640]{1,0:T(8,128)(2,1)} %get-tuple-element.239), channel_id=1, source_target_pairs={{0,2},{1,3},{2,4},{3,5},{4,6},{5,7},{6,0},{7,1},{8,10},{9,11},{10,... | collective-permute-start | bytes 399368 | tf_op jit(solution)/shard_map/ppermute | solution.py:411
  257.9 19.0 %collective-permute-start.54 = (f32[104,1920]{1,0:T(8,128)S(1)}, f32[104,1920]{1,0:T(8,128)}, u32[]{:S(2)}, u32[]{:S(2)}) collective-permute-start(f32[104,1920]{1,0:T(8,128)S(1)} %convert_add_fusion.1.mine), channel_id=1, source_target_pairs={{0,8},{8,0},{16,24},{24,16},{1,9},{9,1},{17,25},{25,17},{2,10},{10... | collective-permute-start | bytes 2396168 | tf_op jit(solution)/shard_map/ppermute | solution.py:420
  (57 other events, 632.6 us)

commit v3 on v2

--- a/solution.py
+++ b/solution.py
@@ -403,8 +403,8 @@
         self.window = window
         self.done = []
 
-    def send(self, x, axis, pairs, *others):
-        if len(self.done) >= self.window:
+    def send(self, x, axis, pairs, *others, free=False):
+        if len(self.done) >= self.window and not free:
             others = others + (self.done[-self.window],)
         if others:
             x = after(x, *others)
@@ -500,11 +500,11 @@
     table = jnp.stack([seq, y, c, z] + pieces + blocks).astype(jnp.int32)
     x_link, y_link, z_link = Link(), Link(), Link()
 
-    def near(v, *others):
-        return x_link.send(v, "fsdp", NEAR_PAIRS, *others)
-
-    def along(v, k, *others):
-        return z_link.send(v, "fsdp", SHIFTS[k], *others)
+    def near(v, *others, free=False):
+        return x_link.send(v, "fsdp", NEAR_PAIRS, *others, free=free)
+
+    def along(v, k, *others, free=False):
+        return z_link.send(v, "fsdp", SHIFTS[k], *others, free=free)
 
     def across(v, *others):
         return y_link.send(v, "seq", CHIP_PAIRS, *others)
@@ -770,13 +770,13 @@
     def finish_half(blocks, got, i):
         if i == 0:
             p2, p1 = pair_sum(blocks[2], got)
-            return along(p2, 2), along(p1, 1), p1
+            return along(p2, 2, free=True), along(p1, 1, free=True), p1
         p3, p0 = pair_sum(blocks[3], got)
-        return along(p3, 3), p0
+        return along(p3, 3, free=True), p0
 
     if ring:
-        sh_got = [near(sh_blocks[0]), near(sh_blocks[1])]
-        em_got = [near(em_blocks[0])]
+        sh_got = [near(sh_blocks[0], free=True), near(sh_blocks[1], free=True)]
+        em_got = [near(em_blocks[0], sh_got[0], free=True)]
         r2, r1, mark = finish_half(sh_blocks, after(sh_got[0], em_blocks[0]), 0)
         sh_sums = [r2, r1]
         gate = mark
@@ -812,7 +812,7 @@
         nbytes=1e7,
     )
     if ring:
-        sh_sums += list(finish_half(sh_blocks, after(sh_got[1], grads), 1))
+        sh_sums += list(finish_half(sh_blocks, after(sh_got[1], grads, r1, r2), 1))
         gate = sh_sums[-1]
     else:
         gate = w_blocks[0]
@@ -833,12 +833,14 @@
 
 
     if ring:
-        em_got.append(near(em_blocks[1]))
+        em_got.append(near(em_blocks[1], grads, free=True))
         r2, r1, mark = finish_half(em_blocks, after(em_got[0], x_send), 0)
         em_sums = [r2, r1]
-        w_got = [near(w_blocks[0])]
+        w_got = [near(w_blocks[0], em_got[1], free=True)]
         em_sums += list(finish_half(em_blocks, after(em_got[1], mark), 1))
-        w_got.append(near(w_blocks[1]))
+        mark = em_sums[-1]
+        w_got.append(near(w_blocks[1], mark, free=True))
+        sh_sums[-1] = after(sh_sums[-1], mark)
         r2, r1, mark = finish_half(w_blocks, after(w_got[0], em_sums[-1]), 0)
         w_sums = [r2, r1] + list(finish_half(w_blocks, after(w_got[1], mark), 1))
         shrink_own, em_own, w_own = [

time: 284 us -> 264 us (0.930)
  starting transfers between devices: 94.9 us -> 83.6 us
  waiting for transfers between devices: 54.2 us -> 47.4 us
  other arithmetic: 12.3 us -> 9.01 us
    ppermute x13, starting transfers between devices: 33.8 us -> 26.1 us  [swap_core(): return lax.ppermute(x, 'seq', CORE_PAIRS)]
    ppermute x43, waiting for transfers between devices: 49.4 us -> 42.7 us  [send(): self.done.append(lax.ppermute(x, axis, pairs))]
    ppermute x43, starting transfers between devices: 61.1 us -> 57.5 us  [send(): self.done.append(lax.ppermute(x, axis, pairs))]
    unnamed x98 -> x108, local copies, waits for them, and re-layouts: 9.89 us -> 11.1 us
  transfers between devices with their start and end apart: 56 -> 56, of which waited for: 21 -> 18; matrix products, arithmetic and copies ran while one was open for 4% -> 4% of each run, Pallas kernels for 27% -> 29%
where the time goes in v3:
time: 264 us; the launch traced here: 263 us
  Pallas kernels  103 us (39%)
  starting transfers between devices  83.6 us (32%)
  waiting for transfers between devices  47.4 us (18%)
  local copies, waits for them, and re-layouts  18.5 us (7%)
  other arithmetic  9.01 us (3%)
    pallas_call x15, Pallas kernels, call(): pl.pallas_call(kernel, name=name, out_shape=[jax.ShapeDtypeStruct(shape,...  90.1 us
    ppermute x43, starting transfers between devices, send(): self.done.append(lax.ppermute(x, axis, pairs))  57.5 us
    ppermute x43, waiting for transfers between devices, send(): self.done.append(lax.ppermute(x, axis, pairs))  42.7 us
    ppermute x13, starting transfers between devices, swap_core(): return lax.ppermute(x, 'seq', CORE_PAIRS)  26.1 us
    pallas_call x6, Pallas kernels, pair_sum(): pl.pallas_call(pair_kernel, name='pair', out_shape=[jax.ShapeDtypeStruct(...  12.6 us
    unnamed x108, local copies, waits for them, and re-layouts  11.1 us
  transfers between devices with their start and end apart: 56, of which 18 were waited for; matrix products, arithmetic and copies ran while one was open for 4% of the time, Pallas kernels for 29%

profile of v3, /device:TPU:9, one launch (start us, length us, event | category | flops | bytes accessed | tf_op | source)
XLA Modules:
  0.0 262.6 jit_solution(9647519143480245806)
XLA Ops:
  5.4 1.9 projection.1.refs_0_
  10.5 1.7 collective-permute-start.6
  12.3 1.7 collective-permute-done.3.refs_1_
  14.0 1.4 collective-permute-start.7
  15.4 2.3 collective-permute-start.5
  17.7 1.9 wide.1.refs_0_
  23.2 1.5 collective-permute-done.5.refs_3_
  24.8 7.7 %collective-permute-start = (bf16[256,896]{1,0:T(8,128)(2,1)S(1)}, bf16[256,896]{1,0:T(8,128)(2,1)S(1)}, u32[]{:S(2)}, u32[]{:S(2)}) collective-permute-start(bf16[256,896]{1,0:T(8,128)(2,1)S(1)} %pad_maximum_fusion.1.t0), channel_id=1, source_target_pairs={{0,8},{8,0},{16,24},{24,16},{1,9},{9,1},{17,25},{25,17},{2,10},{10... | collective-permute-start | bytes 1376264 | tf_op jit(solution)/shard_map/ppermute | solution.py:420
  33.6 6.6 %collective-permute-start.16 = (bf16[96,1536]{1,0:T(8,128)(2,1)}, bf16[96,1536]{1,0:T(8,128)(2,1)}, u32[]{:S(2)}, u32[]{:S(2)}) collective-permute-start(bf16[96,1536]{1,0:T(8,128)(2,1)} %wide.1.refs_0_), channel_id=1, source_target_pairs={{0,6},{1,7},{2,0},{3,1},{4,2},{5,3},{6,4},{7,5},{8,14},{9,15},{10,... | collective-permute-start | bytes 884744 | tf_op jit(solution)/shard_map/ppermute | solution.py:411
  41.6 1.7 collective-permute-start.17
  45.2 14.7 %attend.1 = (bf16[1024,896]{1,0:T(8,128)(2,1)}, bf16[768,640]{1,0:T(8,128)(2,1)}, bf16[768,384]{1,0:T(8,128)(2,1)}, f32[16,1024]{1,0:T(8,128)}, bf16[1024,256]{1...) custom-call(s32[20]{0:T(128)} %stack.110.table, ...), custom_call_target="tpu_custom_call" | custom-call | tf_op jit(solution)/shard_map/attend/pallas_call | solution.py:39
  59.9 5.0 %collective-permute-start.22 = (bf16[192,768]{1,0:T(8,128)(2,1)S(1)}, bf16[192,768]{1,0:T(8,128)(2,1)S(1)}, u32[]{:S(2)}, u32[]{:S(2)}) collective-permute-start(bf16[192,768]{1,0:T(8,128)(2,1)S(1)} %constant_dynamic-slice_fusion.5.refs_0_), channel_id=1, source_target_pairs={{0,2},{1,3},{2,4},{3,5},{4,6},{5,7},{6,0},{7,1},{8,10},{9,11},{10,... | collective-permute-start | bytes 884744 | tf_op jit(solution)/shard_map/ppermute | solution.py:411
  65.5 2.9 %collective-permute-start.15 = (bf16[768,384]{1,0:T(8,128)(2,1)}, bf16[768,384]{1,0:T(8,128)(2,1)S(1)}, u32[]{:S(2)}, u32[]{:S(2)}) collective-permute-start(bf16[768,384]{1,0:T(8,128)(2,1)} %get-tuple-element.138.mine.wm), channel_id=1, source_target_pairs={{0,8},{8,0},{16,24},{24,16},{1,9},{9,1},{17,25},{25,17},{2,10},{10... | collective-permute-start | bytes 1769480 | tf_op jit(solution)/shard_map/ppermute | solution.py:420
  71.8 9.5 %collective-permute-done.23.refs_2_ = bf16[192,768]{1,0:T(8,128)(2,1)S(1)} collective-permute-done((bf16[192,768]{1,0:T(8,128)(2,1)S(1)}, bf16[192,768]{1,0:T(8,128)(2,1)S(1)}, u32[]{:S(2)}, u32[]{:S(2)}) %collective-permute-start.23) | collective-permute-done | bytes 294944 | tf_op jit(solution)/shard_map/ppermute | solution.py:411
  82.9 1.4 collective-permute-done.24.refs_3_
  85.0 9.4 %collective-permute-start.12 = (bf16[192,512]{1,0:T(8,128)(2,1)}, bf16[192,512]{1,0:T(8,128)(2,1)S(1)}, u32[]{:S(2)}, u32[]{:S(2)}) collective-permute-start(bf16[192,512]{1,0:T(8,128)(2,1)} %get-tuple-element.134.a0), channel_id=1, source_target_pairs={{0,8},{8,0},{16,24},{24,16},{1,9},{9,1},{17,25},{25,17},{2,10},{10... | collective-permute-start | bytes 589832 | tf_op jit(solution)/shard_map/ppermute | solution.py:420
  97.4 5.4 %merge.3 = (bf16[768,512]{1,0:T(8,128)(2,1)}, f32[512,768]{1,0:T(8,128)}, f32[512,128]{1,0:T(8,128)}, bf16[512,768]{1,0:T(8,128)(2,1)}, f32[8,1536]{1,0:T(8,128)}) custom-call(s32[20]{0:T(128)} %stack.110.table, bf16[192,512]{1,0:T(8,128)(2,1)} %get-tuple-element.134.a0, bf16[192,512]{1,0:T(8,128)(2,1)} %copy-done.45, bf16[192,512]{1,0:T(8,128)(2,1)} %copy-done.44, ...), custom_call_target="tpu_custom_call" | custom-call | tf_op jit(solution)/shard_map/merge/pallas_call | solution.py:39
  102.9 7.1 %gelu.1 = (bf16[768,1536]{1,0:T(8,128)(2,1)}, bf16[512,1536]{1,0:T(8,128)(2,1)}, bf16[512,1536]{1,0:T(8,128)(2,1)}) custom-call(s32[20]{0:T(128)} %stack.110.table, bf16[512,768]{1,0:T(8,128)(2,1)} %get-tuple-element.140.low, f32[8,1536]{1,0:T(8,128)} %get-tuple-element.141.bias, bf16[96,1536]{1,0:T(8,128)(2,1)} %wide.1.refs_0_, ...), custom_call_target="tpu_custom_call" | custom-call | tf_op jit(solution)/shard_map/gelu/pallas_call | solution.py:39
  110.8 4.5 %shrink.1 = (bf16[1536,768]{1,0:T(8,128)(2,1)}, bf16[512,768]{1,0:T(8,128)(2,1)}) custom-call(s32[20]{0:T(128)} %stack.110.table, bf16[512,1536]{1,0:T(8,128)(2,1)} %get-tuple-element.150.act, bf16[192,768]{1,0:T(8,128)(2,1)} %copy-done.5, bf16[192,768]{1,0:T(8,128)(2,1)} %copy-done.25, bf16[192,768]{1,0:T(8,128)(2,1)} %copy-done.26, ...), custom_call_target="tpu_custom_call" | custom-call | tf_op jit(solution)/shard_map/shrink/pallas_call | solution.py:39
  115.8 2.5 collective-permute-done.29.cot_theirs
  119.4 5.4 %second.1 = (bf16[256,768]{1,0:T(8,128)(2,1)}, f32[512,768]{1,0:T(8,128)}, bf16[512,768]{1,0:T(8,128)(2,1)}, f32[8,768]{1,0:T(8,128)}) custom-call(s32[20]{0:T(128)} %stack.110.table, f32[512,768]{1,0:T(8,128)} %get-tuple-element.139.normed, f32[16,1024]{1,0:T(8,128)} %get-tuple-element.137.vec, bf16[512,768]{1,0:T(8,128)(2,1)} %get-tuple-element.157.mine, ...), custom_call_target="tpu_custom_call" | custom-call | tf_op jit(solution)/shard_map/second/pallas_call | solution.py:39
  124.8 4.5 %shrink_grad.1 = (bf16[2,192,768]{2,1,0:T(8,128)(2,1)}, bf16[2,192,768]{2,1,0:T(8,128)(2,1)}, bf16[2,192,768]{2,1,0:T(8,128)(2,1)}, bf16[2,192,768]{2,1,0:T(8,128)(2,1)}) custom-call(s32[20]{0:T(128)} %stack.110.table, bf16[512,1536]{1,0:T(8,128)(2,1)} %get-tuple-element.150.act, bf16[512,768]{1,0:T(8,128)(2,1)} %get-tuple-element.162.dz), custom_call_target="tpu_custom_call" | custom-call | tf_op jit(solution)/shard_map/shrink_grad/pallas_call | solution.py:39
  129.3 8.0 %hidden.1 = (bf16[512,1536]{1,0:T(8,128)(2,1)}, bf16[512,768]{1,0:T(8,128)(2,1)}, f32[8,1536]{1,0:T(8,128)}) custom-call(s32[20]{0:T(128)} %stack.110.table, bf16[512,768]{1,0:T(8,128)(2,1)} %get-tuple-element.162.dz, bf16[512,1536]{1,0:T(8,128)(2,1)} %get-tuple-element.163.slope, bf16[768,1536]{1,0:T(8,128)(2,1)} %get-tuple-element.164.e, ...), custom_call_target="tpu_custom_call" | custom-call | tf_op jit(solution)/shard_map/hidden/pallas_call | solution.py:39
  140.7 5.4 %first.1 = (f32[256,768]{1,0:T(8,128)}, bf16[512,768]{1,0:T(8,128)(2,1)}, bf16[192,512]{1,0:T(8,128)(2,1)}, bf16[192,512]{1,0:T(8,128)(2,1)}, f32[8,768]{1,0:T(8,128)}) custom-call(s32[20]{0:T(128)} %stack.110.table, bf16[512,768]{1,0:T(8,128)(2,1)} %get-tuple-element.166.mine, bf16[512,768]{1,0:T(8,128)(2,1)} %copy-done.8, ...), custom_call_target="tpu_custom_call" | custom-call | tf_op jit(solution)/shard_map/first/pallas_call | solution.py:39
  147.3 5.7 %expand_grad.1 = (bf16[2,104,1920]{2,1,0:T(8,128)(2,1)}, bf16[2,104,1920]{2,1,0:T(8,128)(2,1)}, bf16[2,104,1920]{2,1,0:T(8,128)(2,1)}, bf16[2,104,1920]{2,1,0:T(8,128)(2,1)}) custom-call(s32[20]{0:T(128)} %stack.110.table, bf16[512,768]{1,0:T(8,128)(2,1)} %get-tuple-element.140.low, bf16[512,1536]{1,0:T(8,128)(2,1)} %get-tuple-element.181.dpre, ...), custom_call_target="tpu_custom_call" | custom-call | tf_op jit(solution)/shard_map/expand_grad/pallas_call | solution.py:39
  153.8 2.1 pair.6
  155.9 1.4 collective-permute-start.35
  157.4 2.7 %collective-permute-start.34 = (bf16[192,768]{1,0:T(8,128)(2,1)}, bf16[192,768]{1,0:T(8,128)(2,1)S(1)}, u32[]{:S(2)}, u32[]{:S(2)}) collective-permute-start(bf16[192,768]{1,0:T(8,128)(2,1)} %get-tuple-element.189), channel_id=1, source_target_pairs={{0,2},{1,3},{2,4},{3,5},{4,6},{5,7},{6,0},{7,1},{8,10},{9,11},{10,... | collective-permute-start | bytes 884744 | tf_op jit(solution)/shard_map/ppermute | solution.py:411
  161.5 16.1 %attend_back.1 = (bf16[2,104,640]{2,1,0:T(8,128)(2,1)}, bf16[2,104,640]{2,1,0:T(8,128)(2,1)}, bf16[2,104,640]{2,1,0:T(8,128)(2,1)}, bf16[2,104,640]{2,1,0:T(8,128)(2,1)}, bf16[1024,640]{1,0:T(8,128)(2,1)}) custom-call(s32[20]{0:T(128)} %stack.110.table, bf16[1024,896]{1,0:T(8,128)(2,1)} %get-tuple-element.136.tok, bf16[1024,256]{1,0:T(8,128)(2,1)} %get-tuple-element.170.qp, ...), custom_call_target="tpu_custom_call" | custom-call | tf_op jit(solution)/shard_map/attend_back/pallas_call | solution.py:39
  179.2 2.1 pair.7
  181.3 4.3 %input_grad.1 = (bf16[2,256,768]{2,1,0:T(8,128)(2,1)}, bf16[2,256,768]{2,1,0:T(8,128)(2,1)}) custom-call(s32[20]{0:T(128)} %stack.110.table, bf16[1024,640]{1,0:T(8,128)(2,1)} %get-tuple-element.197.grads, bf16[768,640]{1,0:T(8,128)(2,1)} %get-tuple-element.198.w), custom_call_target="tpu_custom_call" | custom-call | tf_op jit(solution)/shard_map/input_grad/pallas_call | solution.py:39
  185.6 2.2 collective-permute-start.36
  188.7 2.5 pair.8
  192.1 2.1 collective-permute-start.51
  194.2 5.2 %collective-permute-done.38.got = bf16[2,104,1920]{2,1,0:T(8,128)(2,1)S(1)} collective-permute-done((bf16[2,104,1920]{2,1,0:T(8,128)(2,1)}, bf16[2,104,1920]{2,1,0:T(8,128)(2,1)S(1)}, u32[]{:S(2)}, u32[]{:S(2)}) %collective-permute-start.38) | collective-permute-done | bytes 798752 | tf_op jit(solution)/shard_map/ppermute | solution.py:411
  200.4 2.3 pair.9
  204.8 2.6 %collective-permute-start.52 = (bf16[104,1920]{1,0:T(8,128)(2,1)}, bf16[104,1920]{1,0:T(8,128)(2,1)}, u32[]{:S(2)}, u32[]{:S(2)}) collective-permute-start(bf16[104,1920]{1,0:T(8,128)(2,1)} %get-tuple-element.231), channel_id=1, source_target_pairs={{0,6},{1,7},{2,0},{3,1},{4,2},{5,3},{6,4},{7,5},{8,14},{9,15},{10,... | collective-permute-start | bytes 1198088 | tf_op jit(solution)/shard_map/ppermute | solution.py:411
  210.9 1.8 pair.10
  212.8 1.8 pair.11
  214.6 6.7 %collective-permute-start.42 = (bf16[104,640]{1,0:T(8,128)(2,1)}, bf16[104,640]{1,0:T(8,128)(2,1)S(1)}, u32[]{:S(2)}, u32[]{:S(2)}) collective-permute-start(bf16[104,640]{1,0:T(8,128)(2,1)} %get-tuple-element.216), channel_id=1, source_target_pairs={{0,2},{1,3},{2,4},{3,5},{4,6},{5,7},{6,0},{7,1},{8,10},{9,11},{10,... | collective-permute-start | bytes 399368 | tf_op jit(solution)/shard_map/ppermute | solution.py:411
  221.4 9.1 %collective-permute-done.51 = bf16[104,1920]{1,0:T(8,128)(2,1)} collective-permute-done((bf16[104,1920]{1,0:T(8,128)(2,1)}, bf16[104,1920]{1,0:T(8,128)(2,1)}, u32[]{:S(2)}, u32[]{:S(2)}) %collective-permute-start.51) | collective-permute-done | bytes 399392 | tf_op jit(solution)/shard_map/ppermute | solution.py:411
  230.4 3.1 %collective-permute-done.52 = bf16[104,1920]{1,0:T(8,128)(2,1)} collective-permute-done((bf16[104,1920]{1,0:T(8,128)(2,1)}, bf16[104,1920]{1,0:T(8,128)(2,1)}, u32[]{:S(2)}, u32[]{:S(2)}) %collective-permute-start.52) | collective-permute-done | bytes 399392 | tf_op jit(solution)/shard_map/ppermute | solution.py:411
  234.1 1.3 add_convert_fusion
  236.8 5.0 %collective-permute-done.41 = bf16[104,640]{1,0:T(8,128)(2,1)S(1)} collective-permute-done((bf16[104,640]{1,0:T(8,128)(2,1)}, bf16[104,640]{1,0:T(8,128)(2,1)S(1)}, u32[]{:S(2)}, u32[]{:S(2)}) %collective-permute-start.41) | collective-permute-done | bytes 133152 | tf_op jit(solution)/shard_map/ppermute | solution.py:411
  245.7 2.5 collective-permute-done.48.p2
  248.1 1.9 collective-permute-start.49
  252.7 2.3 final_projection.1
  257.5 2.9 %final_wide.1 = (f32[96,768]{1,0:T(8,128)}, f32[96,3072]{1,0:T(8,128)}, f32[2,8,1920]{2,1,0:T(8,128)}) custom-call(s32[20]{0:T(128)} %stack.110.table, f32[104,1920]{1,0:T(8,128)} %copy-done.2, f32[104,1920]{1,0:T(8,128)} %collective-permute-done.54.theirs), custom_call_target="tpu_custom_call" | custom-call | tf_op jit(solution)/shard_map/final_wide/pallas_call | solution.py:39
  (228 shorter events, 57.3 us)
Async XLA Ops:
  7.3 6.7 %collective-permute-start.3 = (bf16[112,1024]{1,0:T(8,128)(2,1)}, bf16[112,1024]{1,0:T(8,128)(2,1)S(1)}, u32[]{:S(2)}, u32[]{:S(2)}) collective-permute-start(bf16[112,1024]{1,0:T(8,128)(2,1)} %projection.1.refs_0_), channel_id=1, source_target_pairs={{0,2},{1,3},{2,4},{3,5},{4,6},{5,7},{6,0},{7,1},{8,10},{9,11},{10,... | collective-permute-start | bytes 688136 | tf_op jit(solution)/shard_map/ppermute | solution.py:411
  9.1 23.3 %collective-permute-start.1 = (bf16[256,896]{1,0:T(8,128)(2,1)S(1)}, bf16[256,896]{1,0:T(8,128)(2,1)S(1)}, u32[]{:S(2)}, u32[]{:S(2)}) collective-permute-start(bf16[256,896]{1,0:T(8,128)(2,1)S(1)} %pad_maximum_fusion.1.t0), channel_id=1, source_target_pairs={{0,16},{16,0},{8,24},{24,8},{1,17},{17,1},{9,25},{25,9},{2,18},{18... | collective-permute-start | bytes 1376264 | tf_op jit(solution)/shard_map/ppermute | solution.py:411
  10.5 9.1 %collective-permute-start.6 = (bf16[112,1024]{1,0:T(8,128)(2,1)}, bf16[112,1024]{1,0:T(8,128)(2,1)S(1)}, u32[]{:S(2)}, u32[]{:S(2)}) collective-permute-start(bf16[112,1024]{1,0:T(8,128)(2,1)} %projection.1.refs_0_), channel_id=1, source_target_pairs={{0,1},{1,0},{2,3},{3,2},{4,5},{5,4},{6,7},{7,6},{8,9},{9,8},{10,11... | collective-permute-start | bytes 688136 | tf_op jit(solution)/shard_map/ppermute | solution.py:411
  12.2 8.4 %collective-permute-start.4 = (bf16[112,1024]{1,0:T(8,128)(2,1)}, bf16[112,1024]{1,0:T(8,128)(2,1)S(1)}, u32[]{:S(2)}, u32[]{:S(2)}) collective-permute-start(bf16[112,1024]{1,0:T(8,128)(2,1)} %projection.1.refs_0_), channel_id=1, source_target_pairs={{0,6},{1,7},{2,0},{3,1},{4,2},{5,3},{6,4},{7,5},{8,14},{9,15},{10,... | collective-permute-start | bytes 688136 | tf_op jit(solution)/shard_map/ppermute | solution.py:411
  14.0 8.0 %collective-permute-start.7 = (bf16[112,1024]{1,0:T(8,128)(2,1)S(1)}, bf16[112,1024]{1,0:T(8,128)(2,1)S(1)}, u32[]{:S(2)}, u32[]{:S(2)}) collective-permute-start(bf16[112,1024]{1,0:T(8,128)(2,1)S(1)} %collective-permute-done.3.refs_1_), channel_id=1, source_target_pairs={{0,1},{1,0},{2,3},{3,2},{4,5},{5,4},{6,7},{7,6},{8,9},{9,8},{10,11... | collective-permute-start | bytes 688136 | tf_op jit(solution)/shard_map/ppermute | solution.py:411
  15.4 9.4 %collective-permute-start.5 = (bf16[112,1024]{1,0:T(8,128)(2,1)}, bf16[112,1024]{1,0:T(8,128)(2,1)}, u32[]{:S(2)}, u32[]{:S(2)}) collective-permute-start(bf16[112,1024]{1,0:T(8,128)(2,1)} %projection.1.refs_0_), channel_id=1, source_target_pairs={{0,4},{1,5},{2,6},{3,7},{4,0},{5,1},{6,2},{7,3},{8,12},{9,13},{10,... | collective-permute-start | bytes 688136 | tf_op jit(solution)/shard_map/ppermute | solution.py:411
  19.6 12.9 %collective-permute-start.9 = (bf16[96,1536]{1,0:T(8,128)(2,1)}, bf16[96,1536]{1,0:T(8,128)(2,1)S(1)}, u32[]{:S(2)}, u32[]{:S(2)}) collective-permute-start(bf16[96,1536]{1,0:T(8,128)(2,1)} %wide.1.refs_0_), channel_id=1, source_target_pairs={{0,1},{1,0},{2,3},{3,2},{4,5},{5,4},{6,7},{7,6},{8,9},{9,8},{10,11... | collective-permute-start | bytes 884744 | tf_op jit(solution)/shard_map/ppermute | solution.py:411
  20.5 13.0 %collective-permute-start.11 = (bf16[96,1536]{1,0:T(8,128)(2,1)}, bf16[96,1536]{1,0:T(8,128)(2,1)}, u32[]{:S(2)}, u32[]{:S(2)}) collective-permute-start(bf16[96,1536]{1,0:T(8,128)(2,1)} %wide.1.refs_0_), channel_id=1, source_target_pairs={{0,2},{1,3},{2,4},{3,5},{4,6},{5,7},{6,0},{7,1},{8,10},{9,11},{10,... | collective-permute-start | bytes 884744 | tf_op jit(solution)/shard_map/ppermute | solution.py:411
  22.0 18.2 %collective-permute-start.8 = (bf16[112,1024]{1,0:T(8,128)(2,1)S(1)}, bf16[112,1024]{1,0:T(8,128)(2,1)S(1)}, u32[]{:S(2)}, u32[]{:S(2)}) collective-permute-start(bf16[112,1024]{1,0:T(8,128)(2,1)S(1)} %collective-permute-done.4.refs_2_), channel_id=1, source_target_pairs={{0,1},{1,0},{2,3},{3,2},{4,5},{5,4},{6,7},{7,6},{8,9},{9,8},{10,11... | collective-permute-start | bytes 688136 | tf_op jit(solution)/shard_map/ppermute | solution.py:411
  24.8 18.6 %collective-permute-start = (bf16[256,896]{1,0:T(8,128)(2,1)S(1)}, bf16[256,896]{1,0:T(8,128)(2,1)S(1)}, u32[]{:S(2)}, u32[]{:S(2)}) collective-permute-start(bf16[256,896]{1,0:T(8,128)(2,1)S(1)} %pad_maximum_fusion.1.t0), channel_id=1, source_target_pairs={{0,8},{8,0},{16,24},{24,16},{1,9},{9,1},{17,25},{25,17},{2,10},{10... | collective-permute-start | bytes 1376264 | tf_op jit(solution)/shard_map/ppermute | solution.py:420
  32.5 11.9 %collective-permute-start.2 = (bf16[256,896]{1,0:T(8,128)(2,1)S(1)}, bf16[256,896]{1,0:T(8,128)(2,1)S(1)}, u32[]{:S(2)}, u32[]{:S(2)}) collective-permute-start(bf16[256,896]{1,0:T(8,128)(2,1)S(1)} %collective-permute-done.1.t2), channel_id=1, source_target_pairs={{0,8},{8,0},{16,24},{24,16},{1,9},{9,1},{17,25},{25,17},{2,10},{10... | collective-permute-start | bytes 1376264 | tf_op jit(solution)/shard_map/ppermute | solution.py:420
  32.5 7.8 %collective-permute-start.10 = (bf16[112,1024]{1,0:T(8,128)(2,1)}, bf16[112,1024]{1,0:T(8,128)(2,1)S(1)}, u32[]{:S(2)}, u32[]{:S(2)}) collective-permute-start(bf16[112,1024]{1,0:T(8,128)(2,1)} %collective-permute-done.5.refs_3_), channel_id=1, source_target_pairs={{0,1},{1,0},{2,3},{3,2},{4,5},{5,4},{6,7},{7,6},{8,9},{9,8},{10,11... | collective-permute-start | bytes 688136 | tf_op jit(solution)/shard_map/ppermute | solution.py:411
  33.6 26.3 %collective-permute-start.16 = (bf16[96,1536]{1,0:T(8,128)(2,1)}, bf16[96,1536]{1,0:T(8,128)(2,1)}, u32[]{:S(2)}, u32[]{:S(2)}) collective-permute-start(bf16[96,1536]{1,0:T(8,128)(2,1)} %wide.1.refs_0_), channel_id=1, source_target_pairs={{0,6},{1,7},{2,0},{3,1},{4,2},{5,3},{6,4},{7,5},{8,14},{9,15},{10,... | collective-permute-start | bytes 884744 | tf_op jit(solution)/shard_map/ppermute | solution.py:411
  40.2 24.6 %collective-permute-start.18 = (bf16[96,1536]{1,0:T(8,128)(2,1)}, bf16[96,1536]{1,0:T(8,128)(2,1)}, u32[]{:S(2)}, u32[]{:S(2)}) collective-permute-start(bf16[96,1536]{1,0:T(8,128)(2,1)} %collective-permute-done.11.refs_1_), channel_id=1, source_target_pairs={{0,1},{1,0},{2,3},{3,2},{4,5},{5,4},{6,7},{7,6},{8,9},{9,8},{10,11... | collective-permute-start | bytes 884744 | tf_op jit(solution)/shard_map/ppermute | solution.py:411
  41.6 23.9 %collective-permute-start.17 = (bf16[96,1536]{1,0:T(8,128)(2,1)}, bf16[96,1536]{1,0:T(8,128)(2,1)}, u32[]{:S(2)}, u32[]{:S(2)}) collective-permute-start(bf16[96,1536]{1,0:T(8,128)(2,1)} %wide.1.refs_0_), channel_id=1, source_target_pairs={{0,4},{1,5},{2,6},{3,7},{4,0},{5,1},{6,2},{7,3},{8,12},{9,13},{10,... | collective-permute-start | bytes 884744 | tf_op jit(solution)/shard_map/ppermute | solution.py:411
  43.4 25.0 %collective-permute-start.20 = (bf16[192,768]{1,0:T(8,128)(2,1)S(1)}, bf16[192,768]{1,0:T(8,128)(2,1)S(1)}, u32[]{:S(2)}, u32[]{:S(2)}) collective-permute-start(bf16[192,768]{1,0:T(8,128)(2,1)S(1)} %constant_dynamic-slice_fusion.5.refs_0_), channel_id=1, source_target_pairs={{0,1},{1,0},{2,3},{3,2},{4,5},{5,4},{6,7},{7,6},{8,9},{9,8},{10,11... | collective-permute-start | bytes 884744 | tf_op jit(solution)/shard_map/ppermute | solution.py:411
  59.9 9.6 %collective-permute-start.22 = (bf16[192,768]{1,0:T(8,128)(2,1)S(1)}, bf16[192,768]{1,0:T(8,128)(2,1)S(1)}, u32[]{:S(2)}, u32[]{:S(2)}) collective-permute-start(bf16[192,768]{1,0:T(8,128)(2,1)S(1)} %constant_dynamic-slice_fusion.5.refs_0_), channel_id=1, source_target_pairs={{0,2},{1,3},{2,4},{3,5},{4,6},{5,7},{6,0},{7,1},{8,10},{9,11},{10,... | collective-permute-start | bytes 884744 | tf_op jit(solution)/shard_map/ppermute | solution.py:411
  65.5 15.8 %collective-permute-start.23 = (bf16[192,768]{1,0:T(8,128)(2,1)S(1)}, bf16[192,768]{1,0:T(8,128)(2,1)S(1)}, u32[]{:S(2)}, u32[]{:S(2)}) collective-permute-start(bf16[192,768]{1,0:T(8,128)(2,1)S(1)} %constant_dynamic-slice_fusion.5.refs_0_), channel_id=1, source_target_pairs={{0,6},{1,7},{2,0},{3,1},{4,2},{5,3},{6,4},{7,5},{8,14},{9,15},{10,... | collective-permute-start | bytes 884744 | tf_op jit(solution)/shard_map/ppermute | solution.py:411
  65.5 30.4 %collective-permute-start.15 = (bf16[768,384]{1,0:T(8,128)(2,1)}, bf16[768,384]{1,0:T(8,128)(2,1)S(1)}, u32[]{:S(2)}, u32[]{:S(2)}) collective-permute-start(bf16[768,384]{1,0:T(8,128)(2,1)} %get-tuple-element.138.mine.wm), channel_id=1, source_target_pairs={{0,8},{8,0},{16,24},{24,16},{1,9},{9,1},{17,25},{25,17},{2,10},{10... | collective-permute-start | bytes 1769480 | tf_op jit(solution)/shard_map/ppermute | solution.py:420
  68.4 14.2 %collective-permute-start.21 = (bf16[96,1536]{1,0:T(8,128)(2,1)}, bf16[96,1536]{1,0:T(8,128)(2,1)}, u32[]{:S(2)}, u32[]{:S(2)}) collective-permute-start(bf16[96,1536]{1,0:T(8,128)(2,1)} %collective-permute-done.17.refs_3_), channel_id=1, source_target_pairs={{0,1},{1,0},{2,3},{3,2},{4,5},{5,4},{6,7},{7,6},{8,9},{9,8},{10,11... | collective-permute-start | bytes 884744 | tf_op jit(solution)/shard_map/ppermute | solution.py:411
  69.5 14.8 %collective-permute-start.24 = (bf16[192,768]{1,0:T(8,128)(2,1)S(1)}, bf16[192,768]{1,0:T(8,128)(2,1)S(1)}, u32[]{:S(2)}, u32[]{:S(2)}) collective-permute-start(bf16[192,768]{1,0:T(8,128)(2,1)S(1)} %constant_dynamic-slice_fusion.5.refs_0_), channel_id=1, source_target_pairs={{0,4},{1,5},{2,6},{3,7},{4,0},{5,1},{6,2},{7,3},{8,12},{9,13},{10,... | collective-permute-start | bytes 884744 | tf_op jit(solution)/shard_map/ppermute | solution.py:411
  70.9 13.4 %collective-permute-start.25 = (bf16[192,768]{1,0:T(8,128)(2,1)S(1)}, bf16[192,768]{1,0:T(8,128)(2,1)S(1)}, u32[]{:S(2)}, u32[]{:S(2)}) collective-permute-start(bf16[192,768]{1,0:T(8,128)(2,1)S(1)} %collective-permute-done.22.refs_1_), channel_id=1, source_target_pairs={{0,1},{1,0},{2,3},{3,2},{4,5},{5,4},{6,7},{7,6},{8,9},{9,8},{10,11... | collective-permute-start | bytes 884744 | tf_op jit(solution)/shard_map/ppermute | solution.py:411
  81.3 13.0 %collective-permute-start.13 = (bf16[192,512]{1,0:T(8,128)(2,1)}, bf16[192,512]{1,0:T(8,128)(2,1)S(1)}, u32[]{:S(2)}, u32[]{:S(2)}) collective-permute-start(bf16[192,512]{1,0:T(8,128)(2,1)} %get-tuple-element.135), channel_id=1, source_target_pairs={{0,16},{16,0},{8,24},{24,8},{1,17},{17,1},{9,25},{25,9},{2,18},{18... | collective-permute-start | bytes 589832 | tf_op jit(solution)/shard_map/ppermute | solution.py:411
  82.6 27.3 %collective-permute-start.26 = (bf16[192,768]{1,0:T(8,128)(2,1)S(1)}, bf16[192,768]{1,0:T(8,128)(2,1)S(1)}, u32[]{:S(2)}, u32[]{:S(2)}) collective-permute-start(bf16[192,768]{1,0:T(8,128)(2,1)S(1)} %collective-permute-done.23.refs_2_), channel_id=1, source_target_pairs={{0,1},{1,0},{2,3},{3,2},{4,5},{5,4},{6,7},{7,6},{8,9},{9,8},{10,11... | collective-permute-start | bytes 884744 | tf_op jit(solution)/shard_map/ppermute | solution.py:411
  84.3 25.7 %collective-permute-start.27 = (bf16[192,768]{1,0:T(8,128)(2,1)S(1)}, bf16[192,768]{1,0:T(8,128)(2,1)S(1)}, u32[]{:S(2)}, u32[]{:S(2)}) collective-permute-start(bf16[192,768]{1,0:T(8,128)(2,1)S(1)} %collective-permute-done.24.refs_3_), channel_id=1, source_target_pairs={{0,1},{1,0},{2,3},{3,2},{4,5},{5,4},{6,7},{7,6},{8,9},{9,8},{10,11... | collective-permute-start | bytes 884744 | tf_op jit(solution)/shard_map/ppermute | solution.py:411
  85.0 10.6 %collective-permute-start.12 = (bf16[192,512]{1,0:T(8,128)(2,1)}, bf16[192,512]{1,0:T(8,128)(2,1)S(1)}, u32[]{:S(2)}, u32[]{:S(2)}) collective-permute-start(bf16[192,512]{1,0:T(8,128)(2,1)} %get-tuple-element.134.a0), channel_id=1, source_target_pairs={{0,8},{8,0},{16,24},{24,16},{1,9},{9,1},{17,25},{25,17},{2,10},{10... | collective-permute-start | bytes 589832 | tf_op jit(solution)/shard_map/ppermute | solution.py:420
  137.7 15.3 %collective-permute-start.32 = (bf16[2,192,768]{2,1,0:T(8,128)(2,1)S(1)}, bf16[2,192,768]{2,1,0:T(8,128)(2,1)S(1)}, u32[]{:S(2)}, u32[]{:S(2)}) collective-permute-start(bf16[2,192,768]{2,1,0:T(8,128)(2,1)S(1)} %copy-done.52), channel_id=1, source_target_pairs={{0,1},{1,0},{2,3},{3,2},{4,5},{5,4},{6,7},{7,6},{8,9},{9,8},{10,11... | collective-permute-start | bytes 1769480 | tf_op jit(solution)/shard_map/ppermute | solution.py:411
  138.7 39.7 %collective-permute-start.33 = (bf16[2,192,768]{2,1,0:T(8,128)(2,1)S(1)}, bf16[2,192,768]{2,1,0:T(8,128)(2,1)S(1)}, u32[]{:S(2)}, u32[]{:S(2)}) collective-permute-start(bf16[2,192,768]{2,1,0:T(8,128)(2,1)S(1)} %copy-done.51), channel_id=1, source_target_pairs={{0,1},{1,0},{2,3},{3,2},{4,5},{5,4},{6,7},{7,6},{8,9},{9,8},{10,11... | collective-permute-start | bytes 1769480 | tf_op jit(solution)/shard_map/ppermute | solution.py:411
  146.1 14.8 %collective-permute-start.31 = (bf16[192,512]{1,0:T(8,128)(2,1)}, bf16[192,512]{1,0:T(8,128)(2,1)S(1)}, u32[]{:S(2)}, u32[]{:S(2)}) collective-permute-start(bf16[192,512]{1,0:T(8,128)(2,1)} %get-tuple-element.179), channel_id=1, source_target_pairs={{0,16},{16,0},{8,24},{24,8},{1,17},{17,1},{9,25},{25,9},{2,18},{18... | collective-permute-start | bytes 589832 | tf_op jit(solution)/shard_map/ppermute | solution.py:411
  155.9 22.4 %collective-permute-start.35 = (bf16[192,768]{1,0:T(8,128)(2,1)}, bf16[192,768]{1,0:T(8,128)(2,1)S(1)}, u32[]{:S(2)}, u32[]{:S(2)}) collective-permute-start(bf16[192,768]{1,0:T(8,128)(2,1)} %get-tuple-element.194), channel_id=1, source_target_pairs={{0,4},{1,5},{2,6},{3,7},{4,0},{5,1},{6,2},{7,3},{8,12},{9,13},{10,... | collective-permute-start | bytes 884744 | tf_op jit(solution)/shard_map/ppermute | solution.py:411
  157.4 21.0 %collective-permute-start.34 = (bf16[192,768]{1,0:T(8,128)(2,1)}, bf16[192,768]{1,0:T(8,128)(2,1)S(1)}, u32[]{:S(2)}, u32[]{:S(2)}) collective-permute-start(bf16[192,768]{1,0:T(8,128)(2,1)} %get-tuple-element.189), channel_id=1, source_target_pairs={{0,2},{1,3},{2,4},{3,5},{4,6},{5,7},{6,0},{7,1},{8,10},{9,11},{10,... | collective-permute-start | bytes 884744 | tf_op jit(solution)/shard_map/ppermute | solution.py:411
  160.1 27.7 %collective-permute-start.40 = (bf16[2,104,1920]{2,1,0:T(8,128)(2,1)}, bf16[2,104,1920]{2,1,0:T(8,128)(2,1)S(1)}, u32[]{:S(2)}, u32[]{:S(2)}) collective-permute-start(bf16[2,104,1920]{2,1,0:T(8,128)(2,1)} %get-tuple-element.209), channel_id=1, source_target_pairs={{0,1},{1,0},{2,3},{3,2},{4,5},{5,4},{6,7},{7,6},{8,9},{9,8},{10,11... | collective-permute-start | bytes 2396168 | tf_op jit(solution)/shard_map/ppermute | solution.py:411
  177.7 21.8 %collective-permute-start.38 = (bf16[2,104,1920]{2,1,0:T(8,128)(2,1)}, bf16[2,104,1920]{2,1,0:T(8,128)(2,1)S(1)}, u32[]{:S(2)}, u32[]{:S(2)}) collective-permute-start(bf16[2,104,1920]{2,1,0:T(8,128)(2,1)} %get-tuple-element.205), channel_id=1, source_target_pairs={{0,1},{1,0},{2,3},{3,2},{4,5},{5,4},{6,7},{7,6},{8,9},{9,8},{10,11... | collective-permute-start | bytes 2396168 | tf_op jit(solution)/shard_map/ppermute | solution.py:411
  185.6 19.3 %collective-permute-start.36 = (bf16[2,256,768]{2,1,0:T(8,128)(2,1)}, bf16[2,256,768]{2,1,0:T(8,128)(2,1)}, u32[]{:S(2)}, u32[]{:S(2)}) collective-permute-start(bf16[2,256,768]{2,1,0:T(8,128)(2,1)} %get-tuple-element.200), channel_id=1, source_target_pairs={{0,8},{8,0},{16,24},{24,16},{1,9},{9,1},{17,25},{25,17},{2,10},{10... | collective-permute-start | bytes 2359304 | tf_op jit(solution)/shard_map/ppermute | solution.py:420
  187.8 15.0 %collective-permute-start.46 = (bf16[192,768]{1,0:T(8,128)(2,1)S(1)}, bf16[192,768]{1,0:T(8,128)(2,1)}, u32[]{:S(2)}, u32[]{:S(2)}) collective-permute-start(bf16[192,768]{1,0:T(8,128)(2,1)S(1)} %copy-done.53), channel_id=1, source_target_pairs={{0,6},{1,7},{2,0},{3,1},{4,2},{5,3},{6,4},{7,5},{8,14},{9,15},{10,... | collective-permute-start | bytes 884744 | tf_op jit(solution)/shard_map/ppermute | solution.py:411
  191.2 23.4 %collective-permute-start.50 = (bf16[104,1920]{1,0:T(8,128)(2,1)}, bf16[104,1920]{1,0:T(8,128)(2,1)S(1)}, u32[]{:S(2)}, u32[]{:S(2)}) collective-permute-start(bf16[104,1920]{1,0:T(8,128)(2,1)} %get-tuple-element.230), channel_id=1, source_target_pairs={{0,4},{1,5},{2,6},{3,7},{4,0},{5,1},{6,2},{7,3},{8,12},{9,13},{10,... | collective-permute-start | bytes 1198088 | tf_op jit(solution)/shard_map/ppermute | solution.py:411
  192.1 38.3 %collective-permute-start.51 = (bf16[104,1920]{1,0:T(8,128)(2,1)}, bf16[104,1920]{1,0:T(8,128)(2,1)}, u32[]{:S(2)}, u32[]{:S(2)}) collective-permute-start(bf16[104,1920]{1,0:T(8,128)(2,1)} %get-tuple-element.211), channel_id=1, source_target_pairs={{0,2},{1,3},{2,4},{3,5},{4,6},{5,7},{6,0},{7,1},{8,10},{9,11},{10,... | collective-permute-start | bytes 1198088 | tf_op jit(solution)/shard_map/ppermute | solution.py:411
  199.4 10.2 %collective-permute-start.39 = (bf16[2,104,640]{2,1,0:T(8,128)(2,1)}, bf16[2,104,640]{2,1,0:T(8,128)(2,1)}, u32[]{:S(2)}, u32[]{:S(2)}) collective-permute-start(bf16[2,104,640]{2,1,0:T(8,128)(2,1)} %get-tuple-element.206), channel_id=1, source_target_pairs={{0,1},{1,0},{2,3},{3,2},{4,5},{5,4},{6,7},{7,6},{8,9},{9,8},{10,11... | collective-permute-start | bytes 798728 | tf_op jit(solution)/shard_map/ppermute | solution.py:411
  203.9 8.7 %collective-permute-start.43 = (bf16[2,104,640]{2,1,0:T(8,128)(2,1)}, bf16[2,104,640]{2,1,0:T(8,128)(2,1)}, u32[]{:S(2)}, u32[]{:S(2)}) collective-permute-start(bf16[2,104,640]{2,1,0:T(8,128)(2,1)} %get-tuple-element.219), channel_id=1, source_target_pairs={{0,1},{1,0},{2,3},{3,2},{4,5},{5,4},{6,7},{7,6},{8,9},{9,8},{10,11... | collective-permute-start | bytes 798728 | tf_op jit(solution)/shard_map/ppermute | solution.py:411
  204.8 28.7 %collective-permute-start.52 = (bf16[104,1920]{1,0:T(8,128)(2,1)}, bf16[104,1920]{1,0:T(8,128)(2,1)}, u32[]{:S(2)}, u32[]{:S(2)}) collective-permute-start(bf16[104,1920]{1,0:T(8,128)(2,1)} %get-tuple-element.231), channel_id=1, source_target_pairs={{0,6},{1,7},{2,0},{3,1},{4,2},{5,3},{6,4},{7,5},{8,14},{9,15},{10,... | collective-permute-start | bytes 1198088 | tf_op jit(solution)/shard_map/ppermute | solution.py:411
  209.6 32.9 %collective-permute-start.47 = (bf16[192,768]{1,0:T(8,128)(2,1)S(1)}, bf16[192,768]{1,0:T(8,128)(2,1)S(1)}, u32[]{:S(2)}, u32[]{:S(2)}) collective-permute-start(bf16[192,768]{1,0:T(8,128)(2,1)S(1)} %add_convert_fusion.1), channel_id=1, source_target_pairs={{0,16},{16,0},{8,24},{24,8},{1,17},{17,1},{9,25},{25,9},{2,18},{18... | collective-permute-start | bytes 884744 | tf_op jit(solution)/shard_map/ppermute | solution.py:411
  212.6 22.8 %collective-permute-start.37 = (bf16[256,768]{1,0:T(8,128)(2,1)}, bf16[256,768]{1,0:T(8,128)(2,1)S(1)}, u32[]{:S(2)}, u32[]{:S(2)}) collective-permute-start(bf16[256,768]{1,0:T(8,128)(2,1)} %fusion.4), channel_id=1, source_target_pairs={{0,16},{16,0},{8,24},{24,8},{1,17},{17,1},{9,25},{25,9},{2,18},{18... | collective-permute-start | bytes 1179656 | tf_op jit(solution)/shard_map/ppermute | solution.py:411
  214.6 27.2 %collective-permute-start.42 = (bf16[104,640]{1,0:T(8,128)(2,1)}, bf16[104,640]{1,0:T(8,128)(2,1)S(1)}, u32[]{:S(2)}, u32[]{:S(2)}) collective-permute-start(bf16[104,640]{1,0:T(8,128)(2,1)} %get-tuple-element.216), channel_id=1, source_target_pairs={{0,2},{1,3},{2,4},{3,5},{4,6},{5,7},{6,0},{7,1},{8,10},{9,11},{10,... | collective-permute-start | bytes 399368 | tf_op jit(solution)/shard_map/ppermute | solution.py:411
  230.4 11.4 %collective-permute-start.41 = (bf16[104,640]{1,0:T(8,128)(2,1)}, bf16[104,640]{1,0:T(8,128)(2,1)S(1)}, u32[]{:S(2)}, u32[]{:S(2)}) collective-permute-start(bf16[104,640]{1,0:T(8,128)(2,1)} %get-tuple-element.215), channel_id=1, source_target_pairs={{0,4},{1,5},{2,6},{3,7},{4,0},{5,1},{6,2},{7,3},{8,12},{9,13},{10,... | collective-permute-start | bytes 399368 | tf_op jit(solution)/shard_map/ppermute | solution.py:411
  233.5 8.9 %collective-permute-start.44 = (bf16[104,640]{1,0:T(8,128)(2,1)}, bf16[104,640]{1,0:T(8,128)(2,1)S(1)}, u32[]{:S(2)}, u32[]{:S(2)}) collective-permute-start(bf16[104,640]{1,0:T(8,128)(2,1)} %get-tuple-element.221), channel_id=1, source_target_pairs={{0,6},{1,7},{2,0},{3,1},{4,2},{5,3},{6,4},{7,5},{8,14},{9,15},{10,... | collective-permute-start | bytes 399368 | tf_op jit(solution)/shard_map/ppermute | solution.py:411
  235.5 14.6 %collective-permute-start.53 = (bf16[104,1920]{1,0:T(8,128)(2,1)S(1)}, bf16[104,1920]{1,0:T(8,128)(2,1)S(1)}, u32[]{:S(2)}, u32[]{:S(2)}) collective-permute-start(bf16[104,1920]{1,0:T(8,128)(2,1)S(1)} %add_convert_fusion), channel_id=1, source_target_pairs={{0,16},{16,0},{8,24},{24,8},{1,17},{17,1},{9,25},{25,9},{2,18},{18... | collective-permute-start | bytes 1198088 | tf_op jit(solution)/shard_map/ppermute | solution.py:411
  244.7 11.6 %collective-permute-start.55 = (f32[192,768]{1,0:T(8,128)}, f32[192,768]{1,0:T(8,128)S(1)}, u32[]{:S(2)}, u32[]{:S(2)}) collective-permute-start(f32[192,768]{1,0:T(8,128)} %convert_add_fusion.2), channel_id=1, source_target_pairs={{0,8},{8,0},{16,24},{24,16},{1,9},{9,1},{17,25},{25,17},{2,10},{10... | collective-permute-start | bytes 1769480 | tf_op jit(solution)/shard_map/ppermute | solution.py:420
  250.2 7.3 %collective-permute-start.54 = (f32[104,1920]{1,0:T(8,128)S(1)}, f32[104,1920]{1,0:T(8,128)}, u32[]{:S(2)}, u32[]{:S(2)}) collective-permute-start(f32[104,1920]{1,0:T(8,128)S(1)} %convert_add_fusion.1.mine), channel_id=1, source_target_pairs={{0,8},{8,0},{16,24},{24,16},{1,9},{9,1},{17,25},{25,17},{2,10},{10... | collective-permute-start | bytes 2396168 | tf_op jit(solution)/shard_map/ppermute | solution.py:420
  (62 other events, 681.8 us)

commit v4 on v3

--- a/solution.py
+++ b/solution.py
@@ -205,8 +205,8 @@
 
 def put_blocks(parts, table, work, block, outs, extra=None):
     for i, ref in enumerate(outs):
-        for j in range(parts // 4):
-            at = table[4 + parts + i * (parts // 4) + j]
+        for j in range(parts // len(outs)):
+            at = table[4 + parts + i * (parts // len(outs)) + j]
             ref[j, :block, :] = work[rows_at(at, block), :]
             if extra is not None:
                 ref[j, block:, :] = extra
@@ -266,7 +266,7 @@
 def attend_back_kernel(
     parts, table, tok, qp, kp, v, q_t, k_t, o_t, lse, dkeep, dother, *refs
 ):
-    outs, refs = refs[:4], refs[4:]
+    outs, refs = refs[:2], refs[2:]
     grads, probs, dscores, d_t, d_rows, q_rows, heads, v_heads, dq_t, work = refs
     y = table[1]
     length = tok.shape[0]
@@ -785,7 +785,7 @@
     *w_blocks, grads = call(
         partial(attend_back_kernel, parts),
         "attend_back",
-        [((parts // 4, width // parts + EXTRA, 640), LOW)] * 4 + [((length, 640), LOW)],
+        [((parts // 2, width // parts + EXTRA, 640), LOW)] * 2 + [((length, 640), LOW)],
         table,
         tok,
         qp,
@@ -836,13 +836,12 @@
         em_got.append(near(em_blocks[1], grads, free=True))
         r2, r1, mark = finish_half(em_blocks, after(em_got[0], x_send), 0)
         em_sums = [r2, r1]
-        w_got = [near(w_blocks[0], em_got[1], free=True)]
+        w_got = near(w_blocks[0], em_got[1], free=True)
         em_sums += list(finish_half(em_blocks, after(em_got[1], mark), 1))
         mark = em_sums[-1]
-        w_got.append(near(w_blocks[1], mark, free=True))
         sh_sums[-1] = after(sh_sums[-1], mark)
-        r2, r1, mark = finish_half(w_blocks, after(w_got[0], em_sums[-1]), 0)
-        w_sums = [r2, r1] + list(finish_half(w_blocks, after(w_got[1], mark), 1))
+        p2, p1, p3, p0 = pair_sum(w_blocks[1], after(w_got, mark))
+        w_sums = [along(p, k, free=True) for p, k in ((p2, 2), (p1, 1), (p3, 3))] + [p0]
         shrink_own, em_own, w_own = [
             g[0].astype(FULL) + g[1].astype(FULL) + g[2].astype(FULL) + g[3].astype(FULL)
             for g in (sh_sums, em_sums, w_sums)
@@ -850,7 +849,7 @@
     else:
         shrink_own, em_own, w_own = [
             scatter_whole(
-                jnp.concatenate(g[:2], axis=0), jnp.concatenate(g[2:], axis=0), count, extra
+                jnp.concatenate(g[: len(g) // 2], axis=0), jnp.concatenate(g[len(g) // 2 :], axis=0), count, extra
             )
             for g, extra in ((sh_blocks, 0), (em_blocks, EXTRA), (w_blocks, EXTRA))
         ]

time: 264 us -> 270 us (1.023)
  waiting for transfers between devices: 47.4 us -> 56.8 us
    ppermute x43 -> x42, waiting for transfers between devices: 42.7 us -> 52 us  [send(): self.done.append(lax.ppermute(x, axis, pairs))]
    ppermute x43 -> x42, starting transfers between devices: 57.5 us -> 53.3 us  [send(): self.done.append(lax.ppermute(x, axis, pairs))]
    pallas_call x6 -> x5, Pallas kernels: 12.6 us -> 11.1 us  [pair_sum(): pl.pallas_call(pair_kernel, name='pair', out_shape=[jax.ShapeDtypeStruct(...]
    unnamed x108 -> x110, local copies, waits for them, and re-layouts: 11.1 us -> 11.6 us
  transfers between devices with their start and end apart: 56 -> 55, of which waited for: 18 -> 19; matrix products, arithmetic and copies ran while one was open for 4% -> 4% of each run, Pallas kernels for 29% -> 27%
where the time goes in v4:
time: 270 us; the launch traced here: 269 us
  Pallas kernels  101 us (37%)
  starting transfers between devices  81 us (30%)
  waiting for transfers between devices  56.8 us (21%)
  local copies, waits for them, and re-layouts  18.3 us (7%)
  other arithmetic  10 us (4%)
    pallas_call x15, Pallas kernels, call(): pl.pallas_call(kernel, name=name, out_shape=[jax.ShapeDtypeStruct(shape,...  90.1 us
    ppermute x42, starting transfers between devices, send(): self.done.append(lax.ppermute(x, axis, pairs))  53.3 us
    ppermute x42, waiting for transfers between devices, send(): self.done.append(lax.ppermute(x, axis, pairs))  52 us
    ppermute x13, starting transfers between devices, swap_core(): return lax.ppermute(x, 'seq', CORE_PAIRS)  27.8 us
    unnamed x110, local copies, waits for them, and re-layouts  11.6 us
    pallas_call x5, Pallas kernels, pair_sum(): pl.pallas_call(pair_kernel, name='pair', out_shape=[jax.ShapeDtypeStruct(...  11.1 us
  transfers between devices with their start and end apart: 55, of which 19 were waited for; matrix products, arithmetic and copies ran while one was open for 4% of the time, Pallas kernels for 27%

profile of v4, /device:TPU:9, one launch (start us, length us, event | category | flops | bytes accessed | tf_op | source)
XLA Modules:
  0.0 268.8 jit_solution(18133234877980394839)
XLA Ops:
  5.4 1.9 projection.1.refs_0_
  10.5 1.7 collective-permute-start.6
  12.4 1.7 collective-permute-done.3.refs_1_
  14.1 1.4 collective-permute-start.7
  15.5 2.3 collective-permute-start.5
  17.8 1.9 wide.1.refs_0_
  23.3 1.5 collective-permute-done.5.refs_3_
  24.8 7.7 %collective-permute-start = (bf16[256,896]{1,0:T(8,128)(2,1)S(1)}, bf16[256,896]{1,0:T(8,128)(2,1)S(1)}, u32[]{:S(2)}, u32[]{:S(2)}) collective-permute-start(bf16[256,896]{1,0:T(8,128)(2,1)S(1)} %pad_maximum_fusion.1.t0), channel_id=1, source_target_pairs={{0,8},{8,0},{16,24},{24,16},{1,9},{9,1},{17,25},{25,17},{2,10},{10... | collective-permute-start | bytes 1376264 | tf_op jit(solution)/shard_map/ppermute | solution.py:420
  33.7 6.6 %collective-permute-start.16 = (bf16[96,1536]{1,0:T(8,128)(2,1)}, bf16[96,1536]{1,0:T(8,128)(2,1)}, u32[]{:S(2)}, u32[]{:S(2)}) collective-permute-start(bf16[96,1536]{1,0:T(8,128)(2,1)} %wide.1.refs_0_), channel_id=1, source_target_pairs={{0,6},{1,7},{2,0},{3,1},{4,2},{5,3},{6,4},{7,5},{8,14},{9,15},{10,... | collective-permute-start | bytes 884744 | tf_op jit(solution)/shard_map/ppermute | solution.py:411
  41.7 1.7 collective-permute-start.17
  45.2 14.7 %attend.1 = (bf16[1024,896]{1,0:T(8,128)(2,1)}, bf16[768,640]{1,0:T(8,128)(2,1)}, bf16[768,384]{1,0:T(8,128)(2,1)}, f32[16,1024]{1,0:T(8,128)}, bf16[1024,256]{1...) custom-call(s32[20]{0:T(128)} %stack.110.table, ...), custom_call_target="tpu_custom_call" | custom-call | tf_op jit(solution)/shard_map/attend/pallas_call | solution.py:39
  59.9 5.0 %collective-permute-start.22 = (bf16[192,768]{1,0:T(8,128)(2,1)S(1)}, bf16[192,768]{1,0:T(8,128)(2,1)S(1)}, u32[]{:S(2)}, u32[]{:S(2)}) collective-permute-start(bf16[192,768]{1,0:T(8,128)(2,1)S(1)} %constant_dynamic-slice_fusion.5.refs_0_), channel_id=1, source_target_pairs={{0,2},{1,3},{2,4},{3,5},{4,6},{5,7},{6,0},{7,1},{8,10},{9,11},{10,... | collective-permute-start | bytes 884744 | tf_op jit(solution)/shard_map/ppermute | solution.py:411
  65.6 2.9 %collective-permute-start.15 = (bf16[768,384]{1,0:T(8,128)(2,1)}, bf16[768,384]{1,0:T(8,128)(2,1)S(1)}, u32[]{:S(2)}, u32[]{:S(2)}) collective-permute-start(bf16[768,384]{1,0:T(8,128)(2,1)} %get-tuple-element.134.mine.wm), channel_id=1, source_target_pairs={{0,8},{8,0},{16,24},{24,16},{1,9},{9,1},{17,25},{25,17},{2,10},{10... | collective-permute-start | bytes 1769480 | tf_op jit(solution)/shard_map/ppermute | solution.py:420
  71.8 9.5 %collective-permute-done.23.refs_2_ = bf16[192,768]{1,0:T(8,128)(2,1)S(1)} collective-permute-done((bf16[192,768]{1,0:T(8,128)(2,1)S(1)}, bf16[192,768]{1,0:T(8,128)(2,1)S(1)}, u32[]{:S(2)}, u32[]{:S(2)}) %collective-permute-start.23) | collective-permute-done | bytes 294944 | tf_op jit(solution)/shard_map/ppermute | solution.py:411
  83.0 1.4 collective-permute-done.24.refs_3_
  85.0 9.3 %collective-permute-start.12 = (bf16[192,512]{1,0:T(8,128)(2,1)}, bf16[192,512]{1,0:T(8,128)(2,1)S(1)}, u32[]{:S(2)}, u32[]{:S(2)}) collective-permute-start(bf16[192,512]{1,0:T(8,128)(2,1)} %get-tuple-element.130.a0), channel_id=1, source_target_pairs={{0,8},{8,0},{16,24},{24,16},{1,9},{9,1},{17,25},{25,17},{2,10},{10... | collective-permute-start | bytes 589832 | tf_op jit(solution)/shard_map/ppermute | solution.py:420
  97.5 5.4 %merge.3 = (bf16[768,512]{1,0:T(8,128)(2,1)}, f32[512,768]{1,0:T(8,128)}, f32[512,128]{1,0:T(8,128)}, bf16[512,768]{1,0:T(8,128)(2,1)}, f32[8,1536]{1,0:T(8,128)}) custom-call(s32[20]{0:T(128)} %stack.110.table, bf16[192,512]{1,0:T(8,128)(2,1)} %get-tuple-element.130.a0, bf16[192,512]{1,0:T(8,128)(2,1)} %copy-done.46, bf16[192,512]{1,0:T(8,128)(2,1)} %copy-done.45, ...), custom_call_target="tpu_custom_call" | custom-call | tf_op jit(solution)/shard_map/merge/pallas_call | solution.py:39
  102.9 7.1 %gelu.1 = (bf16[768,1536]{1,0:T(8,128)(2,1)}, bf16[512,1536]{1,0:T(8,128)(2,1)}, bf16[512,1536]{1,0:T(8,128)(2,1)}) custom-call(s32[20]{0:T(128)} %stack.110.table, bf16[512,768]{1,0:T(8,128)(2,1)} %get-tuple-element.136.low, f32[8,1536]{1,0:T(8,128)} %get-tuple-element.137.bias, bf16[96,1536]{1,0:T(8,128)(2,1)} %wide.1.refs_0_, ...), custom_call_target="tpu_custom_call" | custom-call | tf_op jit(solution)/shard_map/gelu/pallas_call | solution.py:39
  110.8 4.5 %shrink.1 = (bf16[1536,768]{1,0:T(8,128)(2,1)}, bf16[512,768]{1,0:T(8,128)(2,1)}) custom-call(s32[20]{0:T(128)} %stack.110.table, bf16[512,1536]{1,0:T(8,128)(2,1)} %get-tuple-element.146.act, bf16[192,768]{1,0:T(8,128)(2,1)} %copy-done.5, bf16[192,768]{1,0:T(8,128)(2,1)} %copy-done.26, bf16[192,768]{1,0:T(8,128)(2,1)} %copy-done.27, ...), custom_call_target="tpu_custom_call" | custom-call | tf_op jit(solution)/shard_map/shrink/pallas_call | solution.py:39
  115.9 2.5 collective-permute-done.29.cot_theirs
  119.4 5.4 %second.1 = (bf16[256,768]{1,0:T(8,128)(2,1)}, f32[512,768]{1,0:T(8,128)}, bf16[512,768]{1,0:T(8,128)(2,1)}, f32[8,768]{1,0:T(8,128)}) custom-call(s32[20]{0:T(128)} %stack.110.table, f32[512,768]{1,0:T(8,128)} %get-tuple-element.135.normed, f32[16,1024]{1,0:T(8,128)} %get-tuple-element.133.vec, bf16[512,768]{1,0:T(8,128)(2,1)} %get-tuple-element.153.mine, ...), custom_call_target="tpu_custom_call" | custom-call | tf_op jit(solution)/shard_map/second/pallas_call | solution.py:39
  124.8 4.5 %shrink_grad.1 = (bf16[2,192,768]{2,1,0:T(8,128)(2,1)}, bf16[2,192,768]{2,1,0:T(8,128)(2,1)}, bf16[2,192,768]{2,1,0:T(8,128)(2,1)}, bf16[2,192,768]{2,1,0:T(8,128)(2,1)}) custom-call(s32[20]{0:T(128)} %stack.110.table, bf16[512,1536]{1,0:T(8,128)(2,1)} %get-tuple-element.146.act, bf16[512,768]{1,0:T(8,128)(2,1)} %get-tuple-element.158.dz), custom_call_target="tpu_custom_call" | custom-call | tf_op jit(solution)/shard_map/shrink_grad/pallas_call | solution.py:39
  129.4 8.0 %hidden.1 = (bf16[512,1536]{1,0:T(8,128)(2,1)}, bf16[512,768]{1,0:T(8,128)(2,1)}, f32[8,1536]{1,0:T(8,128)}) custom-call(s32[20]{0:T(128)} %stack.110.table, bf16[512,768]{1,0:T(8,128)(2,1)} %get-tuple-element.158.dz, bf16[512,1536]{1,0:T(8,128)(2,1)} %get-tuple-element.159.slope, bf16[768,1536]{1,0:T(8,128)(2,1)} %get-tuple-element.160.e, ...), custom_call_target="tpu_custom_call" | custom-call | tf_op jit(solution)/shard_map/hidden/pallas_call | solution.py:39
  140.8 5.4 %first.1 = (f32[256,768]{1,0:T(8,128)}, bf16[512,768]{1,0:T(8,128)(2,1)}, bf16[192,512]{1,0:T(8,128)(2,1)}, bf16[192,512]{1,0:T(8,128)(2,1)}, f32[8,768]{1,0:T(8,128)}) custom-call(s32[20]{0:T(128)} %stack.110.table, bf16[512,768]{1,0:T(8,128)(2,1)} %get-tuple-element.162.mine, bf16[512,768]{1,0:T(8,128)(2,1)} %copy-done.8, ...), custom_call_target="tpu_custom_call" | custom-call | tf_op jit(solution)/shard_map/first/pallas_call | solution.py:39
  147.4 5.7 %expand_grad.1 = (bf16[2,104,1920]{2,1,0:T(8,128)(2,1)}, bf16[2,104,1920]{2,1,0:T(8,128)(2,1)}, bf16[2,104,1920]{2,1,0:T(8,128)(2,1)}, bf16[2,104,1920]{2,1,0:T(8,128)(2,1)}) custom-call(s32[20]{0:T(128)} %stack.110.table, bf16[512,768]{1,0:T(8,128)(2,1)} %get-tuple-element.136.low, bf16[512,1536]{1,0:T(8,128)(2,1)} %get-tuple-element.177.dpre, ...), custom_call_target="tpu_custom_call" | custom-call | tf_op jit(solution)/shard_map/expand_grad/pallas_call | solution.py:39
  153.9 2.1 pair.5
  156.0 1.4 collective-permute-start.35
  157.4 2.7 %collective-permute-start.34 = (bf16[192,768]{1,0:T(8,128)(2,1)}, bf16[192,768]{1,0:T(8,128)(2,1)S(1)}, u32[]{:S(2)}, u32[]{:S(2)}) collective-permute-start(bf16[192,768]{1,0:T(8,128)(2,1)} %get-tuple-element.185), channel_id=1, source_target_pairs={{0,2},{1,3},{2,4},{3,5},{4,6},{5,7},{6,0},{7,1},{8,10},{9,11},{10,... | collective-permute-start | bytes 884744 | tf_op jit(solution)/shard_map/ppermute | solution.py:411
  161.6 16.1 %attend_back.1 = (bf16[4,104,640]{2,1,0:T(8,128)(2,1)}, bf16[4,104,640]{2,1,0:T(8,128)(2,1)}, bf16[1024,640]{1,0:T(8,128)(2,1)}) custom-call(s32[20]{0:T(128)} %stack.110.table, bf16[1024,896]{1,0:T(8,128)(2,1)} %get-tuple-element.132.tok, bf16[1024,256]{1,0:T(8,128)(2,1)} %get-tuple-element.166.qp, bf16[1024,256]{1,0:T(8,128)(2,1)} %get-tuple-element.167.kp, ...), custom_call_target="tpu_custom_call" | custom-call | tf_op jit(solution)/shard_map/attend_back/pallas_call | solution.py:39
  179.2 2.1 pair.6
  181.4 4.3 %input_grad.1 = (bf16[2,256,768]{2,1,0:T(8,128)(2,1)}, bf16[2,256,768]{2,1,0:T(8,128)(2,1)}) custom-call(s32[20]{0:T(128)} %stack.110.table, bf16[1024,640]{1,0:T(8,128)(2,1)} %get-tuple-element.193.grads, bf16[768,640]{1,0:T(8,128)(2,1)} %get-tuple-element.194.w), custom_call_target="tpu_custom_call" | custom-call | tf_op jit(solution)/shard_map/input_grad/pallas_call | solution.py:39
  185.7 2.2 collective-permute-start.36
  188.7 2.5 pair.7
  192.2 2.1 collective-permute-start.50
  194.2 5.2 %collective-permute-done.38.got = bf16[2,104,1920]{2,1,0:T(8,128)(2,1)S(1)} collective-permute-done((bf16[2,104,1920]{2,1,0:T(8,128)(2,1)}, bf16[2,104,1920]{2,1,0:T(8,128)(2,1)S(1)}, u32[]{:S(2)}, u32[]{:S(2)}) %collective-permute-start.38) | collective-permute-done | bytes 798752 | tf_op jit(solution)/shard_map/ppermute | solution.py:411
  200.5 2.3 pair.8
  205.3 2.8 %collective-permute-start.51 = (bf16[104,1920]{1,0:T(8,128)(2,1)}, bf16[104,1920]{1,0:T(8,128)(2,1)S(1)}, u32[]{:S(2)}, u32[]{:S(2)}) collective-permute-start(bf16[104,1920]{1,0:T(8,128)(2,1)} %get-tuple-element.223), channel_id=1, source_target_pairs={{0,6},{1,7},{2,0},{3,1},{4,2},{5,3},{6,4},{7,5},{8,14},{9,15},{10,... | collective-permute-start | bytes 1198088 | tf_op jit(solution)/shard_map/ppermute | solution.py:411
  208.0 1.3 convert_add_fusion
  209.4 3.8 %collective-permute-done.49 = bf16[104,1920]{1,0:T(8,128)(2,1)} collective-permute-done((bf16[104,1920]{1,0:T(8,128)(2,1)}, bf16[104,1920]{1,0:T(8,128)(2,1)}, u32[]{:S(2)}, u32[]{:S(2)}) %collective-permute-start.49) | collective-permute-done | bytes 399392 | tf_op jit(solution)/shard_map/ppermute | solution.py:411
  214.5 15.9 %collective-permute-done.50 = bf16[104,1920]{1,0:T(8,128)(2,1)} collective-permute-done((bf16[104,1920]{1,0:T(8,128)(2,1)}, bf16[104,1920]{1,0:T(8,128)(2,1)}, u32[]{:S(2)}, u32[]{:S(2)}) %collective-permute-start.50) | collective-permute-done | bytes 399392 | tf_op jit(solution)/shard_map/ppermute | solution.py:411
  234.1 2.0 pair.9
  236.1 2.1 collective-permute-start.42
  239.4 1.7 collective-permute-start.54
  241.1 4.2 %collective-permute-done.42 = bf16[104,640]{1,0:T(8,128)(2,1)S(1)} collective-permute-done((bf16[104,640]{1,0:T(8,128)(2,1)}, bf16[104,640]{1,0:T(8,128)(2,1)S(1)}, u32[]{:S(2)}, u32[]{:S(2)}) %collective-permute-start.42) | collective-permute-done | bytes 133152 | tf_op jit(solution)/shard_map/ppermute | solution.py:411
  245.4 5.2 %collective-permute-done.43 = bf16[104,640]{1,0:T(8,128)(2,1)S(1)} collective-permute-done((bf16[104,640]{1,0:T(8,128)(2,1)}, bf16[104,640]{1,0:T(8,128)(2,1)S(1)}, u32[]{:S(2)}, u32[]{:S(2)}) %collective-permute-start.43) | collective-permute-done | bytes 133152 | tf_op jit(solution)/shard_map/ppermute | solution.py:411
  255.8 1.8 collective-permute-start.48
  260.1 2.3 final_projection.1
  263.7 2.9 %final_wide.1 = (f32[96,768]{1,0:T(8,128)}, f32[96,3072]{1,0:T(8,128)}, f32[2,8,1920]{2,1,0:T(8,128)}) custom-call(s32[20]{0:T(128)} %stack.110.table, f32[104,1920]{1,0:T(8,128)} %copy-done.2, f32[104,1920]{1,0:T(8,128)} %collective-permute-done.53.theirs), custom_call_target="tpu_custom_call" | custom-call | tf_op jit(solution)/shard_map/final_wide/pallas_call | solution.py:39
  (227 shorter events, 58.4 us)
Async XLA Ops:
  7.4 6.7 %collective-permute-start.3 = (bf16[112,1024]{1,0:T(8,128)(2,1)}, bf16[112,1024]{1,0:T(8,128)(2,1)S(1)}, u32[]{:S(2)}, u32[]{:S(2)}) collective-permute-start(bf16[112,1024]{1,0:T(8,128)(2,1)} %projection.1.refs_0_), channel_id=1, source_target_pairs={{0,2},{1,3},{2,4},{3,5},{4,6},{5,7},{6,0},{7,1},{8,10},{9,11},{10,... | collective-permute-start | bytes 688136 | tf_op jit(solution)/shard_map/ppermute | solution.py:411
  9.2 23.3 %collective-permute-start.1 = (bf16[256,896]{1,0:T(8,128)(2,1)S(1)}, bf16[256,896]{1,0:T(8,128)(2,1)S(1)}, u32[]{:S(2)}, u32[]{:S(2)}) collective-permute-start(bf16[256,896]{1,0:T(8,128)(2,1)S(1)} %pad_maximum_fusion.1.t0), channel_id=1, source_target_pairs={{0,16},{16,0},{8,24},{24,8},{1,17},{17,1},{9,25},{25,9},{2,18},{18... | collective-permute-start | bytes 1376264 | tf_op jit(solution)/shard_map/ppermute | solution.py:411
  10.5 9.1 %collective-permute-start.6 = (bf16[112,1024]{1,0:T(8,128)(2,1)}, bf16[112,1024]{1,0:T(8,128)(2,1)S(1)}, u32[]{:S(2)}, u32[]{:S(2)}) collective-permute-start(bf16[112,1024]{1,0:T(8,128)(2,1)} %projection.1.refs_0_), channel_id=1, source_target_pairs={{0,1},{1,0},{2,3},{3,2},{4,5},{5,4},{6,7},{7,6},{8,9},{9,8},{10,11... | collective-permute-start | bytes 688136 | tf_op jit(solution)/shard_map/ppermute | solution.py:411
  12.2 8.4 %collective-permute-start.4 = (bf16[112,1024]{1,0:T(8,128)(2,1)}, bf16[112,1024]{1,0:T(8,128)(2,1)S(1)}, u32[]{:S(2)}, u32[]{:S(2)}) collective-permute-start(bf16[112,1024]{1,0:T(8,128)(2,1)} %projection.1.refs_0_), channel_id=1, source_target_pairs={{0,6},{1,7},{2,0},{3,1},{4,2},{5,3},{6,4},{7,5},{8,14},{9,15},{10,... | collective-permute-start | bytes 688136 | tf_op jit(solution)/shard_map/ppermute | solution.py:411
  14.1 8.0 %collective-permute-start.7 = (bf16[112,1024]{1,0:T(8,128)(2,1)S(1)}, bf16[112,1024]{1,0:T(8,128)(2,1)S(1)}, u32[]{:S(2)}, u32[]{:S(2)}) collective-permute-start(bf16[112,1024]{1,0:T(8,128)(2,1)S(1)} %collective-permute-done.3.refs_1_), channel_id=1, source_target_pairs={{0,1},{1,0},{2,3},{3,2},{4,5},{5,4},{6,7},{7,6},{8,9},{9,8},{10,11... | collective-permute-start | bytes 688136 | tf_op jit(solution)/shard_map/ppermute | solution.py:411
  15.5 9.4 %collective-permute-start.5 = (bf16[112,1024]{1,0:T(8,128)(2,1)}, bf16[112,1024]{1,0:T(8,128)(2,1)}, u32[]{:S(2)}, u32[]{:S(2)}) collective-permute-start(bf16[112,1024]{1,0:T(8,128)(2,1)} %projection.1.refs_0_), channel_id=1, source_target_pairs={{0,4},{1,5},{2,6},{3,7},{4,0},{5,1},{6,2},{7,3},{8,12},{9,13},{10,... | collective-permute-start | bytes 688136 | tf_op jit(solution)/shard_map/ppermute | solution.py:411
  19.7 12.9 %collective-permute-start.9 = (bf16[96,1536]{1,0:T(8,128)(2,1)}, bf16[96,1536]{1,0:T(8,128)(2,1)S(1)}, u32[]{:S(2)}, u32[]{:S(2)}) collective-permute-start(bf16[96,1536]{1,0:T(8,128)(2,1)} %wide.1.refs_0_), channel_id=1, source_target_pairs={{0,1},{1,0},{2,3},{3,2},{4,5},{5,4},{6,7},{7,6},{8,9},{9,8},{10,11... | collective-permute-start | bytes 884744 | tf_op jit(solution)/shard_map/ppermute | solution.py:411
  20.6 13.0 %collective-permute-start.11 = (bf16[96,1536]{1,0:T(8,128)(2,1)}, bf16[96,1536]{1,0:T(8,128)(2,1)}, u32[]{:S(2)}, u32[]{:S(2)}) collective-permute-start(bf16[96,1536]{1,0:T(8,128)(2,1)} %wide.1.refs_0_), channel_id=1, source_target_pairs={{0,2},{1,3},{2,4},{3,5},{4,6},{5,7},{6,0},{7,1},{8,10},{9,11},{10,... | collective-permute-start | bytes 884744 | tf_op jit(solution)/shard_map/ppermute | solution.py:411
  22.1 18.2 %collective-permute-start.8 = (bf16[112,1024]{1,0:T(8,128)(2,1)S(1)}, bf16[112,1024]{1,0:T(8,128)(2,1)S(1)}, u32[]{:S(2)}, u32[]{:S(2)}) collective-permute-start(bf16[112,1024]{1,0:T(8,128)(2,1)S(1)} %collective-permute-done.4.refs_2_), channel_id=1, source_target_pairs={{0,1},{1,0},{2,3},{3,2},{4,5},{5,4},{6,7},{7,6},{8,9},{9,8},{10,11... | collective-permute-start | bytes 688136 | tf_op jit(solution)/shard_map/ppermute | solution.py:411
  24.8 18.6 %collective-permute-start = (bf16[256,896]{1,0:T(8,128)(2,1)S(1)}, bf16[256,896]{1,0:T(8,128)(2,1)S(1)}, u32[]{:S(2)}, u32[]{:S(2)}) collective-permute-start(bf16[256,896]{1,0:T(8,128)(2,1)S(1)} %pad_maximum_fusion.1.t0), channel_id=1, source_target_pairs={{0,8},{8,0},{16,24},{24,16},{1,9},{9,1},{17,25},{25,17},{2,10},{10... | collective-permute-start | bytes 1376264 | tf_op jit(solution)/shard_map/ppermute | solution.py:420
  32.5 11.9 %collective-permute-start.2 = (bf16[256,896]{1,0:T(8,128)(2,1)S(1)}, bf16[256,896]{1,0:T(8,128)(2,1)S(1)}, u32[]{:S(2)}, u32[]{:S(2)}) collective-permute-start(bf16[256,896]{1,0:T(8,128)(2,1)S(1)} %collective-permute-done.1.t2), channel_id=1, source_target_pairs={{0,8},{8,0},{16,24},{24,16},{1,9},{9,1},{17,25},{25,17},{2,10},{10... | collective-permute-start | bytes 1376264 | tf_op jit(solution)/shard_map/ppermute | solution.py:420
  32.6 7.8 %collective-permute-start.10 = (bf16[112,1024]{1,0:T(8,128)(2,1)}, bf16[112,1024]{1,0:T(8,128)(2,1)S(1)}, u32[]{:S(2)}, u32[]{:S(2)}) collective-permute-start(bf16[112,1024]{1,0:T(8,128)(2,1)} %collective-permute-done.5.refs_3_), channel_id=1, source_target_pairs={{0,1},{1,0},{2,3},{3,2},{4,5},{5,4},{6,7},{7,6},{8,9},{9,8},{10,11... | collective-permute-start | bytes 688136 | tf_op jit(solution)/shard_map/ppermute | solution.py:411
  33.7 26.2 %collective-permute-start.16 = (bf16[96,1536]{1,0:T(8,128)(2,1)}, bf16[96,1536]{1,0:T(8,128)(2,1)}, u32[]{:S(2)}, u32[]{:S(2)}) collective-permute-start(bf16[96,1536]{1,0:T(8,128)(2,1)} %wide.1.refs_0_), channel_id=1, source_target_pairs={{0,6},{1,7},{2,0},{3,1},{4,2},{5,3},{6,4},{7,5},{8,14},{9,15},{10,... | collective-permute-start | bytes 884744 | tf_op jit(solution)/shard_map/ppermute | solution.py:411
  40.3 24.6 %collective-permute-start.18 = (bf16[96,1536]{1,0:T(8,128)(2,1)}, bf16[96,1536]{1,0:T(8,128)(2,1)}, u32[]{:S(2)}, u32[]{:S(2)}) collective-permute-start(bf16[96,1536]{1,0:T(8,128)(2,1)} %collective-permute-done.11.refs_1_), channel_id=1, source_target_pairs={{0,1},{1,0},{2,3},{3,2},{4,5},{5,4},{6,7},{7,6},{8,9},{9,8},{10,11... | collective-permute-start | bytes 884744 | tf_op jit(solution)/shard_map/ppermute | solution.py:411
  41.7 23.9 %collective-permute-start.17 = (bf16[96,1536]{1,0:T(8,128)(2,1)}, bf16[96,1536]{1,0:T(8,128)(2,1)}, u32[]{:S(2)}, u32[]{:S(2)}) collective-permute-start(bf16[96,1536]{1,0:T(8,128)(2,1)} %wide.1.refs_0_), channel_id=1, source_target_pairs={{0,4},{1,5},{2,6},{3,7},{4,0},{5,1},{6,2},{7,3},{8,12},{9,13},{10,... | collective-permute-start | bytes 884744 | tf_op jit(solution)/shard_map/ppermute | solution.py:411
  43.5 25.0 %collective-permute-start.20 = (bf16[192,768]{1,0:T(8,128)(2,1)S(1)}, bf16[192,768]{1,0:T(8,128)(2,1)S(1)}, u32[]{:S(2)}, u32[]{:S(2)}) collective-permute-start(bf16[192,768]{1,0:T(8,128)(2,1)S(1)} %constant_dynamic-slice_fusion.5.refs_0_), channel_id=1, source_target_pairs={{0,1},{1,0},{2,3},{3,2},{4,5},{5,4},{6,7},{7,6},{8,9},{9,8},{10,11... | collective-permute-start | bytes 884744 | tf_op jit(solution)/shard_map/ppermute | solution.py:411
  59.9 9.6 %collective-permute-start.22 = (bf16[192,768]{1,0:T(8,128)(2,1)S(1)}, bf16[192,768]{1,0:T(8,128)(2,1)S(1)}, u32[]{:S(2)}, u32[]{:S(2)}) collective-permute-start(bf16[192,768]{1,0:T(8,128)(2,1)S(1)} %constant_dynamic-slice_fusion.5.refs_0_), channel_id=1, source_target_pairs={{0,2},{1,3},{2,4},{3,5},{4,6},{5,7},{6,0},{7,1},{8,10},{9,11},{10,... | collective-permute-start | bytes 884744 | tf_op jit(solution)/shard_map/ppermute | solution.py:411
  64.9 6.1 %collective-permute-start.19 = (bf16[96,1536]{1,0:T(8,128)(2,1)}, bf16[96,1536]{1,0:T(8,128)(2,1)}, u32[]{:S(2)}, u32[]{:S(2)}) collective-permute-start(bf16[96,1536]{1,0:T(8,128)(2,1)} %collective-permute-done.16.refs_2_), channel_id=1, source_target_pairs={{0,1},{1,0},{2,3},{3,2},{4,5},{5,4},{6,7},{7,6},{8,9},{9,8},{10,11... | collective-permute-start | bytes 884744 | tf_op jit(solution)/shard_map/ppermute | solution.py:411
  65.6 15.8 %collective-permute-start.23 = (bf16[192,768]{1,0:T(8,128)(2,1)S(1)}, bf16[192,768]{1,0:T(8,128)(2,1)S(1)}, u32[]{:S(2)}, u32[]{:S(2)}) collective-permute-start(bf16[192,768]{1,0:T(8,128)(2,1)S(1)} %constant_dynamic-slice_fusion.5.refs_0_), channel_id=1, source_target_pairs={{0,6},{1,7},{2,0},{3,1},{4,2},{5,3},{6,4},{7,5},{8,14},{9,15},{10,... | collective-permute-start | bytes 884744 | tf_op jit(solution)/shard_map/ppermute | solution.py:411
  65.6 30.4 %collective-permute-start.15 = (bf16[768,384]{1,0:T(8,128)(2,1)}, bf16[768,384]{1,0:T(8,128)(2,1)S(1)}, u32[]{:S(2)}, u32[]{:S(2)}) collective-permute-start(bf16[768,384]{1,0:T(8,128)(2,1)} %get-tuple-element.134.mine.wm), channel_id=1, source_target_pairs={{0,8},{8,0},{16,24},{24,16},{1,9},{9,1},{17,25},{25,17},{2,10},{10... | collective-permute-start | bytes 1769480 | tf_op jit(solution)/shard_map/ppermute | solution.py:420
  68.5 14.2 %collective-permute-start.21 = (bf16[96,1536]{1,0:T(8,128)(2,1)}, bf16[96,1536]{1,0:T(8,128)(2,1)}, u32[]{:S(2)}, u32[]{:S(2)}) collective-permute-start(bf16[96,1536]{1,0:T(8,128)(2,1)} %collective-permute-done.17.refs_3_), channel_id=1, source_target_pairs={{0,1},{1,0},{2,3},{3,2},{4,5},{5,4},{6,7},{7,6},{8,9},{9,8},{10,11... | collective-permute-start | bytes 884744 | tf_op jit(solution)/shard_map/ppermute | solution.py:411
  69.5 14.8 %collective-permute-start.24 = (bf16[192,768]{1,0:T(8,128)(2,1)S(1)}, bf16[192,768]{1,0:T(8,128)(2,1)S(1)}, u32[]{:S(2)}, u32[]{:S(2)}) collective-permute-start(bf16[192,768]{1,0:T(8,128)(2,1)S(1)} %constant_dynamic-slice_fusion.5.refs_0_), channel_id=1, source_target_pairs={{0,4},{1,5},{2,6},{3,7},{4,0},{5,1},{6,2},{7,3},{8,12},{9,13},{10,... | collective-permute-start | bytes 884744 | tf_op jit(solution)/shard_map/ppermute | solution.py:411
  71.0 13.4 %collective-permute-start.25 = (bf16[192,768]{1,0:T(8,128)(2,1)S(1)}, bf16[192,768]{1,0:T(8,128)(2,1)S(1)}, u32[]{:S(2)}, u32[]{:S(2)}) collective-permute-start(bf16[192,768]{1,0:T(8,128)(2,1)S(1)} %collective-permute-done.22.refs_1_), channel_id=1, source_target_pairs={{0,1},{1,0},{2,3},{3,2},{4,5},{5,4},{6,7},{7,6},{8,9},{9,8},{10,11... | collective-permute-start | bytes 884744 | tf_op jit(solution)/shard_map/ppermute | solution.py:411
  81.4 13.0 %collective-permute-start.13 = (bf16[192,512]{1,0:T(8,128)(2,1)}, bf16[192,512]{1,0:T(8,128)(2,1)S(1)}, u32[]{:S(2)}, u32[]{:S(2)}) collective-permute-start(bf16[192,512]{1,0:T(8,128)(2,1)} %get-tuple-element.131), channel_id=1, source_target_pairs={{0,16},{16,0},{8,24},{24,8},{1,17},{17,1},{9,25},{25,9},{2,18},{18... | collective-permute-start | bytes 589832 | tf_op jit(solution)/shard_map/ppermute | solution.py:411
  82.6 27.4 %collective-permute-start.26 = (bf16[192,768]{1,0:T(8,128)(2,1)S(1)}, bf16[192,768]{1,0:T(8,128)(2,1)S(1)}, u32[]{:S(2)}, u32[]{:S(2)}) collective-permute-start(bf16[192,768]{1,0:T(8,128)(2,1)S(1)} %collective-permute-done.23.refs_2_), channel_id=1, source_target_pairs={{0,1},{1,0},{2,3},{3,2},{4,5},{5,4},{6,7},{7,6},{8,9},{9,8},{10,11... | collective-permute-start | bytes 884744 | tf_op jit(solution)/shard_map/ppermute | solution.py:411
  84.4 25.6 %collective-permute-start.27 = (bf16[192,768]{1,0:T(8,128)(2,1)S(1)}, bf16[192,768]{1,0:T(8,128)(2,1)S(1)}, u32[]{:S(2)}, u32[]{:S(2)}) collective-permute-start(bf16[192,768]{1,0:T(8,128)(2,1)S(1)} %collective-permute-done.24.refs_3_), channel_id=1, source_target_pairs={{0,1},{1,0},{2,3},{3,2},{4,5},{5,4},{6,7},{7,6},{8,9},{9,8},{10,11... | collective-permute-start | bytes 884744 | tf_op jit(solution)/shard_map/ppermute | solution.py:411
  85.0 10.6 %collective-permute-start.12 = (bf16[192,512]{1,0:T(8,128)(2,1)}, bf16[192,512]{1,0:T(8,128)(2,1)S(1)}, u32[]{:S(2)}, u32[]{:S(2)}) collective-permute-start(bf16[192,512]{1,0:T(8,128)(2,1)} %get-tuple-element.130.a0), channel_id=1, source_target_pairs={{0,8},{8,0},{16,24},{24,16},{1,9},{9,1},{17,25},{25,17},{2,10},{10... | collective-permute-start | bytes 589832 | tf_op jit(solution)/shard_map/ppermute | solution.py:420
  137.8 15.3 %collective-permute-start.32 = (bf16[2,192,768]{2,1,0:T(8,128)(2,1)S(1)}, bf16[2,192,768]{2,1,0:T(8,128)(2,1)S(1)}, u32[]{:S(2)}, u32[]{:S(2)}) collective-permute-start(bf16[2,192,768]{2,1,0:T(8,128)(2,1)S(1)} %copy-done.53), channel_id=1, source_target_pairs={{0,1},{1,0},{2,3},{3,2},{4,5},{5,4},{6,7},{7,6},{8,9},{9,8},{10,11... | collective-permute-start | bytes 1769480 | tf_op jit(solution)/shard_map/ppermute | solution.py:411
  138.7 39.7 %collective-permute-start.33 = (bf16[2,192,768]{2,1,0:T(8,128)(2,1)S(1)}, bf16[2,192,768]{2,1,0:T(8,128)(2,1)S(1)}, u32[]{:S(2)}, u32[]{:S(2)}) collective-permute-start(bf16[2,192,768]{2,1,0:T(8,128)(2,1)S(1)} %copy-done.52), channel_id=1, source_target_pairs={{0,1},{1,0},{2,3},{3,2},{4,5},{5,4},{6,7},{7,6},{8,9},{9,8},{10,11... | collective-permute-start | bytes 1769480 | tf_op jit(solution)/shard_map/ppermute | solution.py:411
  146.1 14.8 %collective-permute-start.31 = (bf16[192,512]{1,0:T(8,128)(2,1)}, bf16[192,512]{1,0:T(8,128)(2,1)S(1)}, u32[]{:S(2)}, u32[]{:S(2)}) collective-permute-start(bf16[192,512]{1,0:T(8,128)(2,1)} %get-tuple-element.175), channel_id=1, source_target_pairs={{0,16},{16,0},{8,24},{24,8},{1,17},{17,1},{9,25},{25,9},{2,18},{18... | collective-permute-start | bytes 589832 | tf_op jit(solution)/shard_map/ppermute | solution.py:411
  156.0 22.4 %collective-permute-start.35 = (bf16[192,768]{1,0:T(8,128)(2,1)}, bf16[192,768]{1,0:T(8,128)(2,1)S(1)}, u32[]{:S(2)}, u32[]{:S(2)}) collective-permute-start(bf16[192,768]{1,0:T(8,128)(2,1)} %get-tuple-element.190), channel_id=1, source_target_pairs={{0,4},{1,5},{2,6},{3,7},{4,0},{5,1},{6,2},{7,3},{8,12},{9,13},{10,... | collective-permute-start | bytes 884744 | tf_op jit(solution)/shard_map/ppermute | solution.py:411
  157.4 21.0 %collective-permute-start.34 = (bf16[192,768]{1,0:T(8,128)(2,1)}, bf16[192,768]{1,0:T(8,128)(2,1)S(1)}, u32[]{:S(2)}, u32[]{:S(2)}) collective-permute-start(bf16[192,768]{1,0:T(8,128)(2,1)} %get-tuple-element.185), channel_id=1, source_target_pairs={{0,2},{1,3},{2,4},{3,5},{4,6},{5,7},{6,0},{7,1},{8,10},{9,11},{10,... | collective-permute-start | bytes 884744 | tf_op jit(solution)/shard_map/ppermute | solution.py:411
  160.1 27.7 %collective-permute-start.40 = (bf16[2,104,1920]{2,1,0:T(8,128)(2,1)}, bf16[2,104,1920]{2,1,0:T(8,128)(2,1)S(1)}, u32[]{:S(2)}, u32[]{:S(2)}) collective-permute-start(bf16[2,104,1920]{2,1,0:T(8,128)(2,1)} %get-tuple-element.205), channel_id=1, source_target_pairs={{0,1},{1,0},{2,3},{3,2},{4,5},{5,4},{6,7},{7,6},{8,9},{9,8},{10,11... | collective-permute-start | bytes 2396168 | tf_op jit(solution)/shard_map/ppermute | solution.py:411
  177.7 21.8 %collective-permute-start.38 = (bf16[2,104,1920]{2,1,0:T(8,128)(2,1)}, bf16[2,104,1920]{2,1,0:T(8,128)(2,1)S(1)}, u32[]{:S(2)}, u32[]{:S(2)}) collective-permute-start(bf16[2,104,1920]{2,1,0:T(8,128)(2,1)} %get-tuple-element.201), channel_id=1, source_target_pairs={{0,1},{1,0},{2,3},{3,2},{4,5},{5,4},{6,7},{7,6},{8,9},{9,8},{10,11... | collective-permute-start | bytes 2396168 | tf_op jit(solution)/shard_map/ppermute | solution.py:411
  185.7 19.6 %collective-permute-start.36 = (bf16[2,256,768]{2,1,0:T(8,128)(2,1)}, bf16[2,256,768]{2,1,0:T(8,128)(2,1)}, u32[]{:S(2)}, u32[]{:S(2)}) collective-permute-start(bf16[2,256,768]{2,1,0:T(8,128)(2,1)} %get-tuple-element.196), channel_id=1, source_target_pairs={{0,8},{8,0},{16,24},{24,16},{1,9},{9,1},{17,25},{25,17},{2,10},{10... | collective-permute-start | bytes 2359304 | tf_op jit(solution)/shard_map/ppermute | solution.py:420
  187.8 15.0 %collective-permute-start.45 = (bf16[192,768]{1,0:T(8,128)(2,1)S(1)}, bf16[192,768]{1,0:T(8,128)(2,1)}, u32[]{:S(2)}, u32[]{:S(2)}) collective-permute-start(bf16[192,768]{1,0:T(8,128)(2,1)S(1)} %copy-done.54), channel_id=1, source_target_pairs={{0,6},{1,7},{2,0},{3,1},{4,2},{5,3},{6,4},{7,5},{8,14},{9,15},{10,... | collective-permute-start | bytes 884744 | tf_op jit(solution)/shard_map/ppermute | solution.py:411
  191.2 22.1 %collective-permute-start.49 = (bf16[104,1920]{1,0:T(8,128)(2,1)}, bf16[104,1920]{1,0:T(8,128)(2,1)}, u32[]{:S(2)}, u32[]{:S(2)}) collective-permute-start(bf16[104,1920]{1,0:T(8,128)(2,1)} %get-tuple-element.222), channel_id=1, source_target_pairs={{0,4},{1,5},{2,6},{3,7},{4,0},{5,1},{6,2},{7,3},{8,12},{9,13},{10,... | collective-permute-start | bytes 1198088 | tf_op jit(solution)/shard_map/ppermute | solution.py:411
  192.2 38.3 %collective-permute-start.50 = (bf16[104,1920]{1,0:T(8,128)(2,1)}, bf16[104,1920]{1,0:T(8,128)(2,1)}, u32[]{:S(2)}, u32[]{:S(2)}) collective-permute-start(bf16[104,1920]{1,0:T(8,128)(2,1)} %get-tuple-element.207), channel_id=1, source_target_pairs={{0,2},{1,3},{2,4},{3,5},{4,6},{5,7},{6,0},{7,1},{8,10},{9,11},{10,... | collective-permute-start | bytes 1198088 | tf_op jit(solution)/shard_map/ppermute | solution.py:411
  199.5 33.8 %collective-permute-start.39 = (bf16[4,104,640]{2,1,0:T(8,128)(2,1)}, bf16[4,104,640]{2,1,0:T(8,128)(2,1)S(1)}, u32[]{:S(2)}, u32[]{:S(2)}) collective-permute-start(bf16[4,104,640]{2,1,0:T(8,128)(2,1)} %get-tuple-element.202), channel_id=1, source_target_pairs={{0,1},{1,0},{2,3},{3,2},{4,5},{5,4},{6,7},{7,6},{8,9},{9,8},{10,11... | collective-permute-start | bytes 1597448 | tf_op jit(solution)/shard_map/ppermute | solution.py:411
  204.0 35.4 %collective-permute-start.46 = (bf16[192,768]{1,0:T(8,128)(2,1)S(1)}, bf16[192,768]{1,0:T(8,128)(2,1)S(1)}, u32[]{:S(2)}, u32[]{:S(2)}) collective-permute-start(bf16[192,768]{1,0:T(8,128)(2,1)S(1)} %add_convert_fusion.1), channel_id=1, source_target_pairs={{0,16},{16,0},{8,24},{24,8},{1,17},{17,1},{9,25},{25,9},{2,18},{18... | collective-permute-start | bytes 884744 | tf_op jit(solution)/shard_map/ppermute | solution.py:411
  205.3 25.3 %collective-permute-start.51 = (bf16[104,1920]{1,0:T(8,128)(2,1)}, bf16[104,1920]{1,0:T(8,128)(2,1)S(1)}, u32[]{:S(2)}, u32[]{:S(2)}) collective-permute-start(bf16[104,1920]{1,0:T(8,128)(2,1)} %get-tuple-element.223), channel_id=1, source_target_pairs={{0,6},{1,7},{2,0},{3,1},{4,2},{5,3},{6,4},{7,5},{8,14},{9,15},{10,... | collective-permute-start | bytes 1198088 | tf_op jit(solution)/shard_map/ppermute | solution.py:411
  213.3 18.7 %collective-permute-start.37 = (bf16[256,768]{1,0:T(8,128)(2,1)S(1)}, bf16[256,768]{1,0:T(8,128)(2,1)S(1)}, u32[]{:S(2)}, u32[]{:S(2)}) collective-permute-start(bf16[256,768]{1,0:T(8,128)(2,1)S(1)} %fusion.4), channel_id=1, source_target_pairs={{0,16},{16,0},{8,24},{24,8},{1,17},{17,1},{9,25},{25,9},{2,18},{18... | collective-permute-start | bytes 1179656 | tf_op jit(solution)/shard_map/ppermute | solution.py:411
  231.9 20.5 %collective-permute-start.52 = (bf16[104,1920]{1,0:T(8,128)(2,1)S(1)}, bf16[104,1920]{1,0:T(8,128)(2,1)}, u32[]{:S(2)}, u32[]{:S(2)}) collective-permute-start(bf16[104,1920]{1,0:T(8,128)(2,1)S(1)} %add_convert_fusion), channel_id=1, source_target_pairs={{0,16},{16,0},{8,24},{24,8},{1,17},{17,1},{9,25},{25,9},{2,18},{18... | collective-permute-start | bytes 1198088 | tf_op jit(solution)/shard_map/ppermute | solution.py:411
  236.1 5.1 %collective-permute-start.41 = (bf16[104,640]{1,0:T(8,128)(2,1)}, bf16[104,640]{1,0:T(8,128)(2,1)S(1)}, u32[]{:S(2)}, u32[]{:S(2)}) collective-permute-start(bf16[104,640]{1,0:T(8,128)(2,1)} %get-tuple-element.211), channel_id=1, source_target_pairs={{0,4},{1,5},{2,6},{3,7},{4,0},{5,1},{6,2},{7,3},{8,12},{9,13},{10,... | collective-permute-start | bytes 399368 | tf_op jit(solution)/shard_map/ppermute | solution.py:411
  236.1 9.3 %collective-permute-start.42 = (bf16[104,640]{1,0:T(8,128)(2,1)}, bf16[104,640]{1,0:T(8,128)(2,1)S(1)}, u32[]{:S(2)}, u32[]{:S(2)}) collective-permute-start(bf16[104,640]{1,0:T(8,128)(2,1)} %get-tuple-element.212), channel_id=1, source_target_pairs={{0,2},{1,3},{2,4},{3,5},{4,6},{5,7},{6,0},{7,1},{8,10},{9,11},{10,... | collective-permute-start | bytes 399368 | tf_op jit(solution)/shard_map/ppermute | solution.py:411
  238.2 12.4 %collective-permute-start.43 = (bf16[104,640]{1,0:T(8,128)(2,1)}, bf16[104,640]{1,0:T(8,128)(2,1)S(1)}, u32[]{:S(2)}, u32[]{:S(2)}) collective-permute-start(bf16[104,640]{1,0:T(8,128)(2,1)} %get-tuple-element.213), channel_id=1, source_target_pairs={{0,6},{1,7},{2,0},{3,1},{4,2},{5,3},{6,4},{7,5},{8,14},{9,15},{10,... | collective-permute-start | bytes 399368 | tf_op jit(solution)/shard_map/ppermute | solution.py:411
  239.4 18.2 %collective-permute-start.54 = (f32[192,768]{1,0:T(8,128)S(1)}, f32[192,768]{1,0:T(8,128)S(1)}, u32[]{:S(2)}, u32[]{:S(2)}) collective-permute-start(f32[192,768]{1,0:T(8,128)S(1)} %convert_add_fusion.2), channel_id=1, source_target_pairs={{0,8},{8,0},{16,24},{24,16},{1,9},{9,1},{17,25},{25,17},{2,10},{10... | collective-permute-start | bytes 1769480 | tf_op jit(solution)/shard_map/ppermute | solution.py:420
  253.5 10.2 %collective-permute-start.53 = (f32[104,1920]{1,0:T(8,128)S(1)}, f32[104,1920]{1,0:T(8,128)}, u32[]{:S(2)}, u32[]{:S(2)}) collective-permute-start(f32[104,1920]{1,0:T(8,128)S(1)} %convert_add_fusion.1.mine), channel_id=1, source_target_pairs={{0,8},{8,0},{16,24},{24,16},{1,9},{9,1},{17,25},{25,17},{2,10},{10... | collective-permute-start | bytes 2396168 | tf_op jit(solution)/shard_map/ppermute | solution.py:420
  (62 other events, 648.1 us)
